TPU v7x, 32 devices: a whole 2x2x4 slice. The times are simulated.
32 devices in a mesh: seq: 8 (over y, x, core), clip: 4 (over z).
Axes of the slice: x: 2, y: 2, z: 4, core: 2. Of those that a mesh axis runs over, the one named last changes fastest.
Arguments:
- queries: bfloat16 [4, 4096, 512], P('clip', 'seq'), may hold values from -8 to 8
- keys: bfloat16 [4, 4096, 512], P('clip', 'seq'), may hold values from -8 to 8
- values: bfloat16 [4, 4096, 512], P('clip', 'seq'), may hold values from -6 to 6
- out_cotangent: bfloat16 [4, 4096, 1024], P('clip', 'seq'), may hold values from -6 to 6
- visible_counts: int32 [4, 8], P('clip'), may hold values from 1 to 96, 384 in all within a row
- span_offset: int32 [4, 8], P('clip'), may hold values from 0 to 511
- out_weight: bfloat16 [512, 1024], P('seq'), may hold values from -0.1875 to 0.1875
Outputs:
- query_grads: bfloat16 [4, 4096, 512], P('clip', 'seq')
- key_grads: bfloat16 [4, 4096, 512], P('clip', 'seq')
- value_grads: bfloat16 [4, 4096, 512], P('clip', 'seq')
- weight_grad: float32 [512, 1024], P('seq')
Inputs may be any that keep to these rules, and one draw needn't show every extreme that they name: `visible_counts`: in each clip the 8 counts sum to 384, and the largest is exactly 96.
All inputs are finite; a program needn't handle non-finite values.
Results may differ from a plain program's by a relative error of at most 0.014.
Values may be sent and summed in bfloat16 or wider, within the bound.
No kernel may reach another device: no remote copies, remote signals or barrier semaphores. Data moves between devices by JAX's collectives and lax.ppermute only.
A program may use at most 64 MiB of HBM per device.

v0:
```python
import jax
import jax.numpy as jnp
from jax import lax
from jax.sharding import PartitionSpec as P

HEADS = 8
HD = 64
VIS_DEV = 48
MAXV = 96


def pick_entry(table, position):
    order = jnp.arange(table.shape[0], dtype=jnp.int32)
    chosen = jnp.where(order[None, :] == position[:, None], table[None, :], 0)
    return jnp.sum(chosen, axis=1)


def split_heads(block):
    return block.reshape(block.shape[0], HEADS, HD).transpose(1, 0, 2)


def join_heads(block):
    return block.transpose(1, 0, 2).reshape(block.shape[1], HEADS * HD)


def query_side(parts):
    query_head, key_head, value_head, dout_head = parts
    factor = HD ** (-0.5)
    scores = (
        lax.dot_general(
            query_head, key_head, (((1,), (1,)), ((), ())), preferred_element_type=jnp.float32
        )
        * factor
    )
    peak_score = jnp.max(scores, axis=1, keepdims=True)
    log_total = peak_score + jnp.log(jnp.sum(jnp.exp(scores - peak_score), axis=1, keepdims=True))
    weights = jnp.exp(scores - log_total)
    weights_low = weights.astype(jnp.bfloat16)
    attended = jnp.dot(weights_low, value_head, preferred_element_type=jnp.float32).astype(
        jnp.bfloat16
    )
    inner_sum = jnp.sum(
        dout_head.astype(jnp.float32) * attended.astype(jnp.float32), axis=1, keepdims=True
    )
    dweights = lax.dot_general(
        dout_head, value_head, (((1,), (1,)), ((), ())), preferred_element_type=jnp.float32
    )
    dscores = (weights * (dweights - inner_sum)).astype(jnp.bfloat16)
    grad_query = (jnp.dot(dscores, key_head, preferred_element_type=jnp.float32) * factor).astype(
        jnp.bfloat16
    )
    return (attended, grad_query, log_total[:, 0], inner_sum[:, 0])


def key_side_add(query_piece, dout_piece, log_piece, inner_piece, key_heads, value_heads):
    factor = HD ** (-0.5)

    def one_head(parts):
        query_head, dout_head, log_head, inner_head, key_head, value_head = parts
        scores = (
            lax.dot_general(
                query_head, key_head, (((1,), (1,)), ((), ())), preferred_element_type=jnp.float32
            )
            * factor
        )
        weights = jnp.exp(scores - log_head[:, None])
        weights_low = weights.astype(jnp.bfloat16)
        value_part = lax.dot_general(
            weights_low, dout_head, (((0,), (0,)), ((), ())), preferred_element_type=jnp.float32
        )
        dweights = lax.dot_general(
            dout_head, value_head, (((1,), (1,)), ((), ())), preferred_element_type=jnp.float32
        )
        dscores = (weights * (dweights - inner_head[:, None])).astype(jnp.bfloat16)
        key_part = lax.dot_general(
            dscores, query_head, (((0,), (0,)), ((), ())), preferred_element_type=jnp.float32
        )
        return (key_part, value_part)

    key_parts, value_parts = lax.map(
        one_head,
        (
            split_heads(query_piece),
            split_heads(dout_piece),
            log_piece.T,
            inner_piece.T,
            key_heads,
            value_heads,
        ),
    )
    return (key_parts, value_parts)


def local(queries, keys, values, out_cotangent, visible_counts, span_offset, out_weight):
    devices = lax.axis_size("seq")
    device = lax.axis_index("seq")
    frames = queries.shape[1]
    visible_rows = VIS_DEV
    capacity = MAXV // devices
    counts = visible_counts[0]
    offsets = span_offset[0]
    shard_ends = jnp.cumsum(counts)
    starts = shard_ends - counts
    this_device = device.reshape(1)
    count_here = pick_entry(counts, this_device)[0]
    start_here = pick_entry(starts, this_device)[0]
    span_begin = pick_entry(offsets, this_device)[0] % (count_here + 1)
    masked = frames - count_here
    send_slots = jnp.arange(devices * capacity, dtype=jnp.int32)
    peer_index = send_slots // capacity
    within = send_slots % capacity
    first_slot = (start_here - peer_index + devices - 1) // devices
    global_index = (first_slot + within) * devices + peer_index
    ranked = global_index - start_here
    live_slot = ranked < count_here
    frame_of = jnp.clip(jnp.where(ranked < span_begin, ranked, ranked + masked), 0, frames - 1)

    def outgoing(block):
        return jnp.where(
            live_slot[:, None], jnp.take(block[0], frame_of, axis=0), jnp.zeros((), block.dtype)
        )

    arrived = (
        lax.all_to_all(outgoing(queries), "seq", split_axis=0, concat_axis=0, tiled=True),
        lax.all_to_all(outgoing(keys), "seq", split_axis=0, concat_axis=0, tiled=True),
        lax.all_to_all(outgoing(values), "seq", split_axis=0, concat_axis=0, tiled=True),
        lax.all_to_all(outgoing(out_cotangent), "seq", split_axis=0, concat_axis=0, tiled=True),
    )
    packed_slot = jnp.arange(visible_rows, dtype=jnp.int32)
    packed_index = packed_slot * devices + device
    owner_shard = jnp.sum((shard_ends[None, :] <= packed_index[:, None]).astype(jnp.int32), axis=1)
    owner_first = (pick_entry(starts, owner_shard) - device + devices - 1) // devices
    arrived_row = owner_shard * capacity + packed_slot - owner_first
    query_pack = jnp.take(arrived[0], arrived_row, axis=0)
    key_pack = jnp.take(arrived[1], arrived_row, axis=0)
    value_pack = jnp.take(arrived[2], arrived_row, axis=0)
    cotangent_pack = jnp.take(arrived[3], arrived_row, axis=0)
    output_grad = lax.dot_general(
        cotangent_pack,
        lax.all_gather(out_weight, "seq", axis=0, tiled=True),
        (((1,), (1,)), ((), ())),
        preferred_element_type=jnp.float32,
    ).astype(jnp.bfloat16)
    key_all, value_all = (
        lax.all_gather(key_pack, "seq", axis=0, tiled=True),
        lax.all_gather(value_pack, "seq", axis=0, tiled=True),
    )
    attended, query_grad, log_totals, inner_sums = lax.map(
        query_side,
        (
            split_heads(query_pack),
            split_heads(key_all),
            split_heads(value_all),
            split_heads(output_grad),
        ),
    )
    attended = join_heads(attended)
    query_grad = join_heads(query_grad)
    log_rows = log_totals.T
    inner_rows = inner_sums.T
    partial_term = lax.dot_general(
        attended, cotangent_pack, (((0,), (0,)), ((), ())), preferred_element_type=jnp.float32
    )
    seq_sum = lax.psum_scatter(
        partial_term.astype(jnp.bfloat16), "seq", scatter_dimension=0, tiled=True
    )
    clip_sum = lax.psum(seq_sum, "clip").astype(jnp.float32)
    weight_grad = clip_sum * (lax.axis_size("clip") * visible_rows * devices) ** (-0.5)
    log_every, inner_every = (
        lax.all_gather(log_rows, "seq", axis=0, tiled=True),
        lax.all_gather(inner_rows, "seq", axis=0, tiled=True),
    )
    key_heads = split_heads(key_pack)
    value_heads = split_heads(value_pack)
    key_sum, value_sum = key_side_add(
        lax.all_gather(query_pack, "seq", axis=0, tiled=True),
        lax.all_gather(output_grad, "seq", axis=0, tiled=True),
        log_every,
        inner_every,
        key_heads,
        value_heads,
    )
    key_grad = join_heads((key_sum * HD ** (-0.5)).astype(jnp.bfloat16))
    value_grad = join_heads(value_sum.astype(jnp.bfloat16))
    back_first = (pick_entry(starts, peer_index) - device + devices - 1) // devices
    back_slot = back_first + within
    back_live = back_slot * devices + device < pick_entry(shard_ends, peer_index)
    back_row = jnp.clip(back_slot, 0, visible_rows - 1)

    def returning(block):
        return jnp.where(
            back_live[:, None], jnp.take(block, back_row, axis=0), jnp.zeros((), block.dtype)
        )

    returned = (
        lax.all_to_all(returning(query_grad), "seq", split_axis=0, concat_axis=0, tiled=True),
        lax.all_to_all(returning(key_grad), "seq", split_axis=0, concat_axis=0, tiled=True),
        lax.all_to_all(returning(value_grad), "seq", split_axis=0, concat_axis=0, tiled=True),
    )
    position = jnp.arange(frames, dtype=jnp.int32)
    visible = (position < span_begin) | (position >= span_begin + masked)
    frame_rank = jnp.where(position < span_begin, position, position - masked)
    frame_global = start_here + frame_rank
    frame_peer = frame_global % devices
    frame_slot = frame_global // devices
    frame_first = (start_here - frame_peer + devices - 1) // devices
    frame_row = jnp.clip(
        frame_peer * capacity + frame_slot - frame_first, 0, devices * capacity - 1
    )

    def placed(block):
        return jnp.where(
            visible[:, None], jnp.take(block, frame_row, axis=0), jnp.zeros((), block.dtype)
        )[None]

    return (placed(returned[0]), placed(returned[1]), placed(returned[2]), weight_grad)


def solution(mesh):
    placed = (
        P("clip", "seq", None),
        P("clip", "seq", None),
        P("clip", "seq", None),
        P("clip", "seq", None),
        P("clip", None),
        P("clip", None),
        P("seq", None),
    )
    return jax.shard_map(
        local,
        mesh=mesh,
        in_specs=placed,
        out_specs=(
            P("clip", "seq", None),
            P("clip", "seq", None),
            P("clip", "seq", None),
            P("seq", None),
        ),
        check_vma=False,
    )
```

profile of v0, /device:TPU:0, one launch (start us, length us, event | category | flops | bytes accessed | tf_op | source)
XLA Modules:
  0.0 217.8 jit_solution(15005196300830094414)
XLA Ops:
  7.2 1.0 reduce-window.4
  8.2 1.3 select_reduce_fusion.3
  11.5 1.3 broadcast_compare_fusion.1
  13.5 1.9 gather_fusion.2
  15.4 0.8 gather_fusion.4
  16.2 0.8 gather_fusion.6
  17.1 0.7 all_to_all.54
  17.8 5.2 %all-to-all-start = ((bf16[8,12,512]{2,1,0:T(8,128)(2,1)}), bf16[8,12,512]{2,1,0:T(8,128)(2,1)S(1)}, u32[]{:S(2)}, u32[]{:S(2)}) async-start(bf16[8,12,512]{2,1,0:T(8,128)(2,1)} %all_to_all.54), calls=%async_computation | async-start | bytes 262144 | tf_op jit(solution)/shard_map/all_to_all | solution.py:124
  23.0 0.7 all-gather.4.cloned.1.call-update
  25.3 0.7 all_to_all.57
  26.0 0.7 all_to_all.60
  26.7 0.8 gather_fusion
  27.6 1.3 broadcast_compare_fusion
  29.0 0.8 select_select_fusion.3
  29.8 4.2 %all-to-all-start.1 = ((bf16[8,12,512]{2,1,0:T(8,128)(2,1)}), bf16[8,12,512]{2,1,0:T(8,128)(2,1)S(1)}, u32[]{:S(2)}, u32[]{:S(2)}) async-start(bf16[8,12,512]{2,1,0:T(8,128)(2,1)} %all_to_all.57), calls=%async_computation.1 | async-start | bytes 262144 | tf_op jit(solution)/shard_map/all_to_all | solution.py:125
  34.0 6.9 %all-to-all-done.1 = bf16[8,12,512]{2,1,0:T(8,128)(2,1)S(1)} async-done(((bf16[8,12,512]{2,1,0:T(8,128)(2,1)}), bf16[8,12,512]{2,1,0:T(8,128)(2,1)S(1)}, u32[]{:S(2)}, u32[]{:S(2)}) %all-to-all-start.1) | async-done | bytes 98336 | tf_op jit(solution)/shard_map/all_to_all | solution.py:125
  40.9 3.4 %all-to-all-start.2 = ((bf16[8,12,512]{2,1,0:T(8,128)(2,1)}), bf16[8,12,512]{2,1,0:T(8,128)(2,1)S(1)}, u32[]{:S(2)}, u32[]{:S(2)}) async-start(bf16[8,12,512]{2,1,0:T(8,128)(2,1)} %all_to_all.60), calls=%async_computation.2 | async-start | bytes 262144 | tf_op jit(solution)/shard_map/all_to_all | solution.py:126
  46.3 4.7 %all-to-all-done.2 = bf16[8,12,512]{2,1,0:T(8,128)(2,1)S(1)} async-done(((bf16[8,12,512]{2,1,0:T(8,128)(2,1)}), bf16[8,12,512]{2,1,0:T(8,128)(2,1)S(1)}, u32[]{:S(2)}, u32[]{:S(2)}) %all-to-all-start.2) | async-done | bytes 98336 | tf_op jit(solution)/shard_map/all_to_all | solution.py:126
  51.1 3.4 %all-to-all-start.3 = ((bf16[8,12,1024]{2,1,0:T(8,128)(2,1)}), bf16[8,12,1024]{2,1,0:T(8,128)(2,1)S(1)}, u32[]{:S(2)}, u32[]{:S(2)}) async-start(bf16[8,12,1024]{2,1,0:T(8,128)(2,1)} %select_select_fusion.3), calls=%async_computation.3 | async-start | bytes 524288 | tf_op jit(solution)/shard_map/all_to_all | solution.py:127
  55.4 10.0 %all_gather.21 = bf16[384,512]{1,0:T(8,128)(2,1)S(1)} all-gather(bf16[48,512]{1,0:T(8,128)(2,1)S(1)} %get-tuple-element.249), channel_id=1, replica_groups=mesh['seq'=8,'clip'=4] {'seq'}, dimensions={0}, use_global_device_ids=true | all-gather | bytes 442368 | tf_op jit(solution)/shard_map/all_gather | solution.py:145
  65.7 9.5 %all_gather.22 = bf16[384,512]{1,0:T(8,128)(2,1)S(1)} all-gather(bf16[48,512]{1,0:T(8,128)(2,1)S(1)} %get-tuple-element.248), channel_id=1, replica_groups=mesh['seq'=8,'clip'=4] {'seq'}, dimensions={0}, use_global_device_ids=true | all-gather | bytes 442368 | tf_op jit(solution)/shard_map/all_gather | solution.py:146
  75.6 8.6 %all_gather.24 = bf16[384,512]{1,0:T(8,128)(2,1)S(1)} all-gather(bf16[48,512]{1,0:T(8,128)(2,1)S(1)} %get-tuple-element.250), channel_id=1, replica_groups=mesh['seq'=8,'clip'=4] {'seq'}, dimensions={0}, use_global_device_ids=true | all-gather | bytes 442368 | tf_op jit(solution)/shard_map/all_gather | solution.py:176
  84.6 0.7 gather_fusion.1
  85.3 1.7 convolution_convert_fusion.2
  87.1 9.5 %all_gather.26 = bf16[384,512]{1,0:T(8,128)(2,1)S(1)} all-gather(bf16[48,512]{1,0:T(8,128)(2,1)S(1)} %convolution_convert_fusion.2), channel_id=1, replica_groups=mesh['seq'=8,'clip'=4] {'seq'}, dimensions={0}, use_global_device_ids=true | all-gather | bytes 442368 | tf_op jit(solution)/shard_map/all_gather | solution.py:177
  96.6 18.4 %while.28 = (s32[]{:T(128)}, bf16[8,48,64]{2,1,0:T(8,128)(2,1)}, bf16[8,48,64]{2,1,0:T(8,128)(2,1)}, f32[8,48]{1,0:T(8,128)S(1)}, f32[8,48]{1,0:T(8,128)S(1)}, /...) while((s32[]{:T(128)}, bf16[8,48,64]{2,1,0:T(8,128)(2,1)}, ...), condition=%wide.region_12.15_spmd, body=%wide.region_8.14_spmd.sunk | while | flops 9642914 | bytes 566969 | solution.py:148
  97.1 0.8 bitcast_dynamic-update-slice_fusion.2
  98.0 0.9 fusion.124
  99.4 0.8 bitcast_dynamic-update-slice_fusion.2
  100.3 0.9 fusion.124
  101.7 0.8 bitcast_dynamic-update-slice_fusion.2
  102.6 0.9 fusion.124
  104.0 0.8 bitcast_dynamic-update-slice_fusion.2
  104.9 0.9 fusion.124
  106.3 0.8 bitcast_dynamic-update-slice_fusion.2
  107.2 0.9 fusion.124
  108.6 0.8 bitcast_dynamic-update-slice_fusion.2
  109.5 0.9 fusion.124
  110.9 0.8 bitcast_dynamic-update-slice_fusion.2
  111.8 0.9 fusion.124
  113.2 0.8 bitcast_dynamic-update-slice_fusion.2
  114.1 0.9 fusion.124
  115.1 8.3 %all-gather = f32[8,48,8]{1,2,0:T(8,128)S(1)} all-gather(f32[1,48,8]{1,2,0:T(8,128)S(1)} %bitcast.209), channel_id=1, replica_groups=mesh['seq'=8,'clip'=4] {'seq'}, dimensions={0}, use_global_device_ids=true | all-gather | bytes 13824 | tf_op jit(solution)/shard_map/all_gather | solution.py:170
  123.5 9.1 %all-gather.1 = f32[8,48,8]{1,2,0:T(8,128)S(1)} all-gather(f32[1,48,8]{1,2,0:T(8,128)S(1)} %bitcast.210), channel_id=1, replica_groups=mesh['seq'=8,'clip'=4] {'seq'}, dimensions={0}, use_global_device_ids=true | all-gather | bytes 13824 | tf_op jit(solution)/shard_map/all_gather | solution.py:171
  133.0 1.5 convolution_convert_fusion.1
  134.5 5.0 %while.29 = (s32[]{:T(128)}, f32[8,48,64]{2,1,0:T(8,128)S(1)}, bf16[8,48,64]{2,1,0:T(8,128)(2,1)S(1)}, bf16[8,384,64]{1,2,0:T(8,128)(2,1)S(1)}, bf16[8,48,64]{2,...) while((s32[]{:T(128)}, f32[8,48,64]{2,1,0:T(8,128)S(1)}, ...), condition=%wide.region_14.19_spmd, body=%wide.region_13.18_spmd.sunk | while | flops 9547778 | bytes 505961 | solution.py:80
  139.9 0.8 gather_fusion.10
  140.6 0.8 gather_fusion.12
  141.6 0.8 gather_fusion.8
  142.5 0.7 all_to_all.65
  143.2 3.4 %all-to-all-start.4 = ((bf16[8,12,512]{2,1,0:T(8,128)(2,1)}), bf16[8,12,512]{2,1,0:T(8,128)(2,1)S(1)}, u32[]{:S(2)}, u32[]{:S(2)}) async-start(bf16[8,12,512]{2,1,0:T(8,128)(2,1)} %all_to_all.65), calls=%async_computation.4 | async-start | bytes 262144 | tf_op jit(solution)/shard_map/all_to_all | solution.py:196
  146.6 0.7 all_to_all.68
  147.2 4.7 %all-to-all-done.4 = bf16[8,12,512]{2,1,0:T(8,128)(2,1)S(1)} async-done(((bf16[8,12,512]{2,1,0:T(8,128)(2,1)}), bf16[8,12,512]{2,1,0:T(8,128)(2,1)S(1)}, u32[]{:S(2)}, u32[]{:S(2)}) %all-to-all-start.4) | async-done | bytes 98336 | tf_op jit(solution)/shard_map/all_to_all | solution.py:196
  152.0 3.4 %all-to-all-start.5 = ((bf16[8,12,512]{2,1,0:T(8,128)(2,1)}), bf16[8,12,512]{2,1,0:T(8,128)(2,1)S(1)}, u32[]{:S(2)}, u32[]{:S(2)}) async-start(bf16[8,12,512]{2,1,0:T(8,128)(2,1)} %all_to_all.68), calls=%async_computation.5 | async-start | bytes 262144 | tf_op jit(solution)/shard_map/all_to_all | solution.py:197
  156.0 0.7 all_to_all.71
  156.7 5.5 %all-to-all-done.5 = bf16[8,12,512]{2,1,0:T(8,128)(2,1)S(1)} async-done(((bf16[8,12,512]{2,1,0:T(8,128)(2,1)}), bf16[8,12,512]{2,1,0:T(8,128)(2,1)S(1)}, u32[]{:S(2)}, u32[]{:S(2)}) %all-to-all-start.5) | async-done | bytes 98336 | tf_op jit(solution)/shard_map/all_to_all | solution.py:197
  162.2 3.4 %all-to-all-start.6 = ((bf16[8,12,512]{2,1,0:T(8,128)(2,1)}), bf16[8,12,512]{2,1,0:T(8,128)(2,1)S(1)}, u32[]{:S(2)}, u32[]{:S(2)}) async-start(bf16[8,12,512]{2,1,0:T(8,128)(2,1)} %all_to_all.71), calls=%async_computation.6 | async-start | bytes 262144 | tf_op jit(solution)/shard_map/all_to_all | solution.py:198
  165.9 2.0 gather_fusion.9
  167.9 2.0 gather_fusion.11
  169.9 1.7 all-to-all-done.6
  171.7 2.0 gather_fusion.13
  173.7 1.4 fusion.64
  175.1 34.6 %all-reduce.2.cloned.1.call-done = bf16[64,1024]{1,0:T(8,128)(2,1)} async-done(((bf16[64,1024]{1,0:T(8,128)(2,1)}), bf16[64,1024]{1,0:T(8,128)(2,1)}) %all-reduce.2.cloned.1.call-update) | async-done | bytes 131088 | tf_op jit(solution)/shard_map/psum | solution.py:167
  209.7 1.6 convert_multiply_fusion
  (167 shorter events, 18.3 us)
Async XLA Ops:
  7.2 19.5 %copy-start = (bf16[1,512,1024]{2,1,0:T(8,128)(2,1)S(1)}, bf16[1,512,1024]{2,1,0:T(8,128)(2,1)}, u32[]{:S(2)}) copy-start(bf16[1,512,1024]{2,1,0:T(8,128)(2,1)} %param.22) | copy-start | bytes 3145732
  7.2 8.2 %copy-start.1 = (bf16[1,512,512]{2,1,0:T(8,128)(2,1)S(1)}, bf16[1,512,512]{2,1,0:T(8,128)(2,1)}, u32[]{:S(2)}) copy-start(bf16[1,512,512]{2,1,0:T(8,128)(2,1)} %param.20) | copy-start | bytes 1572868
  7.2 9.0 %copy-start.2 = (bf16[1,512,512]{2,1,0:T(8,128)(2,1)S(1)}, bf16[1,512,512]{2,1,0:T(8,128)(2,1)}, u32[]{:S(2)}) copy-start(bf16[1,512,512]{2,1,0:T(8,128)(2,1)} %param.21) | copy-start | bytes 1572868
  17.8 12.0 %all-to-all-start = ((bf16[8,12,512]{2,1,0:T(8,128)(2,1)}), bf16[8,12,512]{2,1,0:T(8,128)(2,1)S(1)}, u32[]{:S(2)}, u32[]{:S(2)}) async-start(bf16[8,12,512]{2,1,0:T(8,128)(2,1)} %all_to_all.54), calls=%async_computation | async-start | bytes 262144 | tf_op jit(solution)/shard_map/all_to_all | solution.py:124
  23.0 62.3 %all-gather.4.cloned.1.call-start = ((), (), s32[]{:S(2)}) async-start(), calls=%async_computation.8 | async-start | bytes 1179648 | tf_op jit(solution)/shard_map/all_gather | solution.py:140
  29.8 11.1 %all-to-all-start.1 = ((bf16[8,12,512]{2,1,0:T(8,128)(2,1)}), bf16[8,12,512]{2,1,0:T(8,128)(2,1)S(1)}, u32[]{:S(2)}, u32[]{:S(2)}) async-start(bf16[8,12,512]{2,1,0:T(8,128)(2,1)} %all_to_all.57), calls=%async_computation.1 | async-start | bytes 262144 | tf_op jit(solution)/shard_map/all_to_all | solution.py:125
  40.9 10.2 %all-to-all-start.2 = ((bf16[8,12,512]{2,1,0:T(8,128)(2,1)}), bf16[8,12,512]{2,1,0:T(8,128)(2,1)S(1)}, u32[]{:S(2)}, u32[]{:S(2)}) async-start(bf16[8,12,512]{2,1,0:T(8,128)(2,1)} %all_to_all.60), calls=%async_computation.2 | async-start | bytes 262144 | tf_op jit(solution)/shard_map/all_to_all | solution.py:126
  51.1 33.5 %all-to-all-start.3 = ((bf16[8,12,1024]{2,1,0:T(8,128)(2,1)}), bf16[8,12,1024]{2,1,0:T(8,128)(2,1)S(1)}, u32[]{:S(2)}, u32[]{:S(2)}) async-start(bf16[8,12,1024]{2,1,0:T(8,128)(2,1)} %select_select_fusion.3), calls=%async_computation.3 | async-start | bytes 524288 | tf_op jit(solution)/shard_map/all_to_all | solution.py:127
  54.5 119.2 %reduce-scatter.2.cloned.1.call-start = ((), (), s32[]{:S(2)}) async-start(), calls=%async_computation.9 | async-start | bytes 1179648 | tf_op jit(solution)/shard_map/reduce_scatter | solution.py:164
  115.1 17.8 %copy-start.4 = (bf16[8,48,64]{2,1,0:T(8,128)(2,1)S(1)}, bf16[8,48,64]{2,1,0:T(8,128)(2,1)}, u32[]{:S(2)}) copy-start(bf16[8,48,64]{2,1,0:T(8,128)(2,1)} %get-tuple-element.111) | copy-start | bytes 147460
  133.0 1.5 copy-start.3
  139.7 1.7 copy-start.5
  143.2 8.8 %all-to-all-start.4 = ((bf16[8,12,512]{2,1,0:T(8,128)(2,1)}), bf16[8,12,512]{2,1,0:T(8,128)(2,1)S(1)}, u32[]{:S(2)}, u32[]{:S(2)}) async-start(bf16[8,12,512]{2,1,0:T(8,128)(2,1)} %all_to_all.65), calls=%async_computation.4 | async-start | bytes 262144 | tf_op jit(solution)/shard_map/all_to_all | solution.py:196
  152.0 10.3 %all-to-all-start.5 = ((bf16[8,12,512]{2,1,0:T(8,128)(2,1)}), bf16[8,12,512]{2,1,0:T(8,128)(2,1)S(1)}, u32[]{:S(2)}, u32[]{:S(2)}) async-start(bf16[8,12,512]{2,1,0:T(8,128)(2,1)} %all_to_all.68), calls=%async_computation.5 | async-start | bytes 262144 | tf_op jit(solution)/shard_map/all_to_all | solution.py:197
  162.2 9.4 %all-to-all-start.6 = ((bf16[8,12,512]{2,1,0:T(8,128)(2,1)}), bf16[8,12,512]{2,1,0:T(8,128)(2,1)S(1)}, u32[]{:S(2)}, u32[]{:S(2)}) async-start(bf16[8,12,512]{2,1,0:T(8,128)(2,1)} %all_to_all.71), calls=%async_computation.6 | async-start | bytes 262144 | tf_op jit(solution)/shard_map/all_to_all | solution.py:198
  165.6 44.0 %all-reduce.2.cloned.1.call-start = ((), (), s32[]{:S(2)}) async-start(), calls=%async_computation.10 | async-start | bytes 262144 | tf_op jit(solution)/shard_map/psum | solution.py:167
Sparse Core Ops, SparseCore 0:
  25.7 27.5 all-gather.3
  134.6 38.3 reduce-scatter.1
  175.3 34.3 all-reduce.1
where the time goes:
time: 219 us; the launch traced here: 218 us
  waiting for transfers between devices  59 us (27%)
  blocking collectives  55 us (25%)
  starting transfers between devices  26.6 us (12%)
  matrix products  23 us (11%)
  local copies, waits for them, and re-layouts  22.3 us (10%)
  between operations  16.3 us (7%)
  other arithmetic  15.3 us (7%)
    psum x1, waiting for transfers between devices, local(): clip_sum = lax.psum(seq_sum, 'clip').astype(jnp.float32)  34.6 us
    all_gather x1, blocking collectives, local(): lax.all_gather(key_pack, 'seq', axis=0, tiled=True)  9.95 us
    all_gather x1, blocking collectives, local(): lax.all_gather(value_pack, 'seq', axis=0, tiled=True)  9.54 us
    all_gather x1, blocking collectives, local(): lax.all_gather(output_grad, 'seq', axis=0, tiled=True)  9.54 us
    all_gather x1, blocking collectives, local(): lax.all_gather(inner_rows, 'seq', axis=0, tiled=True)  9.06 us
    all_gather x1, blocking collectives, local(): lax.all_gather(query_pack, 'seq', axis=0, tiled=True)  8.62 us
    all_gather x1, blocking collectives, local(): lax.all_gather(log_rows, 'seq', axis=0, tiled=True)  8.29 us
    dot_general x8, matrix products, query_side(): jnp.dot(dscores, key_head, preferred_element_type=jnp.float32) * factor  6.93 us
  transfers between devices with their start and end apart: 10, of which 6 were waited for; matrix products, arithmetic and copies ran while one was open for 11% of the time, Pallas kernels for 0%

commit v1 on v0

--- a/solution.py
+++ b/solution.py
@@ -1,6 +1,8 @@
 import jax
 import jax.numpy as jnp
 from jax import lax
+from jax.experimental import pallas as pl
+from jax.experimental.pallas import tpu as pltpu
 from jax.sharding import PartitionSpec as P
 
 HEADS = 8
@@ -91,7 +93,7 @@
     return (key_parts, value_parts)
 
 
-def local(queries, keys, values, out_cotangent, visible_counts, span_offset, out_weight):
+def by_rows(queries, keys, values, out_cotangent, visible_counts, span_offset, out_weight):
     devices = lax.axis_size("seq")
     device = lax.axis_index("seq")
     frames = queries.shape[1]
@@ -216,6 +218,268 @@
     return (placed(returned[0]), placed(returned[1]), placed(returned[2]), weight_grad)
 
 
+ROUTES = (0, 2, 4, 6)
+
+
+def head_lanes(core):
+    lane = lax.broadcasted_iota(jnp.int32, (1, 128), 1)
+    return ((lane // HD) == core).astype(jnp.float32).astype(jnp.bfloat16)
+
+
+def span_of(counts_ref, offsets_ref, owner):
+    count = counts_ref[0, owner]
+    begin = lax.rem(offsets_ref[0, owner], count + 1)
+    return begin, MAXV - (count - begin)
+
+
+def slot_masks(begin, end_start):
+    slot = lax.broadcasted_iota(jnp.int32, (MAXV, 1), 0)
+    early = (slot < begin).astype(jnp.float32).astype(jnp.bfloat16)
+    late = (slot >= end_start).astype(jnp.float32).astype(jnp.bfloat16)
+    return early, late
+
+
+def pack_kernel(counts_ref, offsets_ref, q_ref, k_ref, v_ref, g_ref, *rest):
+    sends, cot_ref, narrow, wide, sems = rest[:4], rest[4], rest[5], rest[6], rest[7]
+    frames = q_ref.shape[1]
+    last = frames - MAXV
+    device = lax.axis_index("seq")
+    copies = []
+    for index, source in enumerate((q_ref, k_ref, v_ref)):
+        for side, start in enumerate((0, last)):
+            copies.append(
+                pltpu.make_async_copy(
+                    source.at[0, pl.ds(start, MAXV)], narrow.at[index, side], sems.at[len(copies)]
+                )
+            )
+    for side, start in enumerate((0, last)):
+        copies.append(
+            pltpu.make_async_copy(
+                g_ref.at[0, pl.ds(start, MAXV)], wide.at[side], sems.at[len(copies)]
+            )
+        )
+    for copy in copies:
+        copy.start()
+    begin, end_start = span_of(counts_ref, offsets_ref, device)
+    early, late = slot_masks(begin, end_start)
+    for copy in copies:
+        copy.wait()
+    for route, send in zip(ROUTES, sends):
+        chip = (device ^ route) // 2
+        lanes = pl.ds(pl.multiple_of(chip * 128, 128), 128)
+        for index in range(3):
+            send[:, index * 128 : (index + 1) * 128] = (
+                narrow[index, 0, :, lanes] * early + narrow[index, 1, :, lanes] * late
+            )
+    cot_ref[...] = wide[0] * early + wide[1] * late
+
+
+def attend_kernel(counts_ref, offsets_ref, w_ref, *rest):
+    blocks, cots = rest[:8], rest[8:16]
+    outs, wg_ref = rest[16:24], rest[24]
+    packed, cot, dout, dq, sems = rest[25:]
+    device = lax.axis_index("seq")
+    core = device % 2
+    copies = []
+    for index in range(8):
+        rows = pl.ds(index * MAXV, MAXV)
+        copies.append(pltpu.make_async_copy(blocks[index], packed.at[rows], sems.at[index]))
+        copies.append(pltpu.make_async_copy(cots[index], cot.at[rows], sems.at[8 + index]))
+    for copy in copies:
+        copy.start()
+    lanes = head_lanes(core)
+    top = (core == 0).astype(jnp.float32).astype(jnp.bfloat16)
+    bottom = (core == 1).astype(jnp.float32).astype(jnp.bfloat16)
+    w_both = jnp.concatenate([w_ref[...] * top, w_ref[...] * bottom], axis=0)
+    dead = []
+    for index in range(8):
+        begin, end_start = span_of(counts_ref, offsets_ref, device ^ index)
+        slot = lax.broadcasted_iota(jnp.int32, (MAXV, 256), 0)
+        dead.append((slot >= begin) & (slot < end_start))
+    dead = jnp.concatenate(dead, axis=0)
+    for copy in copies:
+        copy.wait()
+    factor = HD ** (-0.5)
+    dout[...] = lax.dot_general(
+        cot[...], w_both, (((1,), (1,)), ((), ())), preferred_element_type=jnp.float32
+    ).astype(jnp.bfloat16)
+    key = packed[:, 128:256] * lanes
+    value = packed[:, 256:384]
+    key_t = key.T
+    value_t = value.T
+    dout_t = dout[...].astype(jnp.float32).T
+    key_grad = jnp.zeros((8 * MAXV, 128), jnp.float32)
+    value_grad = jnp.zeros((8 * MAXV, 128), jnp.float32)
+    attended = []
+    for step in range(3):
+        rows = slice(step * 256, (step + 1) * 256)
+        query = packed[rows, 0:128]
+        query_own = query * lanes
+        dout_own = dout[rows, :]
+        scores = (
+            lax.dot_general(
+                key, query, (((1,), (1,)), ((), ())), preferred_element_type=jnp.float32
+            )
+            * factor
+        )
+        scores = jnp.where(dead, -1e30, scores)
+        scores = jnp.exp(scores - jnp.max(scores, axis=0, keepdims=True))
+        weights = scores * (1.0 / jnp.sum(scores, axis=0, keepdims=True))
+        low = weights.astype(jnp.bfloat16)
+        att = jnp.dot(value_t, low, preferred_element_type=jnp.float32).astype(jnp.bfloat16)
+        attended.append(att)
+        inner = jnp.sum(dout_t[:, rows] * att.astype(jnp.float32), axis=0, keepdims=True)
+        dweights = lax.dot_general(
+            value, dout_own, (((1,), (1,)), ((), ())), preferred_element_type=jnp.float32
+        )
+        dscores = (weights * (dweights - inner)).astype(jnp.bfloat16)
+        value_grad += jnp.dot(low, dout_own, preferred_element_type=jnp.float32)
+        key_grad += jnp.dot(dscores, query_own, preferred_element_type=jnp.float32)
+        dq_t = jnp.dot(key_t, dscores, preferred_element_type=jnp.float32) * factor
+        dq[rows, :] = dq_t.T.astype(jnp.bfloat16)
+    key_grad = (key_grad * factor).astype(jnp.bfloat16)
+    value_grad = value_grad.astype(jnp.bfloat16)
+    for index in range(8):
+        rows = slice(index * MAXV, (index + 1) * MAXV)
+        outs[index][:, 0:128] = dq[rows, :]
+        outs[index][:, 128:256] = key_grad[rows]
+        outs[index][:, 256:384] = value_grad[rows]
+    att = jnp.concatenate(attended, axis=1)
+    att = jnp.where(core == 0, att[:HD].astype(jnp.float32), att[HD:].astype(jnp.float32))
+    wg_ref[...] = jnp.dot(
+        att.astype(jnp.bfloat16), cot[...], preferred_element_type=jnp.float32
+    ).astype(jnp.bfloat16)
+
+
+def combine_kernel(*refs):
+    for index in range(4):
+        refs[8 + index][...] = refs[index][...] + refs[4 + index][...]
+
+
+def unpack_kernel(counts_ref, offsets_ref, *rest):
+    blocks, outs = rest[:4], rest[4:7]
+    edges, blank, sems = rest[7:]
+    device = lax.axis_index("seq")
+    frames = outs[0].shape[1]
+    last = frames - MAXV
+    blank[...] = jnp.zeros_like(blank)
+    copies = []
+    for index in range(3):
+        copies.append(
+            pltpu.make_async_copy(
+                blank, outs[index].at[0, pl.ds(MAXV, last - MAXV)], sems.at[index]
+            )
+        )
+        copies[-1].start()
+    begin, end_start = span_of(counts_ref, offsets_ref, device)
+    sides = slot_masks(begin, end_start)
+    for route, block in zip(ROUTES, blocks):
+        chip = (device ^ route) // 2
+        lanes = pl.ds(pl.multiple_of(chip * 128, 128), 128)
+        for index in range(3):
+            piece = block[:, index * 128 : (index + 1) * 128]
+            for side in range(2):
+                edges[index, side, :, lanes] = piece * sides[side]
+    for index in range(3):
+        for side, start in enumerate((0, last)):
+            copies.append(
+                pltpu.make_async_copy(
+                    edges.at[index, side],
+                    outs[index].at[0, pl.ds(start, MAXV)],
+                    sems.at[len(copies)],
+                )
+            )
+            copies[-1].start()
+    for copy in copies:
+        copy.wait()
+
+
+ANYWHERE = pl.BlockSpec(memory_space=pl.ANY)
+SCALARS = pl.BlockSpec(memory_space=pltpu.SMEM)
+LOCAL = pl.BlockSpec(memory_space=pltpu.VMEM)
+
+
+def by_heads(queries, keys, values, out_cotangent, visible_counts, span_offset, out_weight):
+    bf16 = jnp.bfloat16
+    pairs = lax.axis_size("seq")
+    clips = lax.axis_size("clip")
+
+    def shift(block, step):
+        return lax.ppermute(block, "seq", [(i, i ^ step) for i in range(pairs)])
+
+    narrow = jax.ShapeDtypeStruct((MAXV, 384), bf16)
+    wide = jax.ShapeDtypeStruct((MAXV, out_cotangent.shape[2]), bf16)
+    *sends, cot = pl.pallas_call(
+        pack_kernel,
+        out_shape=[narrow] * 4 + [wide],
+        in_specs=[SCALARS] * 2 + [ANYWHERE] * 4,
+        out_specs=[LOCAL] * 5,
+        scratch_shapes=[
+            pltpu.VMEM((3, 2, MAXV, queries.shape[2]), bf16),
+            pltpu.VMEM((2, MAXV, out_cotangent.shape[2]), bf16),
+            pltpu.SemaphoreType.DMA((8,)),
+        ],
+        name="pack",
+    )(visible_counts, span_offset, queries, keys, values, out_cotangent)
+    even = [sends[0]] + [shift(sends[i], ROUTES[i]) for i in (1, 2, 3)]
+    even_cot = [cot] + [shift(cot, ROUTES[i]) for i in (1, 2, 3)]
+    odd = [shift(block, 1) for block in even]
+    odd_cot = [shift(block, 1) for block in even_cot]
+    blocks = [block for pair in zip(even, odd) for block in pair]
+    cots = [block for pair in zip(even_cot, odd_cot) for block in pair]
+    *grads, partial = pl.pallas_call(
+        attend_kernel,
+        out_shape=[narrow] * 8 + [jax.ShapeDtypeStruct(out_weight.shape, bf16)],
+        in_specs=[SCALARS] * 2 + [LOCAL] + [ANYWHERE] * 16,
+        out_specs=[LOCAL] * 9,
+        scratch_shapes=[
+            pltpu.VMEM((8 * MAXV, 384), bf16),
+            pltpu.VMEM((8 * MAXV, out_cotangent.shape[2]), bf16),
+            pltpu.VMEM((8 * MAXV, 128), bf16),
+            pltpu.VMEM((8 * MAXV, 128), bf16),
+            pltpu.SemaphoreType.DMA((16,)),
+        ],
+        name="attend",
+    )(visible_counts, span_offset, out_weight, *blocks, *cots)
+    crossed = [shift(grads[i + 1], 1) for i in ROUTES]
+    joined = pl.pallas_call(
+        combine_kernel,
+        out_shape=[narrow] * 4,
+        in_specs=[LOCAL] * 8,
+        out_specs=[LOCAL] * 4,
+        name="combine",
+    )(*[grads[i] for i in ROUTES], *crossed)
+    home = [joined[0]] + [shift(joined[i], ROUTES[i]) for i in (1, 2, 3)]
+    full = jax.ShapeDtypeStruct(queries.shape, bf16)
+    frames = queries.shape[1]
+    outs = pl.pallas_call(
+        unpack_kernel,
+        out_shape=[full] * 3,
+        in_specs=[SCALARS] * 2 + [LOCAL] * 4,
+        out_specs=[ANYWHERE] * 3,
+        scratch_shapes=[
+            pltpu.VMEM((3, 2, MAXV, queries.shape[2]), bf16),
+            pltpu.VMEM((frames - 2 * MAXV, queries.shape[2]), bf16),
+            pltpu.SemaphoreType.DMA((9,)),
+        ],
+        name="unpack",
+    )(visible_counts, span_offset, *home)
+    step = 1
+    while step < clips:
+        other = lax.ppermute(partial, "clip", [(i, i ^ step) for i in range(clips)])
+        total = partial.astype(jnp.float32) + other.astype(jnp.float32)
+        partial = total.astype(bf16)
+        step *= 2
+    weight_grad = total * (clips * VIS_DEV * pairs) ** (-0.5)
+    return (*outs, weight_grad)
+
+
+def local(*arrays):
+    if lax.axis_size("seq") == HEADS and lax.axis_size("clip") in (2, 4, 8, 16):
+        return by_heads(*arrays)
+    return by_rows(*arrays)
+
+
 def solution(mesh):
     placed = (
         P("clip", "seq", None),

time: 219 us -> 60.7 us (0.28)
  blocking collectives: 55 us -> 0 us
  waiting for transfers between devices: 59 us -> 20.8 us
  matrix products: 23 us -> 0 us
  local copies, waits for them, and re-layouts: 22.3 us -> 2.68 us
  between operations: 16.3 us -> 0.86 us
  Pallas kernels: 0 us -> 14.3 us
  other arithmetic: 15.3 us -> 1.68 us
  starting transfers between devices: 26.6 us -> 20 us
    all_gather x6 -> x0, blocking collectives: 55 us -> none  [the longest x1 9.95 us: local(): lax.all_gather(key_pack, 'seq', axis=0, tiled=True)]
    psum x1 -> x0, waiting for transfers between devices: 34.6 us -> none  [local(): clip_sum = lax.psum(seq_sum, 'clip').astype(jnp.float32)]
    all_to_all x7 -> x0, starting transfers between devices: 26.3 us -> none  [the longest x1 5.2 us: local(): lax.all_to_all(outgoing(queries), 'seq', split_axis=0, concat_axis=0, til...]
    all_to_all x7 -> x0, waiting for transfers between devices: 23.6 us -> none  [the longest x1 6.88 us: local(): lax.all_to_all(outgoing(keys), 'seq', split_axis=0, concat_axis=0, tiled=...]
    dot_general x50 -> x0, matrix products: 23 us -> none  [the longest x8 6.93 us: query_side(): jnp.dot(dscores, key_head, preferred_element_type=jnp.float32) * factor]
    ppermute x0 -> x23, waiting for transfers between devices: none -> 20.8 us  [the longest x21 17.4 us: shift(): return lax.ppermute(block, 'seq', [(i, i ^ step) for i in range(pairs)])]
    ppermute x0 -> x23, starting transfers between devices: none -> 20 us  [the longest x21 15.7 us: shift(): return lax.ppermute(block, 'seq', [(i, i ^ step) for i in range(pairs)])]
    gather x15 -> x0, local copies, waits for them, and re-layouts: 15.2 us -> none  [the longest x3 5.91 us: placed(): jnp.take(block, frame_row, axis=0)]
  transfers between devices with their start and end apart: 10 -> 23, of which waited for: 6 -> 9; matrix products, arithmetic and copies ran while one was open for 11% -> 2% of each run, Pallas kernels for 0% -> 7%
where the time goes in v1:
time: 60.7 us; the launch traced here: 60.4 us
  waiting for transfers between devices  20.8 us (34%)
  starting transfers between devices  20 us (33%)
  Pallas kernels  14.3 us (24%)
  local copies, waits for them, and re-layouts  2.68 us (4%)
  other arithmetic  1.68 us (3%)
  between operations  0.86 us (1%)
    ppermute x21, waiting for transfers between devices, shift(): return lax.ppermute(block, 'seq', [(i, i ^ step) for i in range(pairs)])  17.4 us
    ppermute x21, starting transfers between devices, shift(): return lax.ppermute(block, 'seq', [(i, i ^ step) for i in range(pairs)])  15.7 us
    pallas_call x1, Pallas kernels, by_heads(): pl.pallas_call(attend_kernel, out_shape=[narrow] * 8 + [jax.ShapeDtypeStr...  7.38 us
    ppermute x2, starting transfers between devices, by_heads(): other = lax.ppermute(partial, 'clip', [(i, i ^ step) for i in range(clips)])  4.29 us
    ppermute x2, waiting for transfers between devices, by_heads(): other = lax.ppermute(partial, 'clip', [(i, i ^ step) for i in range(clips)])  3.37 us
    pallas_call x1, Pallas kernels, by_heads(): pl.pallas_call(pack_kernel, out_shape=[narrow] * 4 + [wide], in_specs=[SC...  2.87 us
    unnamed x42, local copies, waits for them, and re-layouts  2.68 us
    pallas_call x1, Pallas kernels, by_heads(): pl.pallas_call(unpack_kernel, out_shape=[full] * 3, in_specs=[SCALARS] *...  2.23 us
  transfers between devices with their start and end apart: 23, of which 9 were waited for; matrix products, arithmetic and copies ran while one was open for 2% of the time, Pallas kernels for 7%

profile of v1, /device:TPU:0, one launch (start us, length us, event | category | flops | bytes accessed | tf_op | source)
XLA Modules:
  0.0 60.4 jit_solution(3277740395997303661)
XLA Ops:
  0.6 2.9 %pack.1 = (bf16[96,384]{1,0:T(8,128)(2,1)}, bf16[96,384]{1,0:T(8,128)(2,1)}, bf16[96,384]{1,0:T(8,128)(2,1)}, bf16[96,384]{1,0:T(8,128)(2,1)}, bf16[96,1024]{1,0:T(8,128)(2,1)}) custom-call(s32[1,8]{1,0:T(1,128)} %counts_ref.5, s32[1,8]{1,0:T(1,128)} %offsets_ref.5, bf16[1,512,512]{2,1,0:T(8,128)(2,1)} %q_ref.1, bf16[1,512,512]{2,1,0:T(8,128)(2,1)} %k_ref.1, ...), custom_call_target="tpu_custom_call" | custom-call | tf_op jit(solution)/shard_map/pack/pallas_call | solution.py:412
  3.5 4.0 %collective-permute-start.12 = (bf16[96,1024]{1,0:T(8,128)(2,1)}, bf16[96,1024]{1,0:T(8,128)(2,1)S(1)}, u32[]{:S(2)}, u32[]{:S(2)}) collective-permute-start(bf16[96,1024]{1,0:T(8,128)(2,1)} %get-tuple-element.29.rest_8_), channel_id=1, source_target_pairs={{0,24},{4,28},{8,16},{12,20},{16,8},{20,12},{24,0},{28,4},{1,25},{... | collective-permute-start | bytes 589832 | tf_op jit(solution)/shard_map/ppermute | solution.py:408
  7.5 0.5 collective-permute-start.10
  8.0 0.1 collective-permute-start.8
  8.1 1.9 %collective-permute-start.1 = (bf16[96,384]{1,0:T(8,128)(2,1)}, bf16[96,384]{1,0:T(8,128)(2,1)S(1)}, u32[]{:S(2)}, u32[]{:S(2)}) collective-permute-start(bf16[96,384]{1,0:T(8,128)(2,1)} %get-tuple-element.26), channel_id=1, source_target_pairs={{0,8},{4,12},{8,0},{12,4},{16,24},{20,28},{24,16},{28,20},{1,9},{5... | collective-permute-start | bytes 221192 | tf_op jit(solution)/shard_map/ppermute | solution.py:408
  10.0 1.5 %collective-permute-start.3 = (bf16[96,384]{1,0:T(8,128)(2,1)}, bf16[96,384]{1,0:T(8,128)(2,1)S(1)}, u32[]{:S(2)}, u32[]{:S(2)}) collective-permute-start(bf16[96,384]{1,0:T(8,128)(2,1)} %get-tuple-element.27), channel_id=1, source_target_pairs={{0,16},{4,20},{8,24},{12,28},{16,0},{20,4},{24,8},{28,12},{1,17},{... | collective-permute-start | bytes 221192 | tf_op jit(solution)/shard_map/ppermute | solution.py:408
  11.6 7.1 %collective-permute-done.1.rest_2_ = bf16[96,384]{1,0:T(8,128)(2,1)S(1)} collective-permute-done((bf16[96,384]{1,0:T(8,128)(2,1)}, bf16[96,384]{1,0:T(8,128)(2,1)S(1)}, u32[]{:S(2)}, u32[]{:S(2)}) %collective-permute-start.1) | collective-permute-done | bytes 73760 | tf_op jit(solution)/shard_map/ppermute | solution.py:408
  18.7 1.4 %collective-permute-start.5 = (bf16[96,384]{1,0:T(8,128)(2,1)}, bf16[96,384]{1,0:T(8,128)(2,1)S(1)}, u32[]{:S(2)}, u32[]{:S(2)}) collective-permute-start(bf16[96,384]{1,0:T(8,128)(2,1)} %get-tuple-element.28), channel_id=1, source_target_pairs={{0,24},{4,28},{8,16},{12,20},{16,8},{20,12},{24,0},{28,4},{1,25},{... | collective-permute-start | bytes 221192 | tf_op jit(solution)/shard_map/ppermute | solution.py:408
  20.1 0.0 collective-permute-done.3.rest_4_
  20.1 0.0 collective-permute-start
  20.1 4.0 %collective-permute-done.5.rest_6_ = bf16[96,384]{1,0:T(8,128)(2,1)S(1)} collective-permute-done((bf16[96,384]{1,0:T(8,128)(2,1)}, bf16[96,384]{1,0:T(8,128)(2,1)S(1)}, u32[]{:S(2)}, u32[]{:S(2)}) %collective-permute-start.5) | collective-permute-done | bytes 73760 | tf_op jit(solution)/shard_map/ppermute | solution.py:408
  24.2 0.0 collective-permute-start.2
  24.2 0.0 collective-permute-done.rest_1_
  24.2 0.5 collective-permute-start.7
  24.7 0.0 collective-permute-done.12.rest_14_
  24.7 0.1 collective-permute-start.13
  24.8 0.0 collective-permute-done.10.rest_12_
  24.8 0.4 collective-permute-start.11
  25.2 0.0 collective-permute-done.8.rest_10_
  25.2 0.1 collective-permute-start.9
  25.3 0.1 collective-permute-done.2.rest_3_
  25.4 0.3 collective-permute-start.4
  25.7 1.2 %collective-permute-done.4.rest_5_ = bf16[96,384]{1,0:T(8,128)(2,1)S(1)} collective-permute-done((bf16[96,384]{1,0:T(8,128)(2,1)S(1)}, bf16[96,384]{1,0:T(8,128)(2,1)S(1)}, u32[]{:S(2)}, u32[]{:S(2)}) %collective-permute-start.4) | collective-permute-done | bytes 73760 | tf_op jit(solution)/shard_map/ppermute | solution.py:408
  26.9 0.4 collective-permute-start.6
  27.3 0.9 %collective-permute-done.6.rest_7_ = bf16[96,384]{1,0:T(8,128)(2,1)S(1)} collective-permute-done((bf16[96,384]{1,0:T(8,128)(2,1)S(1)}, bf16[96,384]{1,0:T(8,128)(2,1)S(1)}, u32[]{:S(2)}, u32[]{:S(2)}) %collective-permute-start.6) | collective-permute-done | bytes 73760 | tf_op jit(solution)/shard_map/ppermute | solution.py:408
  28.2 0.0 collective-permute-done.7.rest_9_
  28.2 0.0 collective-permute-done.13.rest_15_
  28.2 0.0 collective-permute-done.11.rest_13_
  28.2 0.0 collective-permute-done.9.rest_11_
  28.3 0.5 copy-done.16
  28.8 0.1 copy-done.3
  28.9 0.1 copy-done.4
  29.0 0.0 copy-done.5
  29.0 0.7 %copy-done.6 = bf16[96,1024]{1,0:T(8,128)(2,1)} copy-done((bf16[96,1024]{1,0:T(8,128)(2,1)}, bf16[96,1024]{1,0:T(8,128)(2,1)S(1)}, u32[]{:S(2)}) %copy-start.6) | copy-done | bytes 196632
  29.7 7.4 %attend.1 = (bf16[96,384]{1,0:T(8,128)(2,1)}, bf16[96,384]{1,0:T(8,128)(2,1)}, bf16[96,384]{1,0:T(8,128)(2,1)}, bf16[96,384]{1,0:T(8,128)(2,1)}, bf16[96,384]{1,...) custom-call(s32[1,8]{1,0:T(1,128)} %counts_ref.5, ...), custom_call_target="tpu_custom_call" | custom-call | tf_op jit(solution)/shard_map/attend/pallas_call | solution.py:430
  37.1 1.6 %collective-permute-start.21 = (bf16[64,1024]{1,0:T(8,128)(2,1)}, bf16[64,1024]{1,0:T(8,128)(2,1)S(1)}, u32[]{:S(2)}, u32[]{:S(2)}) collective-permute-start(bf16[64,1024]{1,0:T(8,128)(2,1)} %get-tuple-element.45), channel_id=1, source_target_pairs={{0,1},{1,0},{2,3},{3,2},{4,5},{5,4},{6,7},{7,6},{8,9},{9,8},{10,11... | collective-permute-start | bytes 393224 | tf_op jit(solution)/shard_map/ppermute | solution.py:469
  38.7 0.1 collective-permute-start.14
  38.8 0.4 collective-permute-start.15
  39.2 0.1 collective-permute-start.16
  39.3 0.4 collective-permute-start.17
  39.7 3.4 %collective-permute-done.21 = bf16[64,1024]{1,0:T(8,128)(2,1)S(1)} collective-permute-done((bf16[64,1024]{1,0:T(8,128)(2,1)}, bf16[64,1024]{1,0:T(8,128)(2,1)S(1)}, u32[]{:S(2)}, u32[]{:S(2)}) %collective-permute-start.21) | collective-permute-done | bytes 131104 | tf_op jit(solution)/shard_map/ppermute | solution.py:469
  43.1 0.9 %add_convert_fusion = bf16[64,1024]{1,0:T(8,128)(2,1)S(1)} fusion(bf16[64,1024]{1,0:T(8,128)(2,1)S(1)} %collective-permute-done.21, bf16[64,1024]{1,0:T(8,128)(2,1)} %get-tuple-element.45), kind=kLoop, calls=%fused_computation.1 | loop fusion | flops 262144 | bytes 393216 | tf_op jit(solution)/shard_map/convert_element_type | solution.py:471
  44.1 2.7 %collective-permute-start.22 = (bf16[64,1024]{1,0:T(8,128)(2,1)S(1)}, bf16[64,1024]{1,0:T(8,128)(2,1)S(1)}, u32[]{:S(2)}, u32[]{:S(2)}) collective-permute-start(bf16[64,1024]{1,0:T(8,128)(2,1)S(1)} %add_convert_fusion), channel_id=1, source_target_pairs={{0,2},{1,3},{2,0},{3,1},{4,6},{5,7},{6,4},{7,5},{8,10},{9,11},{10,... | collective-permute-start | bytes 393224 | tf_op jit(solution)/shard_map/ppermute | solution.py:469
  46.7 0.0 collective-permute-done.14.refs_4_
  46.7 0.0 collective-permute-done.15.refs_5_
  46.7 0.0 copy-start.14
  46.7 0.0 collective-permute-done.16.refs_6_
  46.7 0.0 copy-start.15
  46.8 0.0 copy-start.17
  46.8 0.6 copy-done.12
  47.4 0.0 copy-done.14
  47.4 0.0 copy-done.15
  47.4 0.0 copy-done.17
  47.4 1.9 %combine.1 = (bf16[96,384]{1,0:T(8,128)(2,1)}, bf16[96,384]{1,0:T(8,128)(2,1)}, bf16[96,384]{1,0:T(8,128)(2,1)}, bf16[96,384]{1,0:T(8,128)(2,1)}) custom-call(bf16[96,384]{1,0:T(8,128)(2,1)} %get-tuple-element.30.refs_0_, bf16[96,384]{1,0:T(8,128)(2,1)} %get-tuple-element.31.refs_1_, bf16[96,384]{1,0:T(8,128)(2,1)} %get-tuple-element.32.refs_2_, ...), custom_call_target="tpu_custom_call" | custom-call | tf_op jit(solution)/shard_map/combine/pallas_call | solution.py:445
  49.3 1.5 %collective-permute-start.18 = (bf16[96,384]{1,0:T(8,128)(2,1)}, bf16[96,384]{1,0:T(8,128)(2,1)S(1)}, u32[]{:S(2)}, u32[]{:S(2)}) collective-permute-start(bf16[96,384]{1,0:T(8,128)(2,1)} %get-tuple-element.39), channel_id=1, source_target_pairs={{0,8},{4,12},{8,0},{12,4},{16,24},{20,28},{24,16},{28,20},{1,9},{5... | collective-permute-start | bytes 221192 | tf_op jit(solution)/shard_map/ppermute | solution.py:408
  50.8 0.5 collective-permute-start.19
  51.3 1.5 %collective-permute-start.20 = (bf16[96,384]{1,0:T(8,128)(2,1)}, bf16[96,384]{1,0:T(8,128)(2,1)S(1)}, u32[]{:S(2)}, u32[]{:S(2)}) collective-permute-start(bf16[96,384]{1,0:T(8,128)(2,1)} %get-tuple-element.41), channel_id=1, source_target_pairs={{0,24},{4,28},{8,16},{12,20},{16,8},{20,12},{24,0},{28,4},{1,25},{... | collective-permute-start | bytes 221192 | tf_op jit(solution)/shard_map/ppermute | solution.py:408
  52.8 1.2 %collective-permute-done.18.rest_1_ = bf16[96,384]{1,0:T(8,128)(2,1)S(1)} collective-permute-done((bf16[96,384]{1,0:T(8,128)(2,1)}, bf16[96,384]{1,0:T(8,128)(2,1)S(1)}, u32[]{:S(2)}, u32[]{:S(2)}) %collective-permute-start.18) | collective-permute-done | bytes 73760 | tf_op jit(solution)/shard_map/ppermute | solution.py:408
  54.0 1.4 %collective-permute-done.19.rest_2_ = bf16[96,384]{1,0:T(8,128)(2,1)S(1)} collective-permute-done((bf16[96,384]{1,0:T(8,128)(2,1)}, bf16[96,384]{1,0:T(8,128)(2,1)S(1)}, u32[]{:S(2)}, u32[]{:S(2)}) %collective-permute-start.19) | collective-permute-done | bytes 73760 | tf_op jit(solution)/shard_map/ppermute | solution.py:408
  55.4 1.4 %collective-permute-done.20.rest_3_ = bf16[96,384]{1,0:T(8,128)(2,1)S(1)} collective-permute-done((bf16[96,384]{1,0:T(8,128)(2,1)}, bf16[96,384]{1,0:T(8,128)(2,1)S(1)}, u32[]{:S(2)}, u32[]{:S(2)}) %collective-permute-start.20) | collective-permute-done | bytes 73760 | tf_op jit(solution)/shard_map/ppermute | solution.py:408
  56.8 0.6 %copy-done.20 = bf16[96,384]{1,0:T(8,128)(2,1)} copy-done((bf16[96,384]{1,0:T(8,128)(2,1)}, bf16[96,384]{1,0:T(8,128)(2,1)S(1)}, u32[]{:S(2)}) %copy-start.20) | copy-done | bytes 73752
  57.4 2.2 %unpack.1 = (bf16[1,512,512]{2,1,0:T(8,128)(2,1)}, bf16[1,512,512]{2,1,0:T(8,128)(2,1)}, bf16[1,512,512]{2,1,0:T(8,128)(2,1)}) custom-call(s32[1,8]{1,0:T(1,128)} %counts_ref.5, s32[1,8]{1,0:T(1,128)} %offsets_ref.5, bf16[96,384]{1,0:T(8,128)(2,1)} %get-tuple-element.38.rest_0_, bf16[96,384]{1,0:T(8,128)(2,1)} %copy-done.18, bf16[96,384]{1,0:T(8,128)(2,1)} %copy-done.19, ...), custom_call_target="tpu_custom_call" | custom-call | tf_op jit(solution)/shard_map/unpack/pallas_call | solution.py:455
  59.6 0.0 collective-permute-done.22
  59.6 0.7 %add_multiply_fusion = f32[64,1024]{1,0:T(8,128)} fusion(bf16[64,1024]{1,0:T(8,128)(2,1)S(1)} %collective-permute-done.22, bf16[64,1024]{1,0:T(8,128)(2,1)S(1)} %add_convert_fusion), kind=kLoop, calls=%fused_computation | loop fusion | flops 262144 | bytes 524288 | tf_op jit(solution)/shard_map/mul | solution.py:473
  (30 shorter events, 0.1 us)
Async XLA Ops:
  3.5 21.2 %collective-permute-start.12 = (bf16[96,1024]{1,0:T(8,128)(2,1)}, bf16[96,1024]{1,0:T(8,128)(2,1)S(1)}, u32[]{:S(2)}, u32[]{:S(2)}) collective-permute-start(bf16[96,1024]{1,0:T(8,128)(2,1)} %get-tuple-element.29.rest_8_), channel_id=1, source_target_pairs={{0,24},{4,28},{8,16},{12,20},{16,8},{20,12},{24,0},{28,4},{1,25},{... | collective-permute-start | bytes 589832 | tf_op jit(solution)/shard_map/ppermute | solution.py:408
  7.5 17.3 %collective-permute-start.10 = (bf16[96,1024]{1,0:T(8,128)(2,1)}, bf16[96,1024]{1,0:T(8,128)(2,1)S(1)}, u32[]{:S(2)}, u32[]{:S(2)}) collective-permute-start(bf16[96,1024]{1,0:T(8,128)(2,1)} %get-tuple-element.29.rest_8_), channel_id=1, source_target_pairs={{0,16},{4,20},{8,24},{12,28},{16,0},{20,4},{24,8},{28,12},{1,17},{... | collective-permute-start | bytes 589832 | tf_op jit(solution)/shard_map/ppermute | solution.py:408
  8.0 17.2 %collective-permute-start.8 = (bf16[96,1024]{1,0:T(8,128)(2,1)}, bf16[96,1024]{1,0:T(8,128)(2,1)S(1)}, u32[]{:S(2)}, u32[]{:S(2)}) collective-permute-start(bf16[96,1024]{1,0:T(8,128)(2,1)} %get-tuple-element.29.rest_8_), channel_id=1, source_target_pairs={{0,8},{4,12},{8,0},{12,4},{16,24},{20,28},{24,16},{28,20},{1,9},{5... | collective-permute-start | bytes 589832 | tf_op jit(solution)/shard_map/ppermute | solution.py:408
  8.1 10.6 %collective-permute-start.1 = (bf16[96,384]{1,0:T(8,128)(2,1)}, bf16[96,384]{1,0:T(8,128)(2,1)S(1)}, u32[]{:S(2)}, u32[]{:S(2)}) collective-permute-start(bf16[96,384]{1,0:T(8,128)(2,1)} %get-tuple-element.26), channel_id=1, source_target_pairs={{0,8},{4,12},{8,0},{12,4},{16,24},{20,28},{24,16},{28,20},{1,9},{5... | collective-permute-start | bytes 221192 | tf_op jit(solution)/shard_map/ppermute | solution.py:408
  10.0 10.1 %collective-permute-start.3 = (bf16[96,384]{1,0:T(8,128)(2,1)}, bf16[96,384]{1,0:T(8,128)(2,1)S(1)}, u32[]{:S(2)}, u32[]{:S(2)}) collective-permute-start(bf16[96,384]{1,0:T(8,128)(2,1)} %get-tuple-element.27), channel_id=1, source_target_pairs={{0,16},{4,20},{8,24},{12,28},{16,0},{20,4},{24,8},{28,12},{1,17},{... | collective-permute-start | bytes 221192 | tf_op jit(solution)/shard_map/ppermute | solution.py:408
  18.7 9.6 %copy-start.7 = (bf16[96,384]{1,0:T(8,128)(2,1)}, bf16[96,384]{1,0:T(8,128)(2,1)S(1)}, u32[]{:S(2)}) copy-start(bf16[96,384]{1,0:T(8,128)(2,1)S(1)} %collective-permute-done.1.rest_2_) | copy-start | bytes 221188
  18.7 5.5 %collective-permute-start.5 = (bf16[96,384]{1,0:T(8,128)(2,1)}, bf16[96,384]{1,0:T(8,128)(2,1)S(1)}, u32[]{:S(2)}, u32[]{:S(2)}) collective-permute-start(bf16[96,384]{1,0:T(8,128)(2,1)} %get-tuple-element.28), channel_id=1, source_target_pairs={{0,24},{4,28},{8,16},{12,20},{16,8},{20,12},{24,0},{28,4},{1,25},{... | collective-permute-start | bytes 221192 | tf_op jit(solution)/shard_map/ppermute | solution.py:408
  20.1 8.1 %copy-start.8 = (bf16[96,384]{1,0:T(8,128)(2,1)}, bf16[96,384]{1,0:T(8,128)(2,1)S(1)}, u32[]{:S(2)}) copy-start(bf16[96,384]{1,0:T(8,128)(2,1)S(1)} %collective-permute-done.3.rest_4_) | copy-start | bytes 221188
  20.1 4.0 %collective-permute-start = (bf16[96,384]{1,0:T(8,128)(2,1)}, bf16[96,384]{1,0:T(8,128)(2,1)S(1)}, u32[]{:S(2)}, u32[]{:S(2)}) collective-permute-start(bf16[96,384]{1,0:T(8,128)(2,1)} %get-tuple-element.25.rest_0_), channel_id=1, source_target_pairs={{0,4},{4,0},{8,12},{12,8},{16,20},{20,16},{24,28},{28,24},{1,5},{5... | collective-permute-start | bytes 221192 | tf_op jit(solution)/shard_map/ppermute | solution.py:408
  24.2 4.1 %copy-start.9 = (bf16[96,384]{1,0:T(8,128)(2,1)}, bf16[96,384]{1,0:T(8,128)(2,1)S(1)}, u32[]{:S(2)}) copy-start(bf16[96,384]{1,0:T(8,128)(2,1)S(1)} %collective-permute-done.5.rest_6_) | copy-start | bytes 221188
  24.2 1.3 %collective-permute-start.2 = (bf16[96,384]{1,0:T(8,128)(2,1)S(1)}, bf16[96,384]{1,0:T(8,128)(2,1)S(1)}, u32[]{:S(2)}, u32[]{:S(2)}) collective-permute-start(bf16[96,384]{1,0:T(8,128)(2,1)S(1)} %collective-permute-done.1.rest_2_), channel_id=1, source_target_pairs={{0,4},{4,0},{8,12},{12,8},{16,20},{20,16},{24,28},{28,24},{1,5},{5... | collective-permute-start | bytes 221192 | tf_op jit(solution)/shard_map/ppermute | solution.py:408
  24.2 4.1 %copy-start.10 = (bf16[96,384]{1,0:T(8,128)(2,1)}, bf16[96,384]{1,0:T(8,128)(2,1)S(1)}, u32[]{:S(2)}) copy-start(bf16[96,384]{1,0:T(8,128)(2,1)S(1)} %collective-permute-done.rest_1_) | copy-start | bytes 221188
  24.2 4.0 %collective-permute-start.7 = (bf16[96,1024]{1,0:T(8,128)(2,1)}, bf16[96,1024]{1,0:T(8,128)(2,1)S(1)}, u32[]{:S(2)}, u32[]{:S(2)}) collective-permute-start(bf16[96,1024]{1,0:T(8,128)(2,1)} %get-tuple-element.29.rest_8_), channel_id=1, source_target_pairs={{0,4},{4,0},{8,12},{12,8},{16,20},{20,16},{24,28},{28,24},{1,5},{5... | collective-permute-start | bytes 589832 | tf_op jit(solution)/shard_map/ppermute | solution.py:408
  24.7 3.6 %copy-start = (bf16[96,1024]{1,0:T(8,128)(2,1)}, bf16[96,1024]{1,0:T(8,128)(2,1)S(1)}, u32[]{:S(2)}) copy-start(bf16[96,1024]{1,0:T(8,128)(2,1)S(1)} %collective-permute-done.12.rest_14_) | copy-start | bytes 589828
  24.7 3.5 %collective-permute-start.13 = (bf16[96,1024]{1,0:T(8,128)(2,1)S(1)}, bf16[96,1024]{1,0:T(8,128)(2,1)S(1)}, u32[]{:S(2)}, u32[]{:S(2)}) collective-permute-start(bf16[96,1024]{1,0:T(8,128)(2,1)S(1)} %collective-permute-done.12.rest_14_), channel_id=1, source_target_pairs={{0,4},{4,0},{8,12},{12,8},{16,20},{20,16},{24,28},{28,24},{1,5},{5... | collective-permute-start | bytes 589832 | tf_op jit(solution)/shard_map/ppermute | solution.py:408
  24.8 3.5 %copy-start.1 = (bf16[96,1024]{1,0:T(8,128)(2,1)}, bf16[96,1024]{1,0:T(8,128)(2,1)S(1)}, u32[]{:S(2)}) copy-start(bf16[96,1024]{1,0:T(8,128)(2,1)S(1)} %collective-permute-done.10.rest_12_) | copy-start | bytes 589828
  24.8 3.4 %collective-permute-start.11 = (bf16[96,1024]{1,0:T(8,128)(2,1)S(1)}, bf16[96,1024]{1,0:T(8,128)(2,1)S(1)}, u32[]{:S(2)}, u32[]{:S(2)}) collective-permute-start(bf16[96,1024]{1,0:T(8,128)(2,1)S(1)} %collective-permute-done.10.rest_12_), channel_id=1, source_target_pairs={{0,4},{4,0},{8,12},{12,8},{16,20},{20,16},{24,28},{28,24},{1,5},{5... | collective-permute-start | bytes 589832 | tf_op jit(solution)/shard_map/ppermute | solution.py:408
  25.2 3.1 %copy-start.2 = (bf16[96,1024]{1,0:T(8,128)(2,1)}, bf16[96,1024]{1,0:T(8,128)(2,1)S(1)}, u32[]{:S(2)}) copy-start(bf16[96,1024]{1,0:T(8,128)(2,1)S(1)} %collective-permute-done.8.rest_10_) | copy-start | bytes 589828
  25.2 3.0 %collective-permute-start.9 = (bf16[96,1024]{1,0:T(8,128)(2,1)S(1)}, bf16[96,1024]{1,0:T(8,128)(2,1)S(1)}, u32[]{:S(2)}, u32[]{:S(2)}) collective-permute-start(bf16[96,1024]{1,0:T(8,128)(2,1)S(1)} %collective-permute-done.8.rest_10_), channel_id=1, source_target_pairs={{0,4},{4,0},{8,12},{12,8},{16,20},{20,16},{24,28},{28,24},{1,5},{5... | collective-permute-start | bytes 589832 | tf_op jit(solution)/shard_map/ppermute | solution.py:408
  25.4 2.9 %copy-start.11 = (bf16[96,384]{1,0:T(8,128)(2,1)}, bf16[96,384]{1,0:T(8,128)(2,1)S(1)}, u32[]{:S(2)}) copy-start(bf16[96,384]{1,0:T(8,128)(2,1)S(1)} %collective-permute-done.2.rest_3_) | copy-start | bytes 221188
  25.4 1.5 %collective-permute-start.4 = (bf16[96,384]{1,0:T(8,128)(2,1)S(1)}, bf16[96,384]{1,0:T(8,128)(2,1)S(1)}, u32[]{:S(2)}, u32[]{:S(2)}) collective-permute-start(bf16[96,384]{1,0:T(8,128)(2,1)S(1)} %collective-permute-done.3.rest_4_), channel_id=1, source_target_pairs={{0,4},{4,0},{8,12},{12,8},{16,20},{20,16},{24,28},{28,24},{1,5},{5... | collective-permute-start | bytes 221192 | tf_op jit(solution)/shard_map/ppermute | solution.py:408
  26.9 1.4 %copy-start.13 = (bf16[96,384]{1,0:T(8,128)(2,1)}, bf16[96,384]{1,0:T(8,128)(2,1)S(1)}, u32[]{:S(2)}) copy-start(bf16[96,384]{1,0:T(8,128)(2,1)S(1)} %collective-permute-done.4.rest_5_) | copy-start | bytes 221188
  26.9 1.3 %collective-permute-start.6 = (bf16[96,384]{1,0:T(8,128)(2,1)S(1)}, bf16[96,384]{1,0:T(8,128)(2,1)S(1)}, u32[]{:S(2)}, u32[]{:S(2)}) collective-permute-start(bf16[96,384]{1,0:T(8,128)(2,1)S(1)} %collective-permute-done.5.rest_6_), channel_id=1, source_target_pairs={{0,4},{4,0},{8,12},{12,8},{16,20},{20,16},{24,28},{28,24},{1,5},{5... | collective-permute-start | bytes 221192 | tf_op jit(solution)/shard_map/ppermute | solution.py:408
  28.2 0.6 %copy-start.16 = (bf16[96,384]{1,0:T(8,128)(2,1)}, bf16[96,384]{1,0:T(8,128)(2,1)S(1)}, u32[]{:S(2)}) copy-start(bf16[96,384]{1,0:T(8,128)(2,1)S(1)} %collective-permute-done.6.rest_7_) | copy-start | bytes 221188
  28.2 0.7 %copy-start.3 = (bf16[96,1024]{1,0:T(8,128)(2,1)}, bf16[96,1024]{1,0:T(8,128)(2,1)S(1)}, u32[]{:S(2)}) copy-start(bf16[96,1024]{1,0:T(8,128)(2,1)S(1)} %collective-permute-done.7.rest_9_) | copy-start | bytes 589828
  28.2 0.8 %copy-start.4 = (bf16[96,1024]{1,0:T(8,128)(2,1)}, bf16[96,1024]{1,0:T(8,128)(2,1)S(1)}, u32[]{:S(2)}) copy-start(bf16[96,1024]{1,0:T(8,128)(2,1)S(1)} %collective-permute-done.13.rest_15_) | copy-start | bytes 589828
  28.2 0.8 %copy-start.5 = (bf16[96,1024]{1,0:T(8,128)(2,1)}, bf16[96,1024]{1,0:T(8,128)(2,1)S(1)}, u32[]{:S(2)}) copy-start(bf16[96,1024]{1,0:T(8,128)(2,1)S(1)} %collective-permute-done.11.rest_13_) | copy-start | bytes 589828
  29.0 0.7 %copy-start.6 = (bf16[96,1024]{1,0:T(8,128)(2,1)}, bf16[96,1024]{1,0:T(8,128)(2,1)S(1)}, u32[]{:S(2)}) copy-start(bf16[96,1024]{1,0:T(8,128)(2,1)S(1)} %collective-permute-done.9.rest_11_) | copy-start | bytes 589828
  37.1 6.0 %collective-permute-start.21 = (bf16[64,1024]{1,0:T(8,128)(2,1)}, bf16[64,1024]{1,0:T(8,128)(2,1)S(1)}, u32[]{:S(2)}, u32[]{:S(2)}) collective-permute-start(bf16[64,1024]{1,0:T(8,128)(2,1)} %get-tuple-element.45), channel_id=1, source_target_pairs={{0,1},{1,0},{2,3},{3,2},{4,5},{5,4},{6,7},{7,6},{8,9},{9,8},{10,11... | collective-permute-start | bytes 393224 | tf_op jit(solution)/shard_map/ppermute | solution.py:469
  38.7 8.0 %collective-permute-start.14 = (bf16[96,384]{1,0:T(8,128)(2,1)}, bf16[96,384]{1,0:T(8,128)(2,1)S(1)}, u32[]{:S(2)}, u32[]{:S(2)}) collective-permute-start(bf16[96,384]{1,0:T(8,128)(2,1)} %get-tuple-element.34), channel_id=1, source_target_pairs={{0,4},{4,0},{8,12},{12,8},{16,20},{20,16},{24,28},{28,24},{1,5},{5... | collective-permute-start | bytes 221192 | tf_op jit(solution)/shard_map/ppermute | solution.py:408
  38.8 7.9 %collective-permute-start.15 = (bf16[96,384]{1,0:T(8,128)(2,1)}, bf16[96,384]{1,0:T(8,128)(2,1)S(1)}, u32[]{:S(2)}, u32[]{:S(2)}) collective-permute-start(bf16[96,384]{1,0:T(8,128)(2,1)} %get-tuple-element.35), channel_id=1, source_target_pairs={{0,4},{4,0},{8,12},{12,8},{16,20},{20,16},{24,28},{28,24},{1,5},{5... | collective-permute-start | bytes 221192 | tf_op jit(solution)/shard_map/ppermute | solution.py:408
  39.2 7.5 %collective-permute-start.16 = (bf16[96,384]{1,0:T(8,128)(2,1)}, bf16[96,384]{1,0:T(8,128)(2,1)S(1)}, u32[]{:S(2)}, u32[]{:S(2)}) collective-permute-start(bf16[96,384]{1,0:T(8,128)(2,1)} %get-tuple-element.36), channel_id=1, source_target_pairs={{0,4},{4,0},{8,12},{12,8},{16,20},{20,16},{24,28},{28,24},{1,5},{5... | collective-permute-start | bytes 221192 | tf_op jit(solution)/shard_map/ppermute | solution.py:408
  39.3 7.5 %collective-permute-start.17 = (bf16[96,384]{1,0:T(8,128)(2,1)}, bf16[96,384]{1,0:T(8,128)(2,1)S(1)}, u32[]{:S(2)}, u32[]{:S(2)}) collective-permute-start(bf16[96,384]{1,0:T(8,128)(2,1)} %get-tuple-element.37), channel_id=1, source_target_pairs={{0,4},{4,0},{8,12},{12,8},{16,20},{20,16},{24,28},{28,24},{1,5},{5... | collective-permute-start | bytes 221192 | tf_op jit(solution)/shard_map/ppermute | solution.py:408
  44.1 15.6 %collective-permute-start.22 = (bf16[64,1024]{1,0:T(8,128)(2,1)S(1)}, bf16[64,1024]{1,0:T(8,128)(2,1)S(1)}, u32[]{:S(2)}, u32[]{:S(2)}) collective-permute-start(bf16[64,1024]{1,0:T(8,128)(2,1)S(1)} %add_convert_fusion), channel_id=1, source_target_pairs={{0,2},{1,3},{2,0},{3,1},{4,6},{5,7},{6,4},{7,5},{8,10},{9,11},{10,... | collective-permute-start | bytes 393224 | tf_op jit(solution)/shard_map/ppermute | solution.py:469
  46.7 0.6 %copy-start.12 = (bf16[96,384]{1,0:T(8,128)(2,1)}, bf16[96,384]{1,0:T(8,128)(2,1)S(1)}, u32[]{:S(2)}) copy-start(bf16[96,384]{1,0:T(8,128)(2,1)S(1)} %collective-permute-done.14.refs_4_) | copy-start | bytes 221188
  46.7 0.6 %copy-start.14 = (bf16[96,384]{1,0:T(8,128)(2,1)}, bf16[96,384]{1,0:T(8,128)(2,1)S(1)}, u32[]{:S(2)}) copy-start(bf16[96,384]{1,0:T(8,128)(2,1)S(1)} %collective-permute-done.15.refs_5_) | copy-start | bytes 221188
  46.7 0.7 %copy-start.15 = (bf16[96,384]{1,0:T(8,128)(2,1)}, bf16[96,384]{1,0:T(8,128)(2,1)S(1)}, u32[]{:S(2)}) copy-start(bf16[96,384]{1,0:T(8,128)(2,1)S(1)} %collective-permute-done.16.refs_6_) | copy-start | bytes 221188
  46.8 0.7 %copy-start.17 = (bf16[96,384]{1,0:T(8,128)(2,1)}, bf16[96,384]{1,0:T(8,128)(2,1)S(1)}, u32[]{:S(2)}) copy-start(bf16[96,384]{1,0:T(8,128)(2,1)S(1)} %collective-permute-done.17.refs_7_) | copy-start | bytes 221188
  49.3 4.7 %collective-permute-start.18 = (bf16[96,384]{1,0:T(8,128)(2,1)}, bf16[96,384]{1,0:T(8,128)(2,1)S(1)}, u32[]{:S(2)}, u32[]{:S(2)}) collective-permute-start(bf16[96,384]{1,0:T(8,128)(2,1)} %get-tuple-element.39), channel_id=1, source_target_pairs={{0,8},{4,12},{8,0},{12,4},{16,24},{20,28},{24,16},{28,20},{1,9},{5... | collective-permute-start | bytes 221192 | tf_op jit(solution)/shard_map/ppermute | solution.py:408
  50.8 4.6 %collective-permute-start.19 = (bf16[96,384]{1,0:T(8,128)(2,1)}, bf16[96,384]{1,0:T(8,128)(2,1)S(1)}, u32[]{:S(2)}, u32[]{:S(2)}) collective-permute-start(bf16[96,384]{1,0:T(8,128)(2,1)} %get-tuple-element.40), channel_id=1, source_target_pairs={{0,16},{4,20},{8,24},{12,28},{16,0},{20,4},{24,8},{28,12},{1,17},{... | collective-permute-start | bytes 221192 | tf_op jit(solution)/shard_map/ppermute | solution.py:408
  51.3 5.5 %collective-permute-start.20 = (bf16[96,384]{1,0:T(8,128)(2,1)}, bf16[96,384]{1,0:T(8,128)(2,1)S(1)}, u32[]{:S(2)}, u32[]{:S(2)}) collective-permute-start(bf16[96,384]{1,0:T(8,128)(2,1)} %get-tuple-element.41), channel_id=1, source_target_pairs={{0,24},{4,28},{8,16},{12,20},{16,8},{20,12},{24,0},{28,4},{1,25},{... | collective-permute-start | bytes 221192 | tf_op jit(solution)/shard_map/ppermute | solution.py:408
  54.0 2.8 %copy-start.18 = (bf16[96,384]{1,0:T(8,128)(2,1)}, bf16[96,384]{1,0:T(8,128)(2,1)S(1)}, u32[]{:S(2)}) copy-start(bf16[96,384]{1,0:T(8,128)(2,1)S(1)} %collective-permute-done.18.rest_1_) | copy-start | bytes 221188
  55.4 1.4 %copy-start.19 = (bf16[96,384]{1,0:T(8,128)(2,1)}, bf16[96,384]{1,0:T(8,128)(2,1)S(1)}, u32[]{:S(2)}) copy-start(bf16[96,384]{1,0:T(8,128)(2,1)S(1)} %collective-permute-done.19.rest_2_) | copy-start | bytes 221188
  56.8 0.6 %copy-start.20 = (bf16[96,384]{1,0:T(8,128)(2,1)}, bf16[96,384]{1,0:T(8,128)(2,1)S(1)}, u32[]{:S(2)}) copy-start(bf16[96,384]{1,0:T(8,128)(2,1)S(1)} %collective-permute-done.20.rest_3_) | copy-start | bytes 221188

commit v2 on v1

--- a/solution.py
+++ b/solution.py
@@ -1,9 +1,12 @@
+import functools
+
 import jax
 import jax.numpy as jnp
 from jax import lax
 from jax.experimental import pallas as pl
 from jax.experimental.pallas import tpu as pltpu
 from jax.sharding import PartitionSpec as P
+
 
 HEADS = 8
 HD = 64
@@ -219,11 +222,22 @@
 
 
 ROUTES = (0, 2, 4, 6)
+HALF = MAXV // 2
 
 
 def head_lanes(core):
     lane = lax.broadcasted_iota(jnp.int32, (1, 128), 1)
     return ((lane // HD) == core).astype(jnp.float32).astype(jnp.bfloat16)
+
+
+def scalar_copies(sources, targets, sems):
+    copies = [
+        pltpu.make_async_copy(source, target, sems.at[index])
+        for index, (source, target) in enumerate(zip(sources, targets))
+    ]
+    for copy in copies:
+        copy.start()
+    return copies
 
 
 def span_of(counts_ref, offsets_ref, owner):
@@ -239,8 +253,10 @@
     return early, late
 
 
-def pack_kernel(counts_ref, offsets_ref, q_ref, k_ref, v_ref, g_ref, *rest):
-    sends, cot_ref, narrow, wide, sems = rest[:4], rest[4], rest[5], rest[6], rest[7]
+def pack_kernel(counts_hbm, offsets_hbm, q_ref, k_ref, v_ref, g_ref, *rest):
+    sends, cot_refs = rest[:4], rest[4:7]
+    narrow, wide, counts_ref, offsets_ref, sems, scalar_sems = rest[7:]
+    scalars = scalar_copies((counts_hbm, offsets_hbm), (counts_ref, offsets_ref), scalar_sems)
     frames = q_ref.shape[1]
     last = frames - MAXV
     device = lax.axis_index("seq")
@@ -260,9 +276,11 @@
         )
     for copy in copies:
         copy.start()
+    for copy in scalars:
+        copy.wait()
     begin, end_start = span_of(counts_ref, offsets_ref, device)
     early, late = slot_masks(begin, end_start)
-    for copy in copies:
+    for copy in copies[:6]:
         copy.wait()
     for route, send in zip(ROUTES, sends):
         chip = (device ^ route) // 2
@@ -271,26 +289,28 @@
             send[:, index * 128 : (index + 1) * 128] = (
                 narrow[index, 0, :, lanes] * early + narrow[index, 1, :, lanes] * late
             )
-    cot_ref[...] = wide[0] * early + wide[1] * late
-
-
-def attend_kernel(counts_ref, offsets_ref, w_ref, *rest):
-    blocks, cots = rest[:8], rest[8:16]
-    outs, wg_ref = rest[16:24], rest[24]
-    packed, cot, dout, dq, sems = rest[25:]
+    for copy in copies[6:]:
+        copy.wait()
+    cot = wide[0] * early + wide[1] * late
+    cot_refs[0][...] = cot
+    cot_refs[1][...] = cot[:HALF]
+    cot_refs[2][...] = cot[HALF:]
+
+
+def forward_kernel(counts_hbm, offsets_hbm, *rest):
+    blocks = rest[:8]
+    packed, weights_ref, attended_ref, counts_ref, offsets_ref, sems, scalar_sems = rest[8:]
+    scalars = scalar_copies((counts_hbm, offsets_hbm), (counts_ref, offsets_ref), scalar_sems)
     device = lax.axis_index("seq")
     core = device % 2
     copies = []
     for index in range(8):
         rows = pl.ds(index * MAXV, MAXV)
         copies.append(pltpu.make_async_copy(blocks[index], packed.at[rows], sems.at[index]))
-        copies.append(pltpu.make_async_copy(cots[index], cot.at[rows], sems.at[8 + index]))
-    for copy in copies:
-        copy.start()
+        copies[-1].start()
     lanes = head_lanes(core)
-    top = (core == 0).astype(jnp.float32).astype(jnp.bfloat16)
-    bottom = (core == 1).astype(jnp.float32).astype(jnp.bfloat16)
-    w_both = jnp.concatenate([w_ref[...] * top, w_ref[...] * bottom], axis=0)
+    for copy in scalars:
+        copy.wait()
     dead = []
     for index in range(8):
         begin, end_start = span_of(counts_ref, offsets_ref, device ^ index)
@@ -300,40 +320,96 @@
     for copy in copies:
         copy.wait()
     factor = HD ** (-0.5)
-    dout[...] = lax.dot_general(
+    key = packed[:, 128:256] * lanes
+    value_t = packed[:, 256:384].T
+    for step in range(3):
+        rows = slice(step * 256, (step + 1) * 256)
+        scores = (
+            lax.dot_general(
+                key, packed[rows, 0:128], (((1,), (1,)), ((), ())), preferred_element_type=jnp.float32
+            )
+            * factor
+        )
+        scores = jnp.where(dead, -1e30, scores)
+        scores = jnp.exp(scores - jnp.max(scores, axis=0, keepdims=True))
+        weights = scores * (1.0 / jnp.sum(scores, axis=0, keepdims=True))
+        weights_ref[:, rows] = weights
+        attended_ref[:, rows] = jnp.dot(
+            value_t, weights.astype(jnp.bfloat16), preferred_element_type=jnp.float32
+        ).astype(jnp.bfloat16)
+
+
+def own_rows(ref, core, columns):
+    both = ref[:, columns].astype(jnp.float32)
+    return jnp.where(core == 0, both[:HD], both[HD:]).astype(jnp.bfloat16)
+
+
+def project(cot, w_ref, core):
+    top = (core == 0).astype(jnp.float32).astype(jnp.bfloat16)
+    bottom = (core == 1).astype(jnp.float32).astype(jnp.bfloat16)
+    w_both = jnp.concatenate([w_ref[...] * top, w_ref[...] * bottom], axis=0)
+    return lax.dot_general(
         cot[...], w_both, (((1,), (1,)), ((), ())), preferred_element_type=jnp.float32
     ).astype(jnp.bfloat16)
-    key = packed[:, 128:256] * lanes
+
+
+def early_kernel(attended_ref, w_ref, *rest):
+    cots, dout_ref, wg_ref, cot = rest[:6], rest[6], rest[7], rest[8]
+    core = lax.axis_index("seq") % 2
+    for index in range(6):
+        cot[index * MAXV : (index + 1) * MAXV, :] = cots[index][...]
+    dout_ref[...] = project(cot, w_ref, core)
+    wg_ref[...] = jnp.dot(
+        own_rows(attended_ref, core, slice(0, 6 * MAXV)),
+        cot[...],
+        preferred_element_type=jnp.float32,
+    )
+
+
+def late_kernel(attended_ref, w_ref, begun_ref, *rest):
+    cots, dout_ref, wg_ref, cot = rest[:2], rest[2], rest[3], rest[4]
+    core = lax.axis_index("seq") % 2
+    for index in range(2):
+        cot[index * MAXV : (index + 1) * MAXV, :] = cots[index][...]
+    dout_ref[...] = project(cot, w_ref, core)
+    wg_ref[...] = (
+        begun_ref[...]
+        + jnp.dot(
+            own_rows(attended_ref, core, slice(6 * MAXV, 8 * MAXV)),
+            cot[...],
+            preferred_element_type=jnp.float32,
+        )
+    ).astype(jnp.bfloat16)
+
+
+def backward_kernel(packed, weights_ref, attended_ref, begun_ref, ended_ref, *rest):
+    outs = rest[:8]
+    dout, dq = rest[8:]
+    core = lax.axis_index("seq") % 2
+    lanes = head_lanes(core)
+    dout[: 6 * MAXV, :] = begun_ref[...]
+    dout[6 * MAXV :, :] = ended_ref[...]
+    key_t = (packed[:, 128:256] * lanes).T
     value = packed[:, 256:384]
-    key_t = key.T
-    value_t = value.T
+    factor = HD ** (-0.5)
     dout_t = dout[...].astype(jnp.float32).T
     key_grad = jnp.zeros((8 * MAXV, 128), jnp.float32)
     value_grad = jnp.zeros((8 * MAXV, 128), jnp.float32)
-    attended = []
     for step in range(3):
         rows = slice(step * 256, (step + 1) * 256)
-        query = packed[rows, 0:128]
-        query_own = query * lanes
+        query_own = packed[rows, 0:128] * lanes
         dout_own = dout[rows, :]
-        scores = (
-            lax.dot_general(
-                key, query, (((1,), (1,)), ((), ())), preferred_element_type=jnp.float32
-            )
-            * factor
-        )
-        scores = jnp.where(dead, -1e30, scores)
-        scores = jnp.exp(scores - jnp.max(scores, axis=0, keepdims=True))
-        weights = scores * (1.0 / jnp.sum(scores, axis=0, keepdims=True))
-        low = weights.astype(jnp.bfloat16)
-        att = jnp.dot(value_t, low, preferred_element_type=jnp.float32).astype(jnp.bfloat16)
-        attended.append(att)
-        inner = jnp.sum(dout_t[:, rows] * att.astype(jnp.float32), axis=0, keepdims=True)
+        weights = weights_ref[:, rows]
+        inner = jnp.sum(
+            dout_t[:, rows] * attended_ref[:, rows].astype(jnp.float32), axis=0, keepdims=True
+        )
         dweights = lax.dot_general(
             value, dout_own, (((1,), (1,)), ((), ())), preferred_element_type=jnp.float32
         )
         dscores = (weights * (dweights - inner)).astype(jnp.bfloat16)
-        value_grad += jnp.dot(low, dout_own, preferred_element_type=jnp.float32)
+        value_grad += jnp.dot(
+            weights.astype(jnp.bfloat16), dout_own, preferred_element_type=jnp.float32
+        )
         key_grad += jnp.dot(dscores, query_own, preferred_element_type=jnp.float32)
         dq_t = jnp.dot(key_t, dscores, preferred_element_type=jnp.float32) * factor
         dq[rows, :] = dq_t.T.astype(jnp.bfloat16)
@@ -344,11 +420,6 @@
         outs[index][:, 0:128] = dq[rows, :]
         outs[index][:, 128:256] = key_grad[rows]
         outs[index][:, 256:384] = value_grad[rows]
-    att = jnp.concatenate(attended, axis=1)
-    att = jnp.where(core == 0, att[:HD].astype(jnp.float32), att[HD:].astype(jnp.float32))
-    wg_ref[...] = jnp.dot(
-        att.astype(jnp.bfloat16), cot[...], preferred_element_type=jnp.float32
-    ).astype(jnp.bfloat16)
 
 
 def combine_kernel(*refs):
@@ -356,9 +427,11 @@
         refs[8 + index][...] = refs[index][...] + refs[4 + index][...]
 
 
-def unpack_kernel(counts_ref, offsets_ref, *rest):
-    blocks, outs = rest[:4], rest[4:7]
-    edges, blank, sems = rest[7:]
+def unpack_kernel(scale, counts_hbm, offsets_hbm, *rest):
+    blocks, shares = rest[:4], rest[4:-10]
+    outs, wg_ref = rest[-10:-7], rest[-7]
+    edges, blank, counts_ref, offsets_ref, sems, scalar_sems = rest[-6:]
+    scalars = scalar_copies((counts_hbm, offsets_hbm), (counts_ref, offsets_ref), scalar_sems)
     device = lax.axis_index("seq")
     frames = outs[0].shape[1]
     last = frames - MAXV
@@ -371,6 +444,8 @@
             )
         )
         copies[-1].start()
+    for copy in scalars:
+        copy.wait()
     begin, end_start = span_of(counts_ref, offsets_ref, device)
     sides = slot_masks(begin, end_start)
     for route, block in zip(ROUTES, blocks):
@@ -390,13 +465,22 @@
                 )
             )
             copies[-1].start()
+    terms = [share[...].astype(jnp.float32) for share in shares]
+    while len(terms) > 1:
+        terms = [left + right for left, right in zip(terms[::2], terms[1::2])]
+    wg_ref[...] = terms[0] * scale
     for copy in copies:
         copy.wait()
 
 
+PARAMS = pltpu.CompilerParams(vmem_limit_bytes=24 << 20)
 ANYWHERE = pl.BlockSpec(memory_space=pl.ANY)
 SCALARS = pl.BlockSpec(memory_space=pltpu.SMEM)
 LOCAL = pl.BlockSpec(memory_space=pltpu.VMEM)
+
+
+def in_hbm(block):
+    return pltpu.with_memory_space_constraint(block, pltpu.HBM)
 
 
 def by_heads(queries, keys, values, out_cotangent, visible_counts, span_offset, out_weight):
@@ -409,69 +493,107 @@
 
     narrow = jax.ShapeDtypeStruct((MAXV, 384), bf16)
     wide = jax.ShapeDtypeStruct((MAXV, out_cotangent.shape[2]), bf16)
-    *sends, cot = pl.pallas_call(
+
+    def seen(kernel, outs, specs, operands, scratch=(), out_specs=None):
+        return pl.pallas_call(
+            kernel,
+            out_shape=outs,
+            in_specs=specs,
+            out_specs=out_specs or [LOCAL] * len(outs),
+            scratch_shapes=scratch,
+            compiler_params=PARAMS,
+        )(*operands)
+
+    width = out_cotangent.shape[2]
+    rows = 8 * MAXV
+    counts, offsets = in_hbm(visible_counts), in_hbm(span_offset)
+    table = pltpu.SMEM(visible_counts.shape, jnp.int32)
+    tables = [table, table]
+    pair_sems = pltpu.SemaphoreType.DMA((2,))
+    half = jax.ShapeDtypeStruct((HALF, width), bf16)
+    *sends, cot, cot_a, cot_b = seen(
         pack_kernel,
-        out_shape=[narrow] * 4 + [wide],
-        in_specs=[SCALARS] * 2 + [ANYWHERE] * 4,
-        out_specs=[LOCAL] * 5,
-        scratch_shapes=[
+        [narrow] * 4 + [wide, half, half],
+        [ANYWHERE] * 6,
+        (counts, offsets, *map(in_hbm, (queries, keys, values, out_cotangent))),
+        [
             pltpu.VMEM((3, 2, MAXV, queries.shape[2]), bf16),
-            pltpu.VMEM((2, MAXV, out_cotangent.shape[2]), bf16),
+            pltpu.VMEM((2, MAXV, width), bf16),
+            *tables,
             pltpu.SemaphoreType.DMA((8,)),
+            pair_sems,
         ],
-        name="pack",
-    )(visible_counts, span_offset, queries, keys, values, out_cotangent)
+    )
     even = [sends[0]] + [shift(sends[i], ROUTES[i]) for i in (1, 2, 3)]
-    even_cot = [cot] + [shift(cot, ROUTES[i]) for i in (1, 2, 3)]
+    x_a, y_b = shift(cot_a, 2), shift(cot_b, 4)
+    x_b, y_a = shift(cot_b, 2), shift(cot_a, 4)
+    d_a, d_b = shift(x_a, 4), shift(y_b, 2)
+    even_cot = [cot] + [
+        jnp.concatenate(pair, axis=0) for pair in ((x_a, x_b), (y_a, y_b), (d_a, d_b))
+    ]
     odd = [shift(block, 1) for block in even]
     odd_cot = [shift(block, 1) for block in even_cot]
     blocks = [block for pair in zip(even, odd) for block in pair]
     cots = [block for pair in zip(even_cot, odd_cot) for block in pair]
-    *grads, partial = pl.pallas_call(
-        attend_kernel,
-        out_shape=[narrow] * 8 + [jax.ShapeDtypeStruct(out_weight.shape, bf16)],
-        in_specs=[SCALARS] * 2 + [LOCAL] + [ANYWHERE] * 16,
-        out_specs=[LOCAL] * 9,
-        scratch_shapes=[
-            pltpu.VMEM((8 * MAXV, 384), bf16),
-            pltpu.VMEM((8 * MAXV, out_cotangent.shape[2]), bf16),
-            pltpu.VMEM((8 * MAXV, 128), bf16),
-            pltpu.VMEM((8 * MAXV, 128), bf16),
-            pltpu.SemaphoreType.DMA((16,)),
+    packed, weights, attended = seen(
+        forward_kernel,
+        [
+            pltpu.VMEM((rows, 384), bf16),
+            pltpu.VMEM((rows, rows), jnp.float32),
+            pltpu.VMEM((128, rows), bf16),
         ],
-        name="attend",
-    )(visible_counts, span_offset, out_weight, *blocks, *cots)
+        [ANYWHERE] * 2 + [LOCAL] * 8,
+        (counts, offsets, *blocks),
+        [*tables, pltpu.SemaphoreType.DMA((8,)), pair_sems],
+    )
+    begun, begun_wg = seen(
+        early_kernel,
+        [pltpu.VMEM((6 * MAXV, 128), bf16), pltpu.VMEM(out_weight.shape, jnp.float32)],
+        [LOCAL] * 8,
+        (attended, out_weight, *cots[:6]),
+        [pltpu.VMEM((6 * MAXV, width), bf16)],
+    )
+    ended, partial = seen(
+        late_kernel,
+        [pltpu.VMEM((2 * MAXV, 128), bf16), jax.ShapeDtypeStruct(out_weight.shape, bf16)],
+        [LOCAL] * 5,
+        (attended, out_weight, begun_wg, *cots[6:]),
+        [pltpu.VMEM((2 * MAXV, width), bf16)],
+    )
+    shares = [partial]
+    for step in range(1, clips):
+        shares.append(lax.ppermute(partial, "clip", [(i, i ^ step) for i in range(clips)]))
+    grads = seen(
+        backward_kernel,
+        [narrow] * 8,
+        [LOCAL] * 5,
+        (packed, weights, attended, begun, ended),
+        [pltpu.VMEM((rows, 128), bf16)] * 2,
+    )
     crossed = [shift(grads[i + 1], 1) for i in ROUTES]
-    joined = pl.pallas_call(
-        combine_kernel,
-        out_shape=[narrow] * 4,
-        in_specs=[LOCAL] * 8,
-        out_specs=[LOCAL] * 4,
-        name="combine",
-    )(*[grads[i] for i in ROUTES], *crossed)
+    joined = seen(
+        combine_kernel, [narrow] * 4, [LOCAL] * 8, (*[grads[i] for i in ROUTES], *crossed)
+    )
     home = [joined[0]] + [shift(joined[i], ROUTES[i]) for i in (1, 2, 3)]
-    full = jax.ShapeDtypeStruct(queries.shape, bf16)
     frames = queries.shape[1]
-    outs = pl.pallas_call(
-        unpack_kernel,
-        out_shape=[full] * 3,
-        in_specs=[SCALARS] * 2 + [LOCAL] * 4,
-        out_specs=[ANYWHERE] * 3,
-        scratch_shapes=[
-            pltpu.VMEM((3, 2, MAXV, queries.shape[2]), bf16),
-            pltpu.VMEM((frames - 2 * MAXV, queries.shape[2]), bf16),
-            pltpu.SemaphoreType.DMA((9,)),
-        ],
-        name="unpack",
-    )(visible_counts, span_offset, *home)
-    step = 1
-    while step < clips:
-        other = lax.ppermute(partial, "clip", [(i, i ^ step) for i in range(clips)])
-        total = partial.astype(jnp.float32) + other.astype(jnp.float32)
-        partial = total.astype(bf16)
-        step *= 2
-    weight_grad = total * (clips * VIS_DEV * pairs) ** (-0.5)
-    return (*outs, weight_grad)
+    scale = (clips * VIS_DEV * pairs) ** (-0.5)
+    return tuple(
+        seen(
+            functools.partial(unpack_kernel, scale),
+            [jax.ShapeDtypeStruct(queries.shape, bf16)] * 3
+            + [jax.ShapeDtypeStruct(out_weight.shape, jnp.float32)],
+            [ANYWHERE] * 2 + [LOCAL] * (4 + len(shares)),
+            (counts, offsets, *home, *shares),
+            [
+                pltpu.VMEM((3, 2, MAXV, queries.shape[2]), bf16),
+                pltpu.VMEM((frames - 2 * MAXV, queries.shape[2]), bf16),
+                *tables,
+                pltpu.SemaphoreType.DMA((9,)),
+                pair_sems,
+            ],
+            [ANYWHERE] * 3 + [LOCAL],
+        )
+    )
 
 
 def local(*arrays):

time: 60.7 us -> 50.3 us (0.83)
  Pallas kernels: 14.3 us -> 9.56 us
  waiting for transfers between devices: 20.8 us -> 17.2 us
  local copies, waits for them, and re-layouts: 2.68 us -> 0.05 us
  starting transfers between devices: 20 us -> 22.5 us
  other arithmetic: 1.68 us -> 0 us
    ppermute x21 -> x24, waiting for transfers between devices: 17.4 us -> 10.6 us  [shift(): return lax.ppermute(block, 'seq', [(i, i ^ step) for i in range(pairs)])]
    pallas_call x4 -> x7, Pallas kernels: 14.3 us -> 9.56 us  [seen(): pl.pallas_call(kernel, out_shape=outs, in_specs=specs, out_specs=out_spec...]
    ppermute x2 -> x3, waiting for transfers between devices: 3.37 us -> 6.59 us  [by_heads(): lax.ppermute(partial, 'clip', [(i, i ^ step) for i in range(clips)])]
    unnamed x42 -> x5, local copies, waits for them, and re-layouts: 2.68 us -> 0.03 us
    ppermute x21 -> x24, starting transfers between devices: 15.7 us -> 18.1 us  [shift(): return lax.ppermute(block, 'seq', [(i, i ^ step) for i in range(pairs)])]
    convert_element_type x1 -> x0, other arithmetic: 0.94 us -> none  [by_heads(): partial = total.astype(bf16)]
    mul x1 -> x0, other arithmetic: 0.74 us -> none  [by_heads(): weight_grad = total * (clips * VIS_DEV * pairs) ** (-0.5)]
    ppermute x2 -> x3, starting transfers between devices: 4.29 us -> 4.39 us  [by_heads(): lax.ppermute(partial, 'clip', [(i, i ^ step) for i in range(clips)])]
  transfers between devices with their start and end apart: 23 -> 27, of which waited for: 9 -> 8; matrix products, arithmetic and copies ran while one was open for 2% -> 0% of each run, Pallas kernels for 7% -> 8%
where the time goes in v2:
time: 50.3 us; the launch traced here: 50.1 us
  starting transfers between devices  22.5 us (45%)
  waiting for transfers between devices  17.2 us (34%)
  Pallas kernels  9.56 us (19%)
  between operations  0.79 us (2%)
    ppermute x24, starting transfers between devices, shift(): return lax.ppermute(block, 'seq', [(i, i ^ step) for i in range(pairs)])  18.1 us
    ppermute x24, waiting for transfers between devices, shift(): return lax.ppermute(block, 'seq', [(i, i ^ step) for i in range(pairs)])  10.6 us
    pallas_call x7, Pallas kernels, seen(): pl.pallas_call(kernel, out_shape=outs, in_specs=specs, out_specs=out_spec...  9.56 us
    ppermute x3, waiting for transfers between devices, by_heads(): lax.ppermute(partial, 'clip', [(i, i ^ step) for i in range(clips)])  6.59 us
    ppermute x3, starting transfers between devices, by_heads(): lax.ppermute(partial, 'clip', [(i, i ^ step) for i in range(clips)])  4.39 us
  transfers between devices with their start and end apart: 27, of which 8 were waited for; matrix products, arithmetic and copies ran while one was open for 0% of the time, Pallas kernels for 8%

profile of v2, /device:TPU:0, one launch (start us, length us, event | category | flops | bytes accessed | tf_op | source)
XLA Modules:
  0.0 50.1 jit_solution(10350184307584242082)
XLA Ops:
  0.6 0.0 copy-start
  0.6 1.4 %shard_map.102 = (bf16[96,384]{1,0:T(8,128)(2,1)S(1)}, bf16[96,384]{1,0:T(8,128)(2,1)S(1)}, bf16[96,384]{1,0:T(8,128)(2,1)S(1)}, bf16[96,384]{1,0:T(8,128)(2,1)S...) custom-call(s32[1,8]{1,0:T(1,128)} %counts_hbm.5, ...), custom_call_target="tpu_custom_call" | custom-call | tf_op jit(solution)/shard_map/pallas_call | solution.py:498
  2.1 3.0 %collective-permute-start.8 = (bf16[48,1024]{1,0:T(8,128)(2,1)S(1)}, bf16[48,1024]{1,0:T(8,128)(2,1)S(1)}, u32[]{:S(2)}, u32[]{:S(2)}) collective-permute-start(bf16[48,1024]{1,0:T(8,128)(2,1)S(1)} %get-tuple-element.38), channel_id=1, source_target_pairs={{0,8},{4,12},{8,0},{12,4},{16,24},{20,28},{24,16},{28,20},{1,9},{5... | collective-permute-start | bytes 294920 | tf_op jit(solution)/shard_map/ppermute | solution.py:492
  5.1 1.5 %collective-permute-start.11 = (bf16[48,1024]{1,0:T(8,128)(2,1)S(1)}, bf16[48,1024]{1,0:T(8,128)(2,1)S(1)}, u32[]{:S(2)}, u32[]{:S(2)}) collective-permute-start(bf16[48,1024]{1,0:T(8,128)(2,1)S(1)} %get-tuple-element.38), channel_id=1, source_target_pairs={{0,16},{4,20},{8,24},{12,28},{16,0},{20,4},{24,8},{28,12},{1,17},{... | collective-permute-start | bytes 294920 | tf_op jit(solution)/shard_map/ppermute | solution.py:492
  6.6 0.5 %collective-permute-start.9 = (bf16[48,1024]{1,0:T(8,128)(2,1)S(1)}, bf16[48,1024]{1,0:T(8,128)(2,1)S(1)}, u32[]{:S(2)}, u32[]{:S(2)}) collective-permute-start(bf16[48,1024]{1,0:T(8,128)(2,1)S(1)} %get-tuple-element.39), channel_id=1, source_target_pairs={{0,8},{4,12},{8,0},{12,4},{16,24},{20,28},{24,16},{28,20},{1,9},{5... | collective-permute-start | bytes 294920 | tf_op jit(solution)/shard_map/ppermute | solution.py:492
  7.2 0.1 collective-permute-start.12
  7.2 0.0 collective-permute-start
  7.2 0.7 %collective-permute-done.8 = bf16[48,1024]{1,0:T(8,128)(2,1)S(1)} collective-permute-done((bf16[48,1024]{1,0:T(8,128)(2,1)S(1)}, bf16[48,1024]{1,0:T(8,128)(2,1)S(1)}, u32[]{:S(2)}, u32[]{:S(2)}) %collective-permute-start.8) | collective-permute-done | bytes 98336 | tf_op jit(solution)/shard_map/ppermute | solution.py:492
  7.9 2.5 %collective-permute-start.1 = (bf16[96,384]{1,0:T(8,128)(2,1)S(1)}, bf16[96,384]{1,0:T(8,128)(2,1)S(1)}, u32[]{:S(2)}, u32[]{:S(2)}) collective-permute-start(bf16[96,384]{1,0:T(8,128)(2,1)S(1)} %get-tuple-element.31), channel_id=1, source_target_pairs={{0,8},{4,12},{8,0},{12,4},{16,24},{20,28},{24,16},{28,20},{1,9},{5... | collective-permute-start | bytes 221192 | tf_op jit(solution)/shard_map/ppermute | solution.py:492
  10.4 0.3 collective-permute-done.11
  10.7 1.6 %collective-permute-start.3 = (bf16[96,384]{1,0:T(8,128)(2,1)S(1)}, bf16[96,384]{1,0:T(8,128)(2,1)S(1)}, u32[]{:S(2)}, u32[]{:S(2)}) collective-permute-start(bf16[96,384]{1,0:T(8,128)(2,1)S(1)} %get-tuple-element.32), channel_id=1, source_target_pairs={{0,16},{4,20},{8,24},{12,28},{16,0},{20,4},{24,8},{28,12},{1,17},{... | collective-permute-start | bytes 221192 | tf_op jit(solution)/shard_map/ppermute | solution.py:492
  12.3 0.0 collective-permute-done.9
  12.3 0.4 collective-permute-start.5
  12.7 0.0 collective-permute-done.12
  12.7 1.7 %collective-permute-start.14 = (bf16[48,1024]{1,0:T(8,128)(2,1)S(1)}, bf16[48,1024]{1,0:T(8,128)(2,1)S(1)}, u32[]{:S(2)}, u32[]{:S(2)}) collective-permute-start(bf16[48,1024]{1,0:T(8,128)(2,1)S(1)} %collective-permute-done.8), channel_id=1, source_target_pairs={{0,16},{4,20},{8,24},{12,28},{16,0},{20,4},{24,8},{28,12},{1,17},{... | collective-permute-start | bytes 294920 | tf_op jit(solution)/shard_map/ppermute | solution.py:492
  14.4 4.1 %collective-permute-done.14 = bf16[48,1024]{1,0:T(8,128)(2,1)S(1)} collective-permute-done((bf16[48,1024]{1,0:T(8,128)(2,1)S(1)}, bf16[48,1024]{1,0:T(8,128)(2,1)S(1)}, u32[]{:S(2)}, u32[]{:S(2)}) %collective-permute-start.14) | collective-permute-done | bytes 98336 | tf_op jit(solution)/shard_map/ppermute | solution.py:492
  18.6 0.6 %collective-permute-start.15 = (bf16[48,1024]{1,0:T(8,128)(2,1)S(1)}, bf16[48,1024]{1,0:T(8,128)(2,1)S(1)}, u32[]{:S(2)}, u32[]{:S(2)}) collective-permute-start(bf16[48,1024]{1,0:T(8,128)(2,1)S(1)} %collective-permute-done.12), channel_id=1, source_target_pairs={{0,8},{4,12},{8,0},{12,4},{16,24},{20,28},{24,16},{28,20},{1,9},{5... | collective-permute-start | bytes 294920 | tf_op jit(solution)/shard_map/ppermute | solution.py:492
  19.2 0.0 collective-permute-done.rest_1_
  19.2 0.1 collective-permute-start.7
  19.3 0.0 collective-permute-done.1.rest_2_
  19.3 0.5 collective-permute-start.2
  19.8 0.0 collective-permute-done.3.rest_4_
  19.8 0.1 collective-permute-start.10
  19.9 3.3 %collective-permute-done.15 = bf16[48,1024]{1,0:T(8,128)(2,1)S(1)} collective-permute-done((bf16[48,1024]{1,0:T(8,128)(2,1)S(1)}, bf16[48,1024]{1,0:T(8,128)(2,1)S(1)}, u32[]{:S(2)}, u32[]{:S(2)}) %collective-permute-start.15) | collective-permute-done | bytes 98336 | tf_op jit(solution)/shard_map/ppermute | solution.py:492
  23.2 0.0 collective-permute-start.13
  23.2 0.0 collective-permute-done.5.rest_6_
  23.2 0.6 %collective-permute-start.16 = (bf16[96,1024]{1,0:T(8,128)(2,1)S(1)}, bf16[96,1024]{1,0:T(8,128)(2,1)S(1)}, u32[]{:S(2)}, u32[]{:S(2)}) collective-permute-start(bf16[96,1024]{1,0:T(8,128)(2,1)S(1)} %constant_dynamic-update-slice_fusion.4.rest_0_), channel_id=1, source_target_pairs={{0,4},{4,0},{8,12},{12,8},{16,20},{20,16},{24,28},{28,24},{1,5},{5... | collective-permute-start | bytes 589832 | tf_op jit(solution)/shard_map/ppermute | solution.py:492
  23.8 0.0 collective-permute-done.2.rest_3_
  23.8 0.1 collective-permute-start.4
  23.8 1.2 %collective-permute-done.4.rest_5_ = bf16[96,384]{1,0:T(8,128)(2,1)S(1)} collective-permute-done((bf16[96,384]{1,0:T(8,128)(2,1)S(1)}, bf16[96,384]{1,0:T(8,128)(2,1)S(1)}, u32[]{:S(2)}, u32[]{:S(2)}) %collective-permute-start.4) | collective-permute-done | bytes 73760 | tf_op jit(solution)/shard_map/ppermute | solution.py:492
  25.0 0.3 collective-permute-start.6
  25.3 1.0 %collective-permute-done.6.rest_7_ = bf16[96,384]{1,0:T(8,128)(2,1)S(1)} collective-permute-done((bf16[96,384]{1,0:T(8,128)(2,1)S(1)}, bf16[96,384]{1,0:T(8,128)(2,1)S(1)}, u32[]{:S(2)}, u32[]{:S(2)}) %collective-permute-start.6) | collective-permute-done | bytes 73760 | tf_op jit(solution)/shard_map/ppermute | solution.py:492
  26.3 3.1 %shard_map.103 = (bf16[768,384]{1,0:T(8,128)(2,1)S(1)}, f32[768,768]{1,0:T(8,128)S(1)}, bf16[128,768]{1,0:T(8,128)(2,1)S(1)}) custom-call(s32[1,8]{1,0:T(1,128)} %counts_hbm.5, s32[1,8]{1,0:T(1,128)} %offsets_hbm.5, bf16[96,384]{1,0:T(8,128)(2,1)S(1)} %get-tuple-element.30.rest_0_, bf16[96,384]{1,0:T(8,128)(2,1)S(1)} %collective-permute-done.rest_1_, ...), custom_call_target="tpu_custom_call" | custom-call | tf_op jit(solution)/shard_map/pallas_call | solution.py:498
  29.4 0.0 collective-permute-done.7.rest_1_
  29.4 0.0 collective-permute-done.10.rest_3_
  29.4 0.0 collective-permute-done.13.rest_5_
  29.4 0.0 copy-done
  29.4 0.7 %shard_map.104 = (bf16[576,128]{1,0:T(8,128)(2,1)S(1)}, f32[64,1024]{1,0:T(8,128)S(1)}) custom-call(bf16[128,768]{1,0:T(8,128)(2,1)S(1)} %get-tuple-element.36.attended_ref, bf16[64,1024]{1,0:T(8,128)(2,1)S(1)} %copy-done, bf16[96,1024]{1,0:T(8,128)(2,1)S(1)} %get-tuple-element.37.rest_0_, bf16[96,1024]{1,0:T(8,128)(2,1)S(1)} %collective-permute-done.7.rest_1_, ...), custom_call_target="tpu_custom_call" | custom-call | tf_op jit(solution)/shard_map/pallas_call | solution.py:498
  30.1 0.0 collective-permute-done.16.rest_1_
  30.1 0.3 shard_map.105
  30.5 1.5 %shard_map.106 = (bf16[96,384]{1,0:T(8,128)(2,1)S(1)}, bf16[96,384]{1,0:T(8,128)(2,1)S(1)}, bf16[96,384]{1,0:T(8,128)(2,1)S(1)}, bf16[96,384]{1,0:T(8,128)(2,1)S...) custom-call(bf16[768,384]{1,0:T(8,128)(2,1)S(1)} %get-tuple-element., ...), custom_call_target="tpu_custom_call" | custom-call | tf_op jit(solution)/shard_map/pallas_call | solution.py:498
  32.0 0.4 collective-permute-start.17
  32.4 0.2 collective-permute-start.18
  32.6 1.6 %collective-permute-start.24 = (bf16[64,1024]{1,0:T(8,128)(2,1)S(1)}, bf16[64,1024]{1,0:T(8,128)(2,1)S(1)}, u32[]{:S(2)}, u32[]{:S(2)}) collective-permute-start(bf16[64,1024]{1,0:T(8,128)(2,1)S(1)} %get-tuple-element.55.rest_4_), channel_id=1, source_target_pairs={{0,1},{1,0},{2,3},{3,2},{4,5},{5,4},{6,7},{7,6},{8,9},{9,8},{10,11... | collective-permute-start | bytes 393224 | tf_op jit(solution)/shard_map/ppermute | solution.py:565
  34.2 0.0 collective-permute-start.19
  34.2 0.5 %collective-permute-start.20 = (bf16[96,384]{1,0:T(8,128)(2,1)S(1)}, bf16[96,384]{1,0:T(8,128)(2,1)S(1)}, u32[]{:S(2)}, u32[]{:S(2)}) collective-permute-start(bf16[96,384]{1,0:T(8,128)(2,1)S(1)} %get-tuple-element.50), channel_id=1, source_target_pairs={{0,4},{4,0},{8,12},{12,8},{16,20},{20,16},{24,28},{28,24},{1,5},{5... | collective-permute-start | bytes 221192 | tf_op jit(solution)/shard_map/ppermute | solution.py:492
  34.7 0.0 collective-permute-done.17.refs_4_
  34.7 2.6 %collective-permute-start.25 = (bf16[64,1024]{1,0:T(8,128)(2,1)S(1)}, bf16[64,1024]{1,0:T(8,128)(2,1)S(1)}, u32[]{:S(2)}, u32[]{:S(2)}) collective-permute-start(bf16[64,1024]{1,0:T(8,128)(2,1)S(1)} %get-tuple-element.55.rest_4_), channel_id=1, source_target_pairs={{0,2},{1,3},{2,0},{3,1},{4,6},{5,7},{6,4},{7,5},{8,10},{9,11},{10,... | collective-permute-start | bytes 393224 | tf_op jit(solution)/shard_map/ppermute | solution.py:565
  37.3 0.0 collective-permute-done.18.refs_5_
  37.3 0.2 collective-permute-start.26
  37.5 0.0 collective-permute-done.19.refs_6_
  37.5 0.0 collective-permute-done.20.refs_7_
  37.6 0.7 %collective-permute-start.21 = (bf16[96,384]{1,0:T(8,128)(2,1)S(1)}, bf16[96,384]{1,0:T(8,128)(2,1)S(1)}, u32[]{:S(2)}, u32[]{:S(2)}) collective-permute-start(bf16[96,384]{1,0:T(8,128)(2,1)S(1)} %get-tuple-element.52), channel_id=1, source_target_pairs={{0,8},{4,12},{8,0},{12,4},{16,24},{20,28},{24,16},{28,20},{1,9},{5... | collective-permute-start | bytes 221192 | tf_op jit(solution)/shard_map/ppermute | solution.py:492
  38.3 1.4 %collective-permute-start.22 = (bf16[96,384]{1,0:T(8,128)(2,1)S(1)}, bf16[96,384]{1,0:T(8,128)(2,1)S(1)}, u32[]{:S(2)}, u32[]{:S(2)}) collective-permute-start(bf16[96,384]{1,0:T(8,128)(2,1)S(1)} %get-tuple-element.53), channel_id=1, source_target_pairs={{0,16},{4,20},{8,24},{12,28},{16,0},{20,4},{24,8},{28,12},{1,17},{... | collective-permute-start | bytes 221192 | tf_op jit(solution)/shard_map/ppermute | solution.py:492
  39.7 0.1 collective-permute-done.24.rest_5_
  39.7 1.4 %collective-permute-start.23 = (bf16[96,384]{1,0:T(8,128)(2,1)S(1)}, bf16[96,384]{1,0:T(8,128)(2,1)S(1)}, u32[]{:S(2)}, u32[]{:S(2)}) collective-permute-start(bf16[96,384]{1,0:T(8,128)(2,1)S(1)} %get-tuple-element.54), channel_id=1, source_target_pairs={{0,24},{4,28},{8,16},{12,20},{16,8},{20,12},{24,0},{28,4},{1,25},{... | collective-permute-start | bytes 221192 | tf_op jit(solution)/shard_map/ppermute | solution.py:492
  41.1 6.5 %collective-permute-done.25.rest_6_ = bf16[64,1024]{1,0:T(8,128)(2,1)S(1)} collective-permute-done((bf16[64,1024]{1,0:T(8,128)(2,1)S(1)}, bf16[64,1024]{1,0:T(8,128)(2,1)S(1)}, u32[]{:S(2)}, u32[]{:S(2)}) %collective-permute-start.25) | collective-permute-done | bytes 131104 | tf_op jit(solution)/shard_map/ppermute | solution.py:565
  47.6 0.0 collective-permute-done.26.rest_7_
  47.6 0.0 collective-permute-done.21.rest_1_
  47.6 0.0 collective-permute-done.22.rest_2_
  47.7 0.0 collective-permute-done.23.rest_3_
  47.7 2.4 %shard_map.108 = (bf16[1,512,512]{2,1,0:T(8,128)(2,1)}, bf16[1,512,512]{2,1,0:T(8,128)(2,1)}, bf16[1,512,512]{2,1,0:T(8,128)(2,1)}, f32[64,1024]{1,0:T(8,128)}) custom-call(s32[1,8]{1,0:T(1,128)} %counts_hbm.5, s32[1,8]{1,0:T(1,128)} %offsets_hbm.5, bf16[96,384]{1,0:T(8,128)(2,1)S(1)} %get-tuple-element.51.rest_0_, ...), custom_call_target="tpu_custom_call" | custom-call | tf_op jit(solution)/shard_map/pallas_call | solution.py:498
  (7 shorter events, 0.1 us)
Async XLA Ops:
  0.6 28.8 %copy-start = (bf16[64,1024]{1,0:T(8,128)(2,1)S(1)}, bf16[64,1024]{1,0:T(8,128)(2,1)}, u32[]{:S(2)}) copy-start(bf16[64,1024]{1,0:T(8,128)(2,1)} %w_ref.3) | copy-start | bytes 393220
  2.1 5.9 %collective-permute-start.8 = (bf16[48,1024]{1,0:T(8,128)(2,1)S(1)}, bf16[48,1024]{1,0:T(8,128)(2,1)S(1)}, u32[]{:S(2)}, u32[]{:S(2)}) collective-permute-start(bf16[48,1024]{1,0:T(8,128)(2,1)S(1)} %get-tuple-element.38), channel_id=1, source_target_pairs={{0,8},{4,12},{8,0},{12,4},{16,24},{20,28},{24,16},{28,20},{1,9},{5... | collective-permute-start | bytes 294920 | tf_op jit(solution)/shard_map/ppermute | solution.py:492
  5.1 5.6 %collective-permute-start.11 = (bf16[48,1024]{1,0:T(8,128)(2,1)S(1)}, bf16[48,1024]{1,0:T(8,128)(2,1)S(1)}, u32[]{:S(2)}, u32[]{:S(2)}) collective-permute-start(bf16[48,1024]{1,0:T(8,128)(2,1)S(1)} %get-tuple-element.38), channel_id=1, source_target_pairs={{0,16},{4,20},{8,24},{12,28},{16,0},{20,4},{24,8},{28,12},{1,17},{... | collective-permute-start | bytes 294920 | tf_op jit(solution)/shard_map/ppermute | solution.py:492
  6.6 5.7 %collective-permute-start.9 = (bf16[48,1024]{1,0:T(8,128)(2,1)S(1)}, bf16[48,1024]{1,0:T(8,128)(2,1)S(1)}, u32[]{:S(2)}, u32[]{:S(2)}) collective-permute-start(bf16[48,1024]{1,0:T(8,128)(2,1)S(1)} %get-tuple-element.39), channel_id=1, source_target_pairs={{0,8},{4,12},{8,0},{12,4},{16,24},{20,28},{24,16},{28,20},{1,9},{5... | collective-permute-start | bytes 294920 | tf_op jit(solution)/shard_map/ppermute | solution.py:492
  7.2 5.6 %collective-permute-start.12 = (bf16[48,1024]{1,0:T(8,128)(2,1)S(1)}, bf16[48,1024]{1,0:T(8,128)(2,1)S(1)}, u32[]{:S(2)}, u32[]{:S(2)}) collective-permute-start(bf16[48,1024]{1,0:T(8,128)(2,1)S(1)} %get-tuple-element.39), channel_id=1, source_target_pairs={{0,16},{4,20},{8,24},{12,28},{16,0},{20,4},{24,8},{28,12},{1,17},{... | collective-permute-start | bytes 294920 | tf_op jit(solution)/shard_map/ppermute | solution.py:492
  7.2 12.0 %collective-permute-start = (bf16[96,384]{1,0:T(8,128)(2,1)S(1)}, bf16[96,384]{1,0:T(8,128)(2,1)S(1)}, u32[]{:S(2)}, u32[]{:S(2)}) collective-permute-start(bf16[96,384]{1,0:T(8,128)(2,1)S(1)} %get-tuple-element.30.rest_0_), channel_id=1, source_target_pairs={{0,4},{4,0},{8,12},{12,8},{16,20},{20,16},{24,28},{28,24},{1,5},{5... | collective-permute-start | bytes 221192 | tf_op jit(solution)/shard_map/ppermute | solution.py:492
  7.9 11.4 %collective-permute-start.1 = (bf16[96,384]{1,0:T(8,128)(2,1)S(1)}, bf16[96,384]{1,0:T(8,128)(2,1)S(1)}, u32[]{:S(2)}, u32[]{:S(2)}) collective-permute-start(bf16[96,384]{1,0:T(8,128)(2,1)S(1)} %get-tuple-element.31), channel_id=1, source_target_pairs={{0,8},{4,12},{8,0},{12,4},{16,24},{20,28},{24,16},{28,20},{1,9},{5... | collective-permute-start | bytes 221192 | tf_op jit(solution)/shard_map/ppermute | solution.py:492
  10.7 9.1 %collective-permute-start.3 = (bf16[96,384]{1,0:T(8,128)(2,1)S(1)}, bf16[96,384]{1,0:T(8,128)(2,1)S(1)}, u32[]{:S(2)}, u32[]{:S(2)}) collective-permute-start(bf16[96,384]{1,0:T(8,128)(2,1)S(1)} %get-tuple-element.32), channel_id=1, source_target_pairs={{0,16},{4,20},{8,24},{12,28},{16,0},{20,4},{24,8},{28,12},{1,17},{... | collective-permute-start | bytes 221192 | tf_op jit(solution)/shard_map/ppermute | solution.py:492
  12.3 10.9 %collective-permute-start.5 = (bf16[96,384]{1,0:T(8,128)(2,1)S(1)}, bf16[96,384]{1,0:T(8,128)(2,1)S(1)}, u32[]{:S(2)}, u32[]{:S(2)}) collective-permute-start(bf16[96,384]{1,0:T(8,128)(2,1)S(1)} %get-tuple-element.33), channel_id=1, source_target_pairs={{0,24},{4,28},{8,16},{12,20},{16,8},{20,12},{24,0},{28,4},{1,25},{... | collective-permute-start | bytes 221192 | tf_op jit(solution)/shard_map/ppermute | solution.py:492
  12.7 5.8 %collective-permute-start.14 = (bf16[48,1024]{1,0:T(8,128)(2,1)S(1)}, bf16[48,1024]{1,0:T(8,128)(2,1)S(1)}, u32[]{:S(2)}, u32[]{:S(2)}) collective-permute-start(bf16[48,1024]{1,0:T(8,128)(2,1)S(1)} %collective-permute-done.8), channel_id=1, source_target_pairs={{0,16},{4,20},{8,24},{12,28},{16,0},{20,4},{24,8},{28,12},{1,17},{... | collective-permute-start | bytes 294920 | tf_op jit(solution)/shard_map/ppermute | solution.py:492
  18.6 4.6 %collective-permute-start.15 = (bf16[48,1024]{1,0:T(8,128)(2,1)S(1)}, bf16[48,1024]{1,0:T(8,128)(2,1)S(1)}, u32[]{:S(2)}, u32[]{:S(2)}) collective-permute-start(bf16[48,1024]{1,0:T(8,128)(2,1)S(1)} %collective-permute-done.12), channel_id=1, source_target_pairs={{0,8},{4,12},{8,0},{12,4},{16,24},{20,28},{24,16},{28,20},{1,9},{5... | collective-permute-start | bytes 294920 | tf_op jit(solution)/shard_map/ppermute | solution.py:492
  19.2 10.2 %collective-permute-start.7 = (bf16[96,1024]{1,0:T(8,128)(2,1)S(1)}, bf16[96,1024]{1,0:T(8,128)(2,1)S(1)}, u32[]{:S(2)}, u32[]{:S(2)}) collective-permute-start(bf16[96,1024]{1,0:T(8,128)(2,1)S(1)} %get-tuple-element.37.rest_0_), channel_id=1, source_target_pairs={{0,4},{4,0},{8,12},{12,8},{16,20},{20,16},{24,28},{28,24},{1,5},{5... | collective-permute-start | bytes 589832 | tf_op jit(solution)/shard_map/ppermute | solution.py:492
  19.3 4.5 %collective-permute-start.2 = (bf16[96,384]{1,0:T(8,128)(2,1)S(1)}, bf16[96,384]{1,0:T(8,128)(2,1)S(1)}, u32[]{:S(2)}, u32[]{:S(2)}) collective-permute-start(bf16[96,384]{1,0:T(8,128)(2,1)S(1)} %collective-permute-done.1.rest_2_), channel_id=1, source_target_pairs={{0,4},{4,0},{8,12},{12,8},{16,20},{20,16},{24,28},{28,24},{1,5},{5... | collective-permute-start | bytes 221192 | tf_op jit(solution)/shard_map/ppermute | solution.py:492
  19.8 9.6 %collective-permute-start.10 = (bf16[96,1024]{1,0:T(8,128)(2,1)S(1)}, bf16[96,1024]{1,0:T(8,128)(2,1)S(1)}, u32[]{:S(2)}, u32[]{:S(2)}) collective-permute-start(bf16[96,1024]{1,0:T(8,128)(2,1)S(1)} %constant_dynamic-update-slice_fusion.rest_2_), channel_id=1, source_target_pairs={{0,4},{4,0},{8,12},{12,8},{16,20},{20,16},{24,28},{28,24},{1,5},{5... | collective-permute-start | bytes 589832 | tf_op jit(solution)/shard_map/ppermute | solution.py:492
  23.2 6.3 %collective-permute-start.13 = (bf16[96,1024]{1,0:T(8,128)(2,1)S(1)}, bf16[96,1024]{1,0:T(8,128)(2,1)S(1)}, u32[]{:S(2)}, u32[]{:S(2)}) collective-permute-start(bf16[96,1024]{1,0:T(8,128)(2,1)S(1)} %constant_dynamic-update-slice_fusion.2.rest_4_), channel_id=1, source_target_pairs={{0,4},{4,0},{8,12},{12,8},{16,20},{20,16},{24,28},{28,24},{1,5},{5... | collective-permute-start | bytes 589832 | tf_op jit(solution)/shard_map/ppermute | solution.py:492
  23.2 6.9 %collective-permute-start.16 = (bf16[96,1024]{1,0:T(8,128)(2,1)S(1)}, bf16[96,1024]{1,0:T(8,128)(2,1)S(1)}, u32[]{:S(2)}, u32[]{:S(2)}) collective-permute-start(bf16[96,1024]{1,0:T(8,128)(2,1)S(1)} %constant_dynamic-update-slice_fusion.4.rest_0_), channel_id=1, source_target_pairs={{0,4},{4,0},{8,12},{12,8},{16,20},{20,16},{24,28},{28,24},{1,5},{5... | collective-permute-start | bytes 589832 | tf_op jit(solution)/shard_map/ppermute | solution.py:492
  23.8 1.3 %collective-permute-start.4 = (bf16[96,384]{1,0:T(8,128)(2,1)S(1)}, bf16[96,384]{1,0:T(8,128)(2,1)S(1)}, u32[]{:S(2)}, u32[]{:S(2)}) collective-permute-start(bf16[96,384]{1,0:T(8,128)(2,1)S(1)} %collective-permute-done.3.rest_4_), channel_id=1, source_target_pairs={{0,4},{4,0},{8,12},{12,8},{16,20},{20,16},{24,28},{28,24},{1,5},{5... | collective-permute-start | bytes 221192 | tf_op jit(solution)/shard_map/ppermute | solution.py:492
  25.0 1.3 %collective-permute-start.6 = (bf16[96,384]{1,0:T(8,128)(2,1)S(1)}, bf16[96,384]{1,0:T(8,128)(2,1)S(1)}, u32[]{:S(2)}, u32[]{:S(2)}) collective-permute-start(bf16[96,384]{1,0:T(8,128)(2,1)S(1)} %collective-permute-done.5.rest_6_), channel_id=1, source_target_pairs={{0,4},{4,0},{8,12},{12,8},{16,20},{20,16},{24,28},{28,24},{1,5},{5... | collective-permute-start | bytes 221192 | tf_op jit(solution)/shard_map/ppermute | solution.py:492
  32.0 2.7 %collective-permute-start.17 = (bf16[96,384]{1,0:T(8,128)(2,1)S(1)}, bf16[96,384]{1,0:T(8,128)(2,1)S(1)}, u32[]{:S(2)}, u32[]{:S(2)}) collective-permute-start(bf16[96,384]{1,0:T(8,128)(2,1)S(1)} %get-tuple-element.47), channel_id=1, source_target_pairs={{0,4},{4,0},{8,12},{12,8},{16,20},{20,16},{24,28},{28,24},{1,5},{5... | collective-permute-start | bytes 221192 | tf_op jit(solution)/shard_map/ppermute | solution.py:492
  32.4 4.9 %collective-permute-start.18 = (bf16[96,384]{1,0:T(8,128)(2,1)S(1)}, bf16[96,384]{1,0:T(8,128)(2,1)S(1)}, u32[]{:S(2)}, u32[]{:S(2)}) collective-permute-start(bf16[96,384]{1,0:T(8,128)(2,1)S(1)} %get-tuple-element.48), channel_id=1, source_target_pairs={{0,4},{4,0},{8,12},{12,8},{16,20},{20,16},{24,28},{28,24},{1,5},{5... | collective-permute-start | bytes 221192 | tf_op jit(solution)/shard_map/ppermute | solution.py:492
  32.6 7.1 %collective-permute-start.24 = (bf16[64,1024]{1,0:T(8,128)(2,1)S(1)}, bf16[64,1024]{1,0:T(8,128)(2,1)S(1)}, u32[]{:S(2)}, u32[]{:S(2)}) collective-permute-start(bf16[64,1024]{1,0:T(8,128)(2,1)S(1)} %get-tuple-element.55.rest_4_), channel_id=1, source_target_pairs={{0,1},{1,0},{2,3},{3,2},{4,5},{5,4},{6,7},{7,6},{8,9},{9,8},{10,11... | collective-permute-start | bytes 393224 | tf_op jit(solution)/shard_map/ppermute | solution.py:565
  34.2 3.3 %collective-permute-start.19 = (bf16[96,384]{1,0:T(8,128)(2,1)S(1)}, bf16[96,384]{1,0:T(8,128)(2,1)S(1)}, u32[]{:S(2)}, u32[]{:S(2)}) collective-permute-start(bf16[96,384]{1,0:T(8,128)(2,1)S(1)} %get-tuple-element.49), channel_id=1, source_target_pairs={{0,4},{4,0},{8,12},{12,8},{16,20},{20,16},{24,28},{28,24},{1,5},{5... | collective-permute-start | bytes 221192 | tf_op jit(solution)/shard_map/ppermute | solution.py:492
  34.2 3.3 %collective-permute-start.20 = (bf16[96,384]{1,0:T(8,128)(2,1)S(1)}, bf16[96,384]{1,0:T(8,128)(2,1)S(1)}, u32[]{:S(2)}, u32[]{:S(2)}) collective-permute-start(bf16[96,384]{1,0:T(8,128)(2,1)S(1)} %get-tuple-element.50), channel_id=1, source_target_pairs={{0,4},{4,0},{8,12},{12,8},{16,20},{20,16},{24,28},{28,24},{1,5},{5... | collective-permute-start | bytes 221192 | tf_op jit(solution)/shard_map/ppermute | solution.py:492
  34.7 12.9 %collective-permute-start.25 = (bf16[64,1024]{1,0:T(8,128)(2,1)S(1)}, bf16[64,1024]{1,0:T(8,128)(2,1)S(1)}, u32[]{:S(2)}, u32[]{:S(2)}) collective-permute-start(bf16[64,1024]{1,0:T(8,128)(2,1)S(1)} %get-tuple-element.55.rest_4_), channel_id=1, source_target_pairs={{0,2},{1,3},{2,0},{3,1},{4,6},{5,7},{6,4},{7,5},{8,10},{9,11},{10,... | collective-permute-start | bytes 393224 | tf_op jit(solution)/shard_map/ppermute | solution.py:565
  37.3 10.3 %collective-permute-start.26 = (bf16[64,1024]{1,0:T(8,128)(2,1)S(1)}, bf16[64,1024]{1,0:T(8,128)(2,1)S(1)}, u32[]{:S(2)}, u32[]{:S(2)}) collective-permute-start(bf16[64,1024]{1,0:T(8,128)(2,1)S(1)} %get-tuple-element.55.rest_4_), channel_id=1, source_target_pairs={{0,3},{1,2},{2,1},{3,0},{4,7},{5,6},{6,5},{7,4},{8,11},{9,10},{10,... | collective-permute-start | bytes 393224 | tf_op jit(solution)/shard_map/ppermute | solution.py:565
  37.6 10.1 %collective-permute-start.21 = (bf16[96,384]{1,0:T(8,128)(2,1)S(1)}, bf16[96,384]{1,0:T(8,128)(2,1)S(1)}, u32[]{:S(2)}, u32[]{:S(2)}) collective-permute-start(bf16[96,384]{1,0:T(8,128)(2,1)S(1)} %get-tuple-element.52), channel_id=1, source_target_pairs={{0,8},{4,12},{8,0},{12,4},{16,24},{20,28},{24,16},{28,20},{1,9},{5... | collective-permute-start | bytes 221192 | tf_op jit(solution)/shard_map/ppermute | solution.py:492
  38.3 9.4 %collective-permute-start.22 = (bf16[96,384]{1,0:T(8,128)(2,1)S(1)}, bf16[96,384]{1,0:T(8,128)(2,1)S(1)}, u32[]{:S(2)}, u32[]{:S(2)}) collective-permute-start(bf16[96,384]{1,0:T(8,128)(2,1)S(1)} %get-tuple-element.53), channel_id=1, source_target_pairs={{0,16},{4,20},{8,24},{12,28},{16,0},{20,4},{24,8},{28,12},{1,17},{... | collective-permute-start | bytes 221192 | tf_op jit(solution)/shard_map/ppermute | solution.py:492
  39.7 7.9 %collective-permute-start.23 = (bf16[96,384]{1,0:T(8,128)(2,1)S(1)}, bf16[96,384]{1,0:T(8,128)(2,1)S(1)}, u32[]{:S(2)}, u32[]{:S(2)}) collective-permute-start(bf16[96,384]{1,0:T(8,128)(2,1)S(1)} %get-tuple-element.54), channel_id=1, source_target_pairs={{0,24},{4,28},{8,16},{12,20},{16,8},{20,12},{24,0},{28,4},{1,25},{... | collective-permute-start | bytes 221192 | tf_op jit(solution)/shard_map/ppermute | solution.py:492

commit v3 on v2

--- a/solution.py
+++ b/solution.py
@@ -222,7 +222,6 @@
 
 
 ROUTES = (0, 2, 4, 6)
-HALF = MAXV // 2
 
 
 def head_lanes(core):
@@ -254,8 +253,8 @@
 
 
 def pack_kernel(counts_hbm, offsets_hbm, q_ref, k_ref, v_ref, g_ref, *rest):
-    sends, cot_refs = rest[:4], rest[4:7]
-    narrow, wide, counts_ref, offsets_ref, sems, scalar_sems = rest[7:]
+    sends, cot_ref, sides_ref = rest[:4], rest[4], rest[5]
+    narrow, wide, counts_ref, offsets_ref, sems, scalar_sems = rest[6:]
     scalars = scalar_copies((counts_hbm, offsets_hbm), (counts_ref, offsets_ref), scalar_sems)
     frames = q_ref.shape[1]
     last = frames - MAXV
@@ -291,10 +290,9 @@
             )
     for copy in copies[6:]:
         copy.wait()
-    cot = wide[0] * early + wide[1] * late
-    cot_refs[0][...] = cot
-    cot_refs[1][...] = cot[:HALF]
-    cot_refs[2][...] = cot[HALF:]
+    cot_ref[...] = wide[0] * early + wide[1] * late
+    for side, mask in enumerate((early, late)):
+        sides_ref[side] = jnp.broadcast_to(mask, (MAXV, 128))
 
 
 def forward_kernel(counts_hbm, offsets_hbm, *rest):
@@ -367,24 +365,25 @@
 
 
 def late_kernel(attended_ref, w_ref, begun_ref, *rest):
-    cots, dout_ref, wg_ref, cot = rest[:2], rest[2], rest[3], rest[4]
+    cots, dout_ref, kept_ref, sent_ref, cot = rest[:2], rest[2], rest[3], rest[4], rest[5]
     core = lax.axis_index("seq") % 2
     for index in range(2):
         cot[index * MAXV : (index + 1) * MAXV, :] = cots[index][...]
     dout_ref[...] = project(cot, w_ref, core)
-    wg_ref[...] = (
-        begun_ref[...]
-        + jnp.dot(
-            own_rows(attended_ref, core, slice(6 * MAXV, 8 * MAXV)),
-            cot[...],
-            preferred_element_type=jnp.float32,
-        )
-    ).astype(jnp.bfloat16)
+    total = begun_ref[...] + jnp.dot(
+        own_rows(attended_ref, core, slice(6 * MAXV, 8 * MAXV)),
+        cot[...],
+        preferred_element_type=jnp.float32,
+    )
+    half = total.shape[0] // 2
+    lower = lax.axis_index("clip") % 2 == 0
+    kept_ref[...] = jnp.where(lower, total[:half], total[half:]).astype(jnp.bfloat16)
+    sent_ref[...] = jnp.where(lower, total[half:], total[:half]).astype(jnp.bfloat16)
 
 
 def backward_kernel(packed, weights_ref, attended_ref, begun_ref, ended_ref, *rest):
-    outs = rest[:8]
-    dout, dq = rest[8:]
+    outs = rest[:2]
+    dout, dq = rest[2:]
     core = lax.axis_index("seq") % 2
     lanes = head_lanes(core)
     dout[: 6 * MAXV, :] = begun_ref[...]
@@ -417,21 +416,19 @@
     value_grad = value_grad.astype(jnp.bfloat16)
     for index in range(8):
         rows = slice(index * MAXV, (index + 1) * MAXV)
-        outs[index][:, 0:128] = dq[rows, :]
-        outs[index][:, 128:256] = key_grad[rows]
-        outs[index][:, 256:384] = value_grad[rows]
-
-
-def combine_kernel(*refs):
+        outs[index % 2][index // 2, :, 0:128] = dq[rows, :]
+        outs[index % 2][index // 2, :, 128:256] = key_grad[rows]
+        outs[index % 2][index // 2, :, 256:384] = value_grad[rows]
+
+
+def combine_kernel(kept, crossed, *outs):
     for index in range(4):
-        refs[8 + index][...] = refs[index][...] + refs[4 + index][...]
-
-
-def unpack_kernel(scale, counts_hbm, offsets_hbm, *rest):
-    blocks, shares = rest[:4], rest[4:-10]
-    outs, wg_ref = rest[-10:-7], rest[-7]
-    edges, blank, counts_ref, offsets_ref, sems, scalar_sems = rest[-6:]
-    scalars = scalar_copies((counts_hbm, offsets_hbm), (counts_ref, offsets_ref), scalar_sems)
+        outs[index][...] = kept[index] + crossed[index]
+
+
+def unpack_kernel(scale, sides_ref, *rest):
+    blocks, shares, outs, wg_ref = rest[:4], rest[4:6], rest[6:9], rest[9]
+    edges, blank, sems = rest[10:]
     device = lax.axis_index("seq")
     frames = outs[0].shape[1]
     last = frames - MAXV
@@ -444,17 +441,13 @@
             )
         )
         copies[-1].start()
-    for copy in scalars:
-        copy.wait()
-    begin, end_start = span_of(counts_ref, offsets_ref, device)
-    sides = slot_masks(begin, end_start)
     for route, block in zip(ROUTES, blocks):
         chip = (device ^ route) // 2
         lanes = pl.ds(pl.multiple_of(chip * 128, 128), 128)
         for index in range(3):
             piece = block[:, index * 128 : (index + 1) * 128]
             for side in range(2):
-                edges[index, side, :, lanes] = piece * sides[side]
+                edges[index, side, :, lanes] = piece * sides_ref[side]
     for index in range(3):
         for side, start in enumerate((0, last)):
             copies.append(
@@ -465,10 +458,11 @@
                 )
             )
             copies[-1].start()
-    terms = [share[...].astype(jnp.float32) for share in shares]
-    while len(terms) > 1:
-        terms = [left + right for left, right in zip(terms[::2], terms[1::2])]
-    wg_ref[...] = terms[0] * scale
+    lower = lax.axis_index("clip") % 2 == 0
+    mine, other = [share[...].astype(jnp.float32) * scale for share in shares]
+    half = mine.shape[0]
+    wg_ref[:half, :] = jnp.where(lower, mine, other)
+    wg_ref[half:, :] = jnp.where(lower, other, mine)
     for copy in copies:
         copy.wait()
 
@@ -510,10 +504,9 @@
     table = pltpu.SMEM(visible_counts.shape, jnp.int32)
     tables = [table, table]
     pair_sems = pltpu.SemaphoreType.DMA((2,))
-    half = jax.ShapeDtypeStruct((HALF, width), bf16)
-    *sends, cot, cot_a, cot_b = seen(
+    *sends, cot, sides = seen(
         pack_kernel,
-        [narrow] * 4 + [wide, half, half],
+        [narrow] * 4 + [wide, pltpu.VMEM((2, MAXV, 128), bf16)],
         [ANYWHERE] * 6,
         (counts, offsets, *map(in_hbm, (queries, keys, values, out_cotangent))),
         [
@@ -525,12 +518,7 @@
         ],
     )
     even = [sends[0]] + [shift(sends[i], ROUTES[i]) for i in (1, 2, 3)]
-    x_a, y_b = shift(cot_a, 2), shift(cot_b, 4)
-    x_b, y_a = shift(cot_b, 2), shift(cot_a, 4)
-    d_a, d_b = shift(x_a, 4), shift(y_b, 2)
-    even_cot = [cot] + [
-        jnp.concatenate(pair, axis=0) for pair in ((x_a, x_b), (y_a, y_b), (d_a, d_b))
-    ]
+    even_cot = [cot] + [shift(cot, ROUTES[i]) for i in (1, 2, 3)]
     odd = [shift(block, 1) for block in even]
     odd_cot = [shift(block, 1) for block in even_cot]
     blocks = [block for pair in zip(even, odd) for block in pair]
@@ -553,27 +541,35 @@
         (attended, out_weight, *cots[:6]),
         [pltpu.VMEM((6 * MAXV, width), bf16)],
     )
-    ended, partial = seen(
+    share = jax.ShapeDtypeStruct((out_weight.shape[0] // 2, width), bf16)
+    ended, mine, sent = seen(
         late_kernel,
-        [pltpu.VMEM((2 * MAXV, 128), bf16), jax.ShapeDtypeStruct(out_weight.shape, bf16)],
+        [pltpu.VMEM((2 * MAXV, 128), bf16), share, share],
         [LOCAL] * 5,
         (attended, out_weight, begun_wg, *cots[6:]),
         [pltpu.VMEM((2 * MAXV, width), bf16)],
     )
-    shares = [partial]
-    for step in range(1, clips):
-        shares.append(lax.ppermute(partial, "clip", [(i, i ^ step) for i in range(clips)]))
-    grads = seen(
+
+    def across(block, step):
+        return lax.ppermute(block, "clip", [(i, i ^ step) for i in range(clips)])
+
+    other = across(sent, 1)
+    step = 1
+    while step < clips:
+        mine = (mine.astype(jnp.float32) + other.astype(jnp.float32)).astype(bf16)
+        step *= 2
+        if step < clips:
+            other = across(mine, step)
+    shares = [mine, across(mine, 1)]
+    kept, leaving = seen(
         backward_kernel,
-        [narrow] * 8,
+        [jax.ShapeDtypeStruct((4, MAXV, 384), bf16)] * 2,
         [LOCAL] * 5,
         (packed, weights, attended, begun, ended),
         [pltpu.VMEM((rows, 128), bf16)] * 2,
     )
-    crossed = [shift(grads[i + 1], 1) for i in ROUTES]
-    joined = seen(
-        combine_kernel, [narrow] * 4, [LOCAL] * 8, (*[grads[i] for i in ROUTES], *crossed)
-    )
+    crossed = shift(leaving, 1)
+    joined = seen(combine_kernel, [narrow] * 4, [LOCAL] * 2, (kept, crossed))
     home = [joined[0]] + [shift(joined[i], ROUTES[i]) for i in (1, 2, 3)]
     frames = queries.shape[1]
     scale = (clips * VIS_DEV * pairs) ** (-0.5)
@@ -582,14 +578,12 @@
             functools.partial(unpack_kernel, scale),
             [jax.ShapeDtypeStruct(queries.shape, bf16)] * 3
             + [jax.ShapeDtypeStruct(out_weight.shape, jnp.float32)],
-            [ANYWHERE] * 2 + [LOCAL] * (4 + len(shares)),
-            (counts, offsets, *home, *shares),
+            [LOCAL] * 7,
+            (sides, *home, *shares),
             [
                 pltpu.VMEM((3, 2, MAXV, queries.shape[2]), bf16),
                 pltpu.VMEM((frames - 2 * MAXV, queries.shape[2]), bf16),
-                *tables,
                 pltpu.SemaphoreType.DMA((9,)),
-                pair_sems,
             ],
             [ANYWHERE] * 3 + [LOCAL],
         )

time: 50.3 us -> 46.7 us (0.928)
  waiting for transfers between devices: 17.2 us -> 14.6 us
    ppermute x3, waiting for transfers between devices: 6.59 us -> 3.57 us  [across(): return lax.ppermute(block, 'clip', [(i, i ^ step) for i in range(clips)])]
    ppermute x24 -> x18, starting transfers between devices: 18.1 us -> 15.7 us  [shift(): return lax.ppermute(block, 'seq', [(i, i ^ step) for i in range(pairs)])]
    ppermute x3, starting transfers between devices: 4.39 us -> 6.38 us  [across(): return lax.ppermute(block, 'clip', [(i, i ^ step) for i in range(clips)])]
    ppermute x24 -> x18, waiting for transfers between devices: 10.6 us -> 11 us  [shift(): return lax.ppermute(block, 'seq', [(i, i ^ step) for i in range(pairs)])]
  transfers between devices with their start and end apart: 27 -> 21, of which waited for: 8 -> 7; matrix products, arithmetic and copies ran while one was open for 0% -> 0% of each run, Pallas kernels for 8% -> 12%
where the time goes in v3:
time: 46.7 us; the launch traced here: 46.5 us
  starting transfers between devices  22.1 us (47%)
  waiting for transfers between devices  14.6 us (31%)
  Pallas kernels  9.07 us (19%)
  between operations  0.75 us (2%)
    ppermute x18, starting transfers between devices, shift(): return lax.ppermute(block, 'seq', [(i, i ^ step) for i in range(pairs)])  15.7 us
    ppermute x18, waiting for transfers between devices, shift(): return lax.ppermute(block, 'seq', [(i, i ^ step) for i in range(pairs)])  11 us
    pallas_call x7, Pallas kernels, seen(): pl.pallas_call(kernel, out_shape=outs, in_specs=specs, out_specs=out_spec...  9.07 us
    ppermute x3, starting transfers between devices, across(): return lax.ppermute(block, 'clip', [(i, i ^ step) for i in range(clips)])  6.38 us
    ppermute x3, waiting for transfers between devices, across(): return lax.ppermute(block, 'clip', [(i, i ^ step) for i in range(clips)])  3.57 us
  transfers between devices with their start and end apart: 21, of which 7 were waited for; matrix products, arithmetic and copies ran while one was open for 0% of the time, Pallas kernels for 12%

profile of v3, /device:TPU:0, one launch (start us, length us, event | category | flops | bytes accessed | tf_op | source)
XLA Modules:
  0.0 46.5 jit_solution(5188834244018164138)
XLA Ops:
  0.6 0.0 copy-start
  0.6 1.4 %shard_map.102 = (bf16[96,384]{1,0:T(8,128)(2,1)S(1)}, bf16[96,384]{1,0:T(8,128)(2,1)S(1)}, bf16[96,384]{1,0:T(8,128)(2,1)S(1)}, bf16[96,384]{1,0:T(8,128)(2,1)S...) custom-call(s32[1,8]{1,0:T(1,128)} %counts_hbm.3, s32[1,8]{1,0:T(1,128)} %offsets_hbm.3, ...), custom_call_target="tpu_custom_call" | custom-call | tf_op jit(solution)/shard_map/pallas_call | solution.py:492
  2.1 3.0 %collective-permute-start.8 = (bf16[96,1024]{1,0:T(8,128)(2,1)S(1)}, bf16[96,1024]{1,0:T(8,128)(2,1)S(1)}, u32[]{:S(2)}, u32[]{:S(2)}) collective-permute-start(bf16[96,1024]{1,0:T(8,128)(2,1)S(1)} %get-tuple-element.32.rest_0_), channel_id=1, source_target_pairs={{0,8},{4,12},{8,0},{12,4},{16,24},{20,28},{24,16},{28,20},{1,9},{5... | collective-permute-start | bytes 589832 | tf_op jit(solution)/shard_map/ppermute | solution.py:486
  5.1 1.5 %collective-permute-start.10 = (bf16[96,1024]{1,0:T(8,128)(2,1)S(1)}, bf16[96,1024]{1,0:T(8,128)(2,1)S(1)}, u32[]{:S(2)}, u32[]{:S(2)}) collective-permute-start(bf16[96,1024]{1,0:T(8,128)(2,1)S(1)} %get-tuple-element.32.rest_0_), channel_id=1, source_target_pairs={{0,16},{4,20},{8,24},{12,28},{16,0},{20,4},{24,8},{28,12},{1,17},{... | collective-permute-start | bytes 589832 | tf_op jit(solution)/shard_map/ppermute | solution.py:486
  6.6 0.0 collective-permute-start.12
  6.6 0.0 collective-permute-start
  6.6 1.9 %collective-permute-start.1 = (bf16[96,384]{1,0:T(8,128)(2,1)S(1)}, bf16[96,384]{1,0:T(8,128)(2,1)S(1)}, u32[]{:S(2)}, u32[]{:S(2)}) collective-permute-start(bf16[96,384]{1,0:T(8,128)(2,1)S(1)} %get-tuple-element.26), channel_id=1, source_target_pairs={{0,8},{4,12},{8,0},{12,4},{16,24},{20,28},{24,16},{28,20},{1,9},{5... | collective-permute-start | bytes 221192 | tf_op jit(solution)/shard_map/ppermute | solution.py:486
  8.6 0.0 collective-permute-done.rest_1_
  8.6 1.5 %collective-permute-start.3 = (bf16[96,384]{1,0:T(8,128)(2,1)S(1)}, bf16[96,384]{1,0:T(8,128)(2,1)S(1)}, u32[]{:S(2)}, u32[]{:S(2)}) collective-permute-start(bf16[96,384]{1,0:T(8,128)(2,1)S(1)} %get-tuple-element.27), channel_id=1, source_target_pairs={{0,16},{4,20},{8,24},{12,28},{16,0},{20,4},{24,8},{28,12},{1,17},{... | collective-permute-start | bytes 221192 | tf_op jit(solution)/shard_map/ppermute | solution.py:486
  10.1 5.7 %collective-permute-done.1.rest_2_ = bf16[96,384]{1,0:T(8,128)(2,1)S(1)} collective-permute-done((bf16[96,384]{1,0:T(8,128)(2,1)S(1)}, bf16[96,384]{1,0:T(8,128)(2,1)S(1)}, u32[]{:S(2)}, u32[]{:S(2)}) %collective-permute-start.1) | collective-permute-done | bytes 73760 | tf_op jit(solution)/shard_map/ppermute | solution.py:486
  15.8 2.7 %collective-permute-start.5 = (bf16[96,384]{1,0:T(8,128)(2,1)S(1)}, bf16[96,384]{1,0:T(8,128)(2,1)S(1)}, u32[]{:S(2)}, u32[]{:S(2)}) collective-permute-start(bf16[96,384]{1,0:T(8,128)(2,1)S(1)} %get-tuple-element.28), channel_id=1, source_target_pairs={{0,24},{4,28},{8,16},{12,20},{16,8},{20,12},{24,0},{28,4},{1,25},{... | collective-permute-start | bytes 221192 | tf_op jit(solution)/shard_map/ppermute | solution.py:486
  18.5 0.0 collective-permute-done.3.rest_4_
  18.5 0.0 collective-permute-start.2
  18.5 2.6 %collective-permute-done.5.rest_6_ = bf16[96,384]{1,0:T(8,128)(2,1)S(1)} collective-permute-done((bf16[96,384]{1,0:T(8,128)(2,1)S(1)}, bf16[96,384]{1,0:T(8,128)(2,1)S(1)}, u32[]{:S(2)}, u32[]{:S(2)}) %collective-permute-start.5) | collective-permute-done | bytes 73760 | tf_op jit(solution)/shard_map/ppermute | solution.py:486
  21.1 0.0 collective-permute-start.7
  21.1 0.0 collective-permute-done.8.rest_2_
  21.1 0.5 %collective-permute-start.9 = (bf16[96,1024]{1,0:T(8,128)(2,1)S(1)}, bf16[96,1024]{1,0:T(8,128)(2,1)S(1)}, u32[]{:S(2)}, u32[]{:S(2)}) collective-permute-start(bf16[96,1024]{1,0:T(8,128)(2,1)S(1)} %collective-permute-done.8.rest_2_), channel_id=1, source_target_pairs={{0,4},{4,0},{8,12},{12,8},{16,20},{20,16},{24,28},{28,24},{1,5},{5... | collective-permute-start | bytes 589832 | tf_op jit(solution)/shard_map/ppermute | solution.py:486
  21.6 0.0 collective-permute-done.10.rest_4_
  21.6 0.1 collective-permute-start.11
  21.7 0.0 collective-permute-done.12.rest_0_
  21.7 0.4 collective-permute-start.13
  22.1 0.0 collective-permute-done.2.rest_3_
  22.1 0.1 collective-permute-start.4
  22.2 1.3 %collective-permute-done.4.rest_5_ = bf16[96,384]{1,0:T(8,128)(2,1)S(1)} collective-permute-done((bf16[96,384]{1,0:T(8,128)(2,1)S(1)}, bf16[96,384]{1,0:T(8,128)(2,1)S(1)}, u32[]{:S(2)}, u32[]{:S(2)}) %collective-permute-start.4) | collective-permute-done | bytes 73760 | tf_op jit(solution)/shard_map/ppermute | solution.py:486
  23.5 0.2 collective-permute-start.6
  23.7 1.0 %collective-permute-done.6.rest_7_ = bf16[96,384]{1,0:T(8,128)(2,1)S(1)} collective-permute-done((bf16[96,384]{1,0:T(8,128)(2,1)S(1)}, bf16[96,384]{1,0:T(8,128)(2,1)S(1)}, u32[]{:S(2)}, u32[]{:S(2)}) %collective-permute-start.6) | collective-permute-done | bytes 73760 | tf_op jit(solution)/shard_map/ppermute | solution.py:486
  24.8 3.1 %shard_map.103 = (bf16[768,384]{1,0:T(8,128)(2,1)S(1)}, f32[768,768]{1,0:T(8,128)S(1)}, bf16[128,768]{1,0:T(8,128)(2,1)S(1)}) custom-call(s32[1,8]{1,0:T(1,128)} %counts_hbm.3, s32[1,8]{1,0:T(1,128)} %offsets_hbm.3, bf16[96,384]{1,0:T(8,128)(2,1)S(1)} %get-tuple-element.25.rest_0_, bf16[96,384]{1,0:T(8,128)(2,1)S(1)} %collective-permute-done.rest_1_, ...), custom_call_target="tpu_custom_call" | custom-call | tf_op jit(solution)/shard_map/pallas_call | solution.py:492
  27.9 0.0 collective-permute-done.7.rest_1_
  27.9 0.0 collective-permute-done.9.rest_3_
  27.9 0.0 collective-permute-done.11.rest_5_
  27.9 0.0 copy-done
  27.9 0.7 %shard_map.104 = (bf16[576,128]{1,0:T(8,128)(2,1)S(1)}, f32[64,1024]{1,0:T(8,128)S(1)}) custom-call(bf16[128,768]{1,0:T(8,128)(2,1)S(1)} %get-tuple-element.31.attended_ref, bf16[64,1024]{1,0:T(8,128)(2,1)S(1)} %copy-done, bf16[96,1024]{1,0:T(8,128)(2,1)S(1)} %get-tuple-element.32.rest_0_, bf16[96,1024]{1,0:T(8,128)(2,1)S(1)} %collective-permute-done.7.rest_1_, ...), custom_call_target="tpu_custom_call" | custom-call | tf_op jit(solution)/shard_map/pallas_call | solution.py:492
  28.6 0.0 collective-permute-done.13.rest_1_
  28.6 0.3 shard_map.105
  29.0 1.9 %collective-permute-start.18 = (bf16[32,1024]{1,0:T(8,128)(2,1)S(1)}, bf16[32,1024]{1,0:T(8,128)(2,1)S(1)}, u32[]{:S(2)}, u32[]{:S(2)}) collective-permute-start(bf16[32,1024]{1,0:T(8,128)(2,1)S(1)} %get-tuple-element.43), channel_id=1, source_target_pairs={{0,1},{1,0},{2,3},{3,2},{4,5},{5,4},{6,7},{7,6},{8,9},{9,8},{10,11... | collective-permute-start | bytes 196616 | tf_op jit(solution)/shard_map/ppermute | solution.py:554
  30.8 1.5 %shard_map.106 = (bf16[4,96,384]{2,1,0:T(8,128)(2,1)S(1)}, bf16[4,96,384]{2,1,0:T(8,128)(2,1)S(1)}) custom-call(bf16[768,384]{1,0:T(8,128)(2,1)S(1)} %get-tuple-element.29.packed, f32[768,768]{1,0:T(8,128)S(1)} %get-tuple-element.30.weights_ref, bf16[128,768]{1,0:T(8,128)(2,1)S(1)} %get-tuple-element.31.attended_ref, ...), custom_call_target="tpu_custom_call" | custom-call | tf_op jit(solution)/shard_map/pallas_call | solution.py:492
  32.4 0.1 collective-permute-start.14
  32.5 0.9 %collective-permute-done.18 = bf16[32,1024]{1,0:T(8,128)(2,1)S(1)} collective-permute-done((bf16[32,1024]{1,0:T(8,128)(2,1)S(1)}, bf16[32,1024]{1,0:T(8,128)(2,1)S(1)}, u32[]{:S(2)}, u32[]{:S(2)}) %collective-permute-start.18) | collective-permute-done | bytes 65568 | tf_op jit(solution)/shard_map/ppermute | solution.py:554
  33.4 2.8 %collective-permute-start.19 = (bf16[32,1024]{1,0:T(8,128)(2,1)S(1)}, bf16[32,1024]{1,0:T(8,128)(2,1)S(1)}, u32[]{:S(2)}, u32[]{:S(2)}) collective-permute-start(bf16[32,1024]{1,0:T(8,128)(2,1)S(1)} %add_convert_fusion.1), channel_id=1, source_target_pairs={{0,2},{1,3},{2,0},{3,1},{4,6},{5,7},{6,4},{7,5},{8,10},{9,11},{10,... | collective-permute-start | bytes 196616 | tf_op jit(solution)/shard_map/ppermute | solution.py:554
  36.2 0.0 collective-permute-done.14.crossed
  36.3 1.6 %collective-permute-start.15 = (bf16[96,384]{1,0:T(8,128)(2,1)S(1)}, bf16[96,384]{1,0:T(8,128)(2,1)S(1)}, u32[]{:S(2)}, u32[]{:S(2)}) collective-permute-start(bf16[96,384]{1,0:T(8,128)(2,1)S(1)} %get-tuple-element.39), channel_id=1, source_target_pairs={{0,8},{4,12},{8,0},{12,4},{16,24},{20,28},{24,16},{28,20},{1,9},{5... | collective-permute-start | bytes 221192 | tf_op jit(solution)/shard_map/ppermute | solution.py:486
  37.8 1.5 %collective-permute-start.16 = (bf16[96,384]{1,0:T(8,128)(2,1)S(1)}, bf16[96,384]{1,0:T(8,128)(2,1)S(1)}, u32[]{:S(2)}, u32[]{:S(2)}) collective-permute-start(bf16[96,384]{1,0:T(8,128)(2,1)S(1)} %get-tuple-element.40), channel_id=1, source_target_pairs={{0,16},{4,20},{8,24},{12,28},{16,0},{20,4},{24,8},{28,12},{1,17},{... | collective-permute-start | bytes 221192 | tf_op jit(solution)/shard_map/ppermute | solution.py:486
  39.3 0.5 collective-permute-start.17
  39.8 0.0 collective-permute-done.19
  39.8 1.6 %collective-permute-start.20 = (bf16[32,1024]{1,0:T(8,128)(2,1)S(1)}, bf16[32,1024]{1,0:T(8,128)(2,1)S(1)}, u32[]{:S(2)}, u32[]{:S(2)}) collective-permute-start(bf16[32,1024]{1,0:T(8,128)(2,1)S(1)} %add_convert_fusion.rest_4_), channel_id=1, source_target_pairs={{0,1},{1,0},{2,3},{3,2},{4,5},{5,4},{6,7},{7,6},{8,9},{9,8},{10,11... | collective-permute-start | bytes 196616 | tf_op jit(solution)/shard_map/ppermute | solution.py:554
  41.5 2.7 %collective-permute-done.20.rest_5_ = bf16[32,1024]{1,0:T(8,128)(2,1)S(1)} collective-permute-done((bf16[32,1024]{1,0:T(8,128)(2,1)S(1)}, bf16[32,1024]{1,0:T(8,128)(2,1)S(1)}, u32[]{:S(2)}, u32[]{:S(2)}) %collective-permute-start.20) | collective-permute-done | bytes 65568 | tf_op jit(solution)/shard_map/ppermute | solution.py:554
  44.2 0.0 collective-permute-done.15.rest_1_
  44.2 0.0 collective-permute-done.16.rest_2_
  44.2 0.4 collective-permute-done.17.rest_3_
  44.6 1.9 %shard_map.108 = (bf16[1,512,512]{2,1,0:T(8,128)(2,1)}, bf16[1,512,512]{2,1,0:T(8,128)(2,1)}, bf16[1,512,512]{2,1,0:T(8,128)(2,1)}, f32[64,1024]{1,0:T(8,128)}) custom-call(bf16[2,96,128]{2,1,0:T(8,128)(2,1)S(1)} %get-tuple-element.24.sides_ref, bf16[96,384]{1,0:T(8,128)(2,1)S(1)} %get-tuple-element.38.rest_0_, ...), custom_call_target="tpu_custom_call" | custom-call | tf_op jit(solution)/shard_map/pallas_call | solution.py:492
  (3 shorter events, 0.1 us)
Async XLA Ops:
  0.6 27.3 %copy-start = (bf16[64,1024]{1,0:T(8,128)(2,1)S(1)}, bf16[64,1024]{1,0:T(8,128)(2,1)}, u32[]{:S(2)}) copy-start(bf16[64,1024]{1,0:T(8,128)(2,1)} %w_ref.3) | copy-start | bytes 393220
  2.1 19.0 %collective-permute-start.8 = (bf16[96,1024]{1,0:T(8,128)(2,1)S(1)}, bf16[96,1024]{1,0:T(8,128)(2,1)S(1)}, u32[]{:S(2)}, u32[]{:S(2)}) collective-permute-start(bf16[96,1024]{1,0:T(8,128)(2,1)S(1)} %get-tuple-element.32.rest_0_), channel_id=1, source_target_pairs={{0,8},{4,12},{8,0},{12,4},{16,24},{20,28},{24,16},{28,20},{1,9},{5... | collective-permute-start | bytes 589832 | tf_op jit(solution)/shard_map/ppermute | solution.py:486
  5.1 16.5 %collective-permute-start.10 = (bf16[96,1024]{1,0:T(8,128)(2,1)S(1)}, bf16[96,1024]{1,0:T(8,128)(2,1)S(1)}, u32[]{:S(2)}, u32[]{:S(2)}) collective-permute-start(bf16[96,1024]{1,0:T(8,128)(2,1)S(1)} %get-tuple-element.32.rest_0_), channel_id=1, source_target_pairs={{0,16},{4,20},{8,24},{12,28},{16,0},{20,4},{24,8},{28,12},{1,17},{... | collective-permute-start | bytes 589832 | tf_op jit(solution)/shard_map/ppermute | solution.py:486
  6.6 15.1 %collective-permute-start.12 = (bf16[96,1024]{1,0:T(8,128)(2,1)S(1)}, bf16[96,1024]{1,0:T(8,128)(2,1)S(1)}, u32[]{:S(2)}, u32[]{:S(2)}) collective-permute-start(bf16[96,1024]{1,0:T(8,128)(2,1)S(1)} %get-tuple-element.32.rest_0_), channel_id=1, source_target_pairs={{0,24},{4,28},{8,16},{12,20},{16,8},{20,12},{24,0},{28,4},{1,25},{... | collective-permute-start | bytes 589832 | tf_op jit(solution)/shard_map/ppermute | solution.py:486
  6.6 2.0 %collective-permute-start = (bf16[96,384]{1,0:T(8,128)(2,1)S(1)}, bf16[96,384]{1,0:T(8,128)(2,1)S(1)}, u32[]{:S(2)}, u32[]{:S(2)}) collective-permute-start(bf16[96,384]{1,0:T(8,128)(2,1)S(1)} %get-tuple-element.25.rest_0_), channel_id=1, source_target_pairs={{0,4},{4,0},{8,12},{12,8},{16,20},{20,16},{24,28},{28,24},{1,5},{5... | collective-permute-start | bytes 221192 | tf_op jit(solution)/shard_map/ppermute | solution.py:486
  6.6 9.2 %collective-permute-start.1 = (bf16[96,384]{1,0:T(8,128)(2,1)S(1)}, bf16[96,384]{1,0:T(8,128)(2,1)S(1)}, u32[]{:S(2)}, u32[]{:S(2)}) collective-permute-start(bf16[96,384]{1,0:T(8,128)(2,1)S(1)} %get-tuple-element.26), channel_id=1, source_target_pairs={{0,8},{4,12},{8,0},{12,4},{16,24},{20,28},{24,16},{28,20},{1,9},{5... | collective-permute-start | bytes 221192 | tf_op jit(solution)/shard_map/ppermute | solution.py:486
  8.6 9.9 %collective-permute-start.3 = (bf16[96,384]{1,0:T(8,128)(2,1)S(1)}, bf16[96,384]{1,0:T(8,128)(2,1)S(1)}, u32[]{:S(2)}, u32[]{:S(2)}) collective-permute-start(bf16[96,384]{1,0:T(8,128)(2,1)S(1)} %get-tuple-element.27), channel_id=1, source_target_pairs={{0,16},{4,20},{8,24},{12,28},{16,0},{20,4},{24,8},{28,12},{1,17},{... | collective-permute-start | bytes 221192 | tf_op jit(solution)/shard_map/ppermute | solution.py:486
  15.8 5.3 %collective-permute-start.5 = (bf16[96,384]{1,0:T(8,128)(2,1)S(1)}, bf16[96,384]{1,0:T(8,128)(2,1)S(1)}, u32[]{:S(2)}, u32[]{:S(2)}) collective-permute-start(bf16[96,384]{1,0:T(8,128)(2,1)S(1)} %get-tuple-element.28), channel_id=1, source_target_pairs={{0,24},{4,28},{8,16},{12,20},{16,8},{20,12},{24,0},{28,4},{1,25},{... | collective-permute-start | bytes 221192 | tf_op jit(solution)/shard_map/ppermute | solution.py:486
  18.5 3.6 %collective-permute-start.2 = (bf16[96,384]{1,0:T(8,128)(2,1)S(1)}, bf16[96,384]{1,0:T(8,128)(2,1)S(1)}, u32[]{:S(2)}, u32[]{:S(2)}) collective-permute-start(bf16[96,384]{1,0:T(8,128)(2,1)S(1)} %collective-permute-done.1.rest_2_), channel_id=1, source_target_pairs={{0,4},{4,0},{8,12},{12,8},{16,20},{20,16},{24,28},{28,24},{1,5},{5... | collective-permute-start | bytes 221192 | tf_op jit(solution)/shard_map/ppermute | solution.py:486
  21.1 6.8 %collective-permute-start.7 = (bf16[96,1024]{1,0:T(8,128)(2,1)S(1)}, bf16[96,1024]{1,0:T(8,128)(2,1)S(1)}, u32[]{:S(2)}, u32[]{:S(2)}) collective-permute-start(bf16[96,1024]{1,0:T(8,128)(2,1)S(1)} %get-tuple-element.32.rest_0_), channel_id=1, source_target_pairs={{0,4},{4,0},{8,12},{12,8},{16,20},{20,16},{24,28},{28,24},{1,5},{5... | collective-permute-start | bytes 589832 | tf_op jit(solution)/shard_map/ppermute | solution.py:486
  21.1 6.8 %collective-permute-start.9 = (bf16[96,1024]{1,0:T(8,128)(2,1)S(1)}, bf16[96,1024]{1,0:T(8,128)(2,1)S(1)}, u32[]{:S(2)}, u32[]{:S(2)}) collective-permute-start(bf16[96,1024]{1,0:T(8,128)(2,1)S(1)} %collective-permute-done.8.rest_2_), channel_id=1, source_target_pairs={{0,4},{4,0},{8,12},{12,8},{16,20},{20,16},{24,28},{28,24},{1,5},{5... | collective-permute-start | bytes 589832 | tf_op jit(solution)/shard_map/ppermute | solution.py:486
  21.6 6.3 %collective-permute-start.11 = (bf16[96,1024]{1,0:T(8,128)(2,1)S(1)}, bf16[96,1024]{1,0:T(8,128)(2,1)S(1)}, u32[]{:S(2)}, u32[]{:S(2)}) collective-permute-start(bf16[96,1024]{1,0:T(8,128)(2,1)S(1)} %collective-permute-done.10.rest_4_), channel_id=1, source_target_pairs={{0,4},{4,0},{8,12},{12,8},{16,20},{20,16},{24,28},{28,24},{1,5},{5... | collective-permute-start | bytes 589832 | tf_op jit(solution)/shard_map/ppermute | solution.py:486
  21.7 6.9 %collective-permute-start.13 = (bf16[96,1024]{1,0:T(8,128)(2,1)S(1)}, bf16[96,1024]{1,0:T(8,128)(2,1)S(1)}, u32[]{:S(2)}, u32[]{:S(2)}) collective-permute-start(bf16[96,1024]{1,0:T(8,128)(2,1)S(1)} %collective-permute-done.12.rest_0_), channel_id=1, source_target_pairs={{0,4},{4,0},{8,12},{12,8},{16,20},{20,16},{24,28},{28,24},{1,5},{5... | collective-permute-start | bytes 589832 | tf_op jit(solution)/shard_map/ppermute | solution.py:486
  22.1 1.4 %collective-permute-start.4 = (bf16[96,384]{1,0:T(8,128)(2,1)S(1)}, bf16[96,384]{1,0:T(8,128)(2,1)S(1)}, u32[]{:S(2)}, u32[]{:S(2)}) collective-permute-start(bf16[96,384]{1,0:T(8,128)(2,1)S(1)} %collective-permute-done.3.rest_4_), channel_id=1, source_target_pairs={{0,4},{4,0},{8,12},{12,8},{16,20},{20,16},{24,28},{28,24},{1,5},{5... | collective-permute-start | bytes 221192 | tf_op jit(solution)/shard_map/ppermute | solution.py:486
  23.5 1.3 %collective-permute-start.6 = (bf16[96,384]{1,0:T(8,128)(2,1)S(1)}, bf16[96,384]{1,0:T(8,128)(2,1)S(1)}, u32[]{:S(2)}, u32[]{:S(2)}) collective-permute-start(bf16[96,384]{1,0:T(8,128)(2,1)S(1)} %collective-permute-done.5.rest_6_), channel_id=1, source_target_pairs={{0,4},{4,0},{8,12},{12,8},{16,20},{20,16},{24,28},{28,24},{1,5},{5... | collective-permute-start | bytes 221192 | tf_op jit(solution)/shard_map/ppermute | solution.py:486
  29.0 4.4 %collective-permute-start.18 = (bf16[32,1024]{1,0:T(8,128)(2,1)S(1)}, bf16[32,1024]{1,0:T(8,128)(2,1)S(1)}, u32[]{:S(2)}, u32[]{:S(2)}) collective-permute-start(bf16[32,1024]{1,0:T(8,128)(2,1)S(1)} %get-tuple-element.43), channel_id=1, source_target_pairs={{0,1},{1,0},{2,3},{3,2},{4,5},{5,4},{6,7},{7,6},{8,9},{9,8},{10,11... | collective-permute-start | bytes 196616 | tf_op jit(solution)/shard_map/ppermute | solution.py:554
  32.4 3.8 %collective-permute-start.14 = (bf16[4,96,384]{2,1,0:T(8,128)(2,1)S(1)}, bf16[4,96,384]{2,1,0:T(8,128)(2,1)S(1)}, u32[]{:S(2)}, u32[]{:S(2)}) collective-permute-start(bf16[4,96,384]{2,1,0:T(8,128)(2,1)S(1)} %get-tuple-element.37), channel_id=1, source_target_pairs={{0,4},{4,0},{8,12},{12,8},{16,20},{20,16},{24,28},{28,24},{1,5},{5... | collective-permute-start | bytes 884744 | tf_op jit(solution)/shard_map/ppermute | solution.py:486
  33.4 6.5 %collective-permute-start.19 = (bf16[32,1024]{1,0:T(8,128)(2,1)S(1)}, bf16[32,1024]{1,0:T(8,128)(2,1)S(1)}, u32[]{:S(2)}, u32[]{:S(2)}) collective-permute-start(bf16[32,1024]{1,0:T(8,128)(2,1)S(1)} %add_convert_fusion.1), channel_id=1, source_target_pairs={{0,2},{1,3},{2,0},{3,1},{4,6},{5,7},{6,4},{7,5},{8,10},{9,11},{10,... | collective-permute-start | bytes 196616 | tf_op jit(solution)/shard_map/ppermute | solution.py:554
  36.3 7.9 %collective-permute-start.15 = (bf16[96,384]{1,0:T(8,128)(2,1)S(1)}, bf16[96,384]{1,0:T(8,128)(2,1)S(1)}, u32[]{:S(2)}, u32[]{:S(2)}) collective-permute-start(bf16[96,384]{1,0:T(8,128)(2,1)S(1)} %get-tuple-element.39), channel_id=1, source_target_pairs={{0,8},{4,12},{8,0},{12,4},{16,24},{20,28},{24,16},{28,20},{1,9},{5... | collective-permute-start | bytes 221192 | tf_op jit(solution)/shard_map/ppermute | solution.py:486
  37.8 6.4 %collective-permute-start.16 = (bf16[96,384]{1,0:T(8,128)(2,1)S(1)}, bf16[96,384]{1,0:T(8,128)(2,1)S(1)}, u32[]{:S(2)}, u32[]{:S(2)}) collective-permute-start(bf16[96,384]{1,0:T(8,128)(2,1)S(1)} %get-tuple-element.40), channel_id=1, source_target_pairs={{0,16},{4,20},{8,24},{12,28},{16,0},{20,4},{24,8},{28,12},{1,17},{... | collective-permute-start | bytes 221192 | tf_op jit(solution)/shard_map/ppermute | solution.py:486
  39.3 5.3 %collective-permute-start.17 = (bf16[96,384]{1,0:T(8,128)(2,1)S(1)}, bf16[96,384]{1,0:T(8,128)(2,1)S(1)}, u32[]{:S(2)}, u32[]{:S(2)}) collective-permute-start(bf16[96,384]{1,0:T(8,128)(2,1)S(1)} %get-tuple-element.41), channel_id=1, source_target_pairs={{0,24},{4,28},{8,16},{12,20},{16,8},{20,12},{24,0},{28,4},{1,25},{... | collective-permute-start | bytes 221192 | tf_op jit(solution)/shard_map/ppermute | solution.py:486
  39.8 4.3 %collective-permute-start.20 = (bf16[32,1024]{1,0:T(8,128)(2,1)S(1)}, bf16[32,1024]{1,0:T(8,128)(2,1)S(1)}, u32[]{:S(2)}, u32[]{:S(2)}) collective-permute-start(bf16[32,1024]{1,0:T(8,128)(2,1)S(1)} %add_convert_fusion.rest_4_), channel_id=1, source_target_pairs={{0,1},{1,0},{2,3},{3,2},{4,5},{5,4},{6,7},{7,6},{8,9},{9,8},{10,11... | collective-permute-start | bytes 196616 | tf_op jit(solution)/shard_map/ppermute | solution.py:554

commit v4 on v3

--- a/solution.py
+++ b/solution.py
@@ -295,28 +295,37 @@
         sides_ref[side] = jnp.broadcast_to(mask, (MAXV, 128))
 
 
-def forward_kernel(counts_hbm, offsets_hbm, *rest):
-    blocks = rest[:8]
-    packed, weights_ref, attended_ref, counts_ref, offsets_ref, sems, scalar_sems = rest[8:]
+def tables_kernel(counts_hbm, offsets_hbm, bias_ref, *rest):
+    outs, (blank, counts_ref, offsets_ref, sems, scalar_sems) = rest[:3], rest[3:]
     scalars = scalar_copies((counts_hbm, offsets_hbm), (counts_ref, offsets_ref), scalar_sems)
+    blank[...] = jnp.zeros_like(blank)
+    copies = [
+        pltpu.make_async_copy(blank, out.at[0, pl.ds(MAXV, blank.shape[0])], sems.at[index])
+        for index, out in enumerate(outs)
+    ]
+    for copy in copies:
+        copy.start()
     device = lax.axis_index("seq")
-    core = device % 2
-    copies = []
-    for index in range(8):
-        rows = pl.ds(index * MAXV, MAXV)
-        copies.append(pltpu.make_async_copy(blocks[index], packed.at[rows], sems.at[index]))
-        copies[-1].start()
-    lanes = head_lanes(core)
     for copy in scalars:
         copy.wait()
-    dead = []
+    slot = lax.broadcasted_iota(jnp.int32, (MAXV, 128), 0)
     for index in range(8):
-        begin, end_start = span_of(counts_ref, offsets_ref, device ^ index)
-        slot = lax.broadcasted_iota(jnp.int32, (MAXV, 256), 0)
-        dead.append((slot >= begin) & (slot < end_start))
-    dead = jnp.concatenate(dead, axis=0)
+        owner = device ^ (ROUTES[index // 2] + index % 2)
+        begin, end_start = span_of(counts_ref, offsets_ref, owner)
+        dead = (slot >= begin) & (slot < end_start)
+        bias_ref[index * MAXV : (index + 1) * MAXV, :] = jnp.where(dead, -1e30, 0.0)
     for copy in copies:
         copy.wait()
+
+
+def forward_kernel(bias_ref, *rest):
+    blocks = rest[:8]
+    packed, weights_ref, attended_ref = rest[8:]
+    lanes = head_lanes(lax.axis_index("seq") % 2)
+    for index in range(8):
+        packed[index * MAXV : (index + 1) * MAXV, :] = blocks[index][...]
+    bias = bias_ref[...]
+    bias = jnp.concatenate([bias, bias], axis=1)
     factor = HD ** (-0.5)
     key = packed[:, 128:256] * lanes
     value_t = packed[:, 256:384].T
@@ -328,7 +337,7 @@
             )
             * factor
         )
-        scores = jnp.where(dead, -1e30, scores)
+        scores = scores + bias
         scores = jnp.exp(scores - jnp.max(scores, axis=0, keepdims=True))
         weights = scores * (1.0 / jnp.sum(scores, axis=0, keepdims=True))
         weights_ref[:, rows] = weights
@@ -427,28 +436,18 @@
 
 
 def unpack_kernel(scale, sides_ref, *rest):
-    blocks, shares, outs, wg_ref = rest[:4], rest[4:6], rest[6:9], rest[9]
-    edges, blank, sems = rest[10:]
+    blocks, shares, outs, wg_hbm = rest[:4], rest[4:6], rest[9:12], rest[12]
+    edges, wg_ref, sems = rest[13:]
     device = lax.axis_index("seq")
-    frames = outs[0].shape[1]
-    last = frames - MAXV
-    blank[...] = jnp.zeros_like(blank)
+    last = outs[0].shape[1] - MAXV
     copies = []
     for index in range(3):
-        copies.append(
-            pltpu.make_async_copy(
-                blank, outs[index].at[0, pl.ds(MAXV, last - MAXV)], sems.at[index]
-            )
-        )
-        copies[-1].start()
-    for route, block in zip(ROUTES, blocks):
-        chip = (device ^ route) // 2
-        lanes = pl.ds(pl.multiple_of(chip * 128, 128), 128)
-        for index in range(3):
+        for route, block in zip(ROUTES, blocks):
+            chip = (device ^ route) // 2
+            lanes = pl.ds(pl.multiple_of(chip * 128, 128), 128)
             piece = block[:, index * 128 : (index + 1) * 128]
             for side in range(2):
                 edges[index, side, :, lanes] = piece * sides_ref[side]
-    for index in range(3):
         for side, start in enumerate((0, last)):
             copies.append(
                 pltpu.make_async_copy(
@@ -463,6 +462,8 @@
     half = mine.shape[0]
     wg_ref[:half, :] = jnp.where(lower, mine, other)
     wg_ref[half:, :] = jnp.where(lower, other, mine)
+    copies.append(pltpu.make_async_copy(wg_ref, wg_hbm, sems.at[len(copies)]))
+    copies[-1].start()
     for copy in copies:
         copy.wait()
 
@@ -523,6 +524,20 @@
     odd_cot = [shift(block, 1) for block in even_cot]
     blocks = [block for pair in zip(even, odd) for block in pair]
     cots = [block for pair in zip(even_cot, odd_cot) for block in pair]
+    full = jax.ShapeDtypeStruct(queries.shape, bf16)
+    bias, *blanks = seen(
+        tables_kernel,
+        [pltpu.VMEM((rows, 128), jnp.float32)] + [full] * 3,
+        [ANYWHERE] * 2,
+        (counts, offsets),
+        [
+            pltpu.VMEM((queries.shape[1] - 2 * MAXV, queries.shape[2]), bf16),
+            *tables,
+            pltpu.SemaphoreType.DMA((3,)),
+            pair_sems,
+        ],
+        [LOCAL] + [ANYWHERE] * 3,
+    )
     packed, weights, attended = seen(
         forward_kernel,
         [
@@ -530,9 +545,8 @@
             pltpu.VMEM((rows, rows), jnp.float32),
             pltpu.VMEM((128, rows), bf16),
         ],
-        [ANYWHERE] * 2 + [LOCAL] * 8,
-        (counts, offsets, *blocks),
-        [*tables, pltpu.SemaphoreType.DMA((8,)), pair_sems],
+        [LOCAL] * 9,
+        (bias, *blocks),
     )
     begun, begun_wg = seen(
         early_kernel,
@@ -571,22 +585,22 @@
     crossed = shift(leaving, 1)
     joined = seen(combine_kernel, [narrow] * 4, [LOCAL] * 2, (kept, crossed))
     home = [joined[0]] + [shift(joined[i], ROUTES[i]) for i in (1, 2, 3)]
-    frames = queries.shape[1]
     scale = (clips * VIS_DEV * pairs) ** (-0.5)
     return tuple(
-        seen(
+        pl.pallas_call(
             functools.partial(unpack_kernel, scale),
-            [jax.ShapeDtypeStruct(queries.shape, bf16)] * 3
-            + [jax.ShapeDtypeStruct(out_weight.shape, jnp.float32)],
-            [LOCAL] * 7,
-            (sides, *home, *shares),
-            [
+            out_shape=[full] * 3 + [jax.ShapeDtypeStruct(out_weight.shape, jnp.float32)],
+            in_specs=[LOCAL] * 7 + [ANYWHERE] * 3,
+            out_specs=[ANYWHERE] * 4,
+            scratch_shapes=[
                 pltpu.VMEM((3, 2, MAXV, queries.shape[2]), bf16),
-                pltpu.VMEM((frames - 2 * MAXV, queries.shape[2]), bf16),
-                pltpu.SemaphoreType.DMA((9,)),
+                pltpu.VMEM(out_weight.shape, jnp.float32),
+                pltpu.SemaphoreType.DMA((7,)),
             ],
-            [ANYWHERE] * 3 + [LOCAL],
-        )
+            input_output_aliases={7: 0, 8: 1, 9: 2},
+            compiler_params=PARAMS,
+            name="unpack",
+        )(sides, *home, *shares, *blanks)
     )
 
 

time: 46.7 us -> 44.8 us (0.959)
  waiting for transfers between devices: 14.6 us -> 13.6 us
  Pallas kernels: 9.07 us -> 8.22 us
    pallas_call x7, Pallas kernels: 9.07 us -> 7.19 us  [seen(): pl.pallas_call(kernel, out_shape=outs, in_specs=specs, out_specs=out_spec...]
    pallas_call x0 -> x1, Pallas kernels: none -> 1.03 us  [by_heads(): pl.pallas_call(functools.partial(unpack_kernel, scale), out_shape=[full]...]
    ppermute x18, waiting for transfers between devices: 11 us -> 10 us  [shift(): return lax.ppermute(block, 'seq', [(i, i ^ step) for i in range(pairs)])]
  transfers between devices with their start and end apart: 21 -> 21, of which waited for: 7 -> 6; matrix products, arithmetic and copies ran while one was open for 0% -> 0% of each run, Pallas kernels for 12% -> 12%
where the time goes in v4:
time: 44.8 us; the launch traced here: 44.7 us
  starting transfers between devices  22 us (49%)
  waiting for transfers between devices  13.6 us (30%)
  Pallas kernels  8.22 us (18%)
  between operations  0.76 us (2%)
    ppermute x18, starting transfers between devices, shift(): return lax.ppermute(block, 'seq', [(i, i ^ step) for i in range(pairs)])  15.7 us
    ppermute x18, waiting for transfers between devices, shift(): return lax.ppermute(block, 'seq', [(i, i ^ step) for i in range(pairs)])  10 us
    pallas_call x7, Pallas kernels, seen(): pl.pallas_call(kernel, out_shape=outs, in_specs=specs, out_specs=out_spec...  7.19 us
    ppermute x3, starting transfers between devices, across(): return lax.ppermute(block, 'clip', [(i, i ^ step) for i in range(clips)])  6.36 us
    ppermute x3, waiting for transfers between devices, across(): return lax.ppermute(block, 'clip', [(i, i ^ step) for i in range(clips)])  3.6 us
    pallas_call x1, Pallas kernels, by_heads(): pl.pallas_call(functools.partial(unpack_kernel, scale), out_shape=[full]...  1.03 us
  transfers between devices with their start and end apart: 21, of which 6 were waited for; matrix products, arithmetic and copies ran while one was open for 0% of the time, Pallas kernels for 12%

profile of v4, /device:TPU:0, one launch (start us, length us, event | category | flops | bytes accessed | tf_op | source)
XLA Modules:
  0.0 44.7 jit_solution(6594956990255997695)
XLA Ops:
  0.6 0.0 copy-start
  0.6 1.4 %shard_map.102 = (bf16[96,384]{1,0:T(8,128)(2,1)S(1)}, bf16[96,384]{1,0:T(8,128)(2,1)S(1)}, bf16[96,384]{1,0:T(8,128)(2,1)S(1)}, bf16[96,384]{1,0:T(8,128)(2,1)S...) custom-call(s32[1,8]{1,0:T(1,128)} %counts_hbm.3, s32[1,8]{1,0:T(1,128)} %offsets_hbm.3, ...), custom_call_target="tpu_custom_call" | custom-call | tf_op jit(solution)/shard_map/pallas_call | solution.py:493
  2.1 3.0 %collective-permute-start.8 = (bf16[96,1024]{1,0:T(8,128)(2,1)S(1)}, bf16[96,1024]{1,0:T(8,128)(2,1)S(1)}, u32[]{:S(2)}, u32[]{:S(2)}) collective-permute-start(bf16[96,1024]{1,0:T(8,128)(2,1)S(1)} %get-tuple-element.37.rest_0_), channel_id=1, source_target_pairs={{0,8},{4,12},{8,0},{12,4},{16,24},{20,28},{24,16},{28,20},{1,9},{5... | collective-permute-start | bytes 589832 | tf_op jit(solution)/shard_map/ppermute | solution.py:487
  5.1 1.5 %collective-permute-start.10 = (bf16[96,1024]{1,0:T(8,128)(2,1)S(1)}, bf16[96,1024]{1,0:T(8,128)(2,1)S(1)}, u32[]{:S(2)}, u32[]{:S(2)}) collective-permute-start(bf16[96,1024]{1,0:T(8,128)(2,1)S(1)} %get-tuple-element.37.rest_0_), channel_id=1, source_target_pairs={{0,16},{4,20},{8,24},{12,28},{16,0},{20,4},{24,8},{28,12},{1,17},{... | collective-permute-start | bytes 589832 | tf_op jit(solution)/shard_map/ppermute | solution.py:487
  6.6 0.0 collective-permute-start.12
  6.6 0.0 collective-permute-start
  6.6 1.9 %collective-permute-start.1 = (bf16[96,384]{1,0:T(8,128)(2,1)S(1)}, bf16[96,384]{1,0:T(8,128)(2,1)S(1)}, u32[]{:S(2)}, u32[]{:S(2)}) collective-permute-start(bf16[96,384]{1,0:T(8,128)(2,1)S(1)} %get-tuple-element.31), channel_id=1, source_target_pairs={{0,8},{4,12},{8,0},{12,4},{16,24},{20,28},{24,16},{28,20},{1,9},{5... | collective-permute-start | bytes 221192 | tf_op jit(solution)/shard_map/ppermute | solution.py:487
  8.6 0.0 collective-permute-done.rest_1_
  8.6 1.5 %collective-permute-start.3 = (bf16[96,384]{1,0:T(8,128)(2,1)S(1)}, bf16[96,384]{1,0:T(8,128)(2,1)S(1)}, u32[]{:S(2)}, u32[]{:S(2)}) collective-permute-start(bf16[96,384]{1,0:T(8,128)(2,1)S(1)} %get-tuple-element.32), channel_id=1, source_target_pairs={{0,16},{4,20},{8,24},{12,28},{16,0},{20,4},{24,8},{28,12},{1,17},{... | collective-permute-start | bytes 221192 | tf_op jit(solution)/shard_map/ppermute | solution.py:487
  10.1 5.7 %collective-permute-done.1.rest_2_ = bf16[96,384]{1,0:T(8,128)(2,1)S(1)} collective-permute-done((bf16[96,384]{1,0:T(8,128)(2,1)S(1)}, bf16[96,384]{1,0:T(8,128)(2,1)S(1)}, u32[]{:S(2)}, u32[]{:S(2)}) %collective-permute-start.1) | collective-permute-done | bytes 73760 | tf_op jit(solution)/shard_map/ppermute | solution.py:487
  15.8 2.7 %collective-permute-start.5 = (bf16[96,384]{1,0:T(8,128)(2,1)S(1)}, bf16[96,384]{1,0:T(8,128)(2,1)S(1)}, u32[]{:S(2)}, u32[]{:S(2)}) collective-permute-start(bf16[96,384]{1,0:T(8,128)(2,1)S(1)} %get-tuple-element.33), channel_id=1, source_target_pairs={{0,24},{4,28},{8,16},{12,20},{16,8},{20,12},{24,0},{28,4},{1,25},{... | collective-permute-start | bytes 221192 | tf_op jit(solution)/shard_map/ppermute | solution.py:487
  18.5 0.0 collective-permute-done.3.rest_4_
  18.5 0.0 collective-permute-start.2
  18.5 2.6 %collective-permute-done.5.rest_6_ = bf16[96,384]{1,0:T(8,128)(2,1)S(1)} collective-permute-done((bf16[96,384]{1,0:T(8,128)(2,1)S(1)}, bf16[96,384]{1,0:T(8,128)(2,1)S(1)}, u32[]{:S(2)}, u32[]{:S(2)}) %collective-permute-start.5) | collective-permute-done | bytes 73760 | tf_op jit(solution)/shard_map/ppermute | solution.py:487
  21.1 0.0 collective-permute-start.7
  21.1 0.0 collective-permute-done.8.rest_2_
  21.1 0.5 %collective-permute-start.9 = (bf16[96,1024]{1,0:T(8,128)(2,1)S(1)}, bf16[96,1024]{1,0:T(8,128)(2,1)S(1)}, u32[]{:S(2)}, u32[]{:S(2)}) collective-permute-start(bf16[96,1024]{1,0:T(8,128)(2,1)S(1)} %collective-permute-done.8.rest_2_), channel_id=1, source_target_pairs={{0,4},{4,0},{8,12},{12,8},{16,20},{20,16},{24,28},{28,24},{1,5},{5... | collective-permute-start | bytes 589832 | tf_op jit(solution)/shard_map/ppermute | solution.py:487
  21.6 0.0 collective-permute-done.10.rest_4_
  21.6 0.1 collective-permute-start.11
  21.7 0.0 collective-permute-done.12.rest_0_
  21.7 0.4 collective-permute-start.13
  22.1 0.0 collective-permute-done.2.rest_3_
  22.1 0.1 collective-permute-start.4
  22.2 1.3 %collective-permute-done.4.rest_5_ = bf16[96,384]{1,0:T(8,128)(2,1)S(1)} collective-permute-done((bf16[96,384]{1,0:T(8,128)(2,1)S(1)}, bf16[96,384]{1,0:T(8,128)(2,1)S(1)}, u32[]{:S(2)}, u32[]{:S(2)}) %collective-permute-start.4) | collective-permute-done | bytes 73760 | tf_op jit(solution)/shard_map/ppermute | solution.py:487
  23.5 0.2 collective-permute-start.6
  23.7 1.0 %shard_map.103 = (f32[768,128]{1,0:T(8,128)S(1)}, bf16[1,512,512]{2,1,0:T(8,128)(2,1)}, bf16[1,512,512]{2,1,0:T(8,128)(2,1)}, bf16[1,512,512]{2,1,0:T(8,128)(2,1)}) custom-call(s32[1,8]{1,0:T(1,128)} %counts_hbm.3, s32[1,8]{1,0:T(1,128)} %offsets_hbm.3), custom_call_target="tpu_custom_call" | custom-call | tf_op jit(solution)/shard_map/pallas_call | solution.py:493
  24.7 0.0 collective-permute-done.6.rest_7_
  24.8 2.2 %shard_map.104 = (bf16[768,384]{1,0:T(8,128)(2,1)S(1)}, f32[768,768]{1,0:T(8,128)S(1)}, bf16[128,768]{1,0:T(8,128)(2,1)S(1)}) custom-call(f32[768,128]{1,0:T(8,128)S(1)} %get-tuple-element.29.bias_ref, bf16[96,384]{1,0:T(8,128)(2,1)S(1)} %get-tuple-element.30.rest_0_, bf16[96,384]{1,0:T(8,128)(2,1)S(1)} %collective-permute-done.rest_1_, ...), custom_call_target="tpu_custom_call" | custom-call | tf_op jit(solution)/shard_map/pallas_call | solution.py:493
  26.9 0.0 collective-permute-done.7.rest_1_
  26.9 0.0 collective-permute-done.9.rest_3_
  26.9 0.0 collective-permute-done.11.rest_5_
  27.0 0.0 copy-done
  27.0 0.7 %shard_map.105 = (bf16[576,128]{1,0:T(8,128)(2,1)S(1)}, f32[64,1024]{1,0:T(8,128)S(1)}) custom-call(bf16[128,768]{1,0:T(8,128)(2,1)S(1)} %get-tuple-element.36.attended_ref, bf16[64,1024]{1,0:T(8,128)(2,1)S(1)} %copy-done, bf16[96,1024]{1,0:T(8,128)(2,1)S(1)} %get-tuple-element.37.rest_0_, bf16[96,1024]{1,0:T(8,128)(2,1)S(1)} %collective-permute-done.7.rest_1_, ...), custom_call_target="tpu_custom_call" | custom-call | tf_op jit(solution)/shard_map/pallas_call | solution.py:493
  27.7 0.0 collective-permute-done.13.rest_1_
  27.7 0.3 shard_map.106
  28.0 1.9 %collective-permute-start.18 = (bf16[32,1024]{1,0:T(8,128)(2,1)S(1)}, bf16[32,1024]{1,0:T(8,128)(2,1)S(1)}, u32[]{:S(2)}, u32[]{:S(2)}) collective-permute-start(bf16[32,1024]{1,0:T(8,128)(2,1)S(1)} %get-tuple-element.48), channel_id=1, source_target_pairs={{0,1},{1,0},{2,3},{3,2},{4,5},{5,4},{6,7},{7,6},{8,9},{9,8},{10,11... | collective-permute-start | bytes 196616 | tf_op jit(solution)/shard_map/ppermute | solution.py:568
  29.9 1.5 %shard_map.107 = (bf16[4,96,384]{2,1,0:T(8,128)(2,1)S(1)}, bf16[4,96,384]{2,1,0:T(8,128)(2,1)S(1)}) custom-call(bf16[768,384]{1,0:T(8,128)(2,1)S(1)} %get-tuple-element.34.packed, f32[768,768]{1,0:T(8,128)S(1)} %get-tuple-element.35.weights_ref, bf16[128,768]{1,0:T(8,128)(2,1)S(1)} %get-tuple-element.36.attended_ref, ...), custom_call_target="tpu_custom_call" | custom-call | tf_op jit(solution)/shard_map/pallas_call | solution.py:493
  31.5 0.1 collective-permute-start.14
  31.5 0.9 %collective-permute-done.18 = bf16[32,1024]{1,0:T(8,128)(2,1)S(1)} collective-permute-done((bf16[32,1024]{1,0:T(8,128)(2,1)S(1)}, bf16[32,1024]{1,0:T(8,128)(2,1)S(1)}, u32[]{:S(2)}, u32[]{:S(2)}) %collective-permute-start.18) | collective-permute-done | bytes 65568 | tf_op jit(solution)/shard_map/ppermute | solution.py:568
  32.5 2.8 %collective-permute-start.19 = (bf16[32,1024]{1,0:T(8,128)(2,1)S(1)}, bf16[32,1024]{1,0:T(8,128)(2,1)S(1)}, u32[]{:S(2)}, u32[]{:S(2)}) collective-permute-start(bf16[32,1024]{1,0:T(8,128)(2,1)S(1)} %add_convert_fusion.1), channel_id=1, source_target_pairs={{0,2},{1,3},{2,0},{3,1},{4,6},{5,7},{6,4},{7,5},{8,10},{9,11},{10,... | collective-permute-start | bytes 196616 | tf_op jit(solution)/shard_map/ppermute | solution.py:568
  35.3 0.0 collective-permute-done.14.crossed
  35.3 1.6 %collective-permute-start.15 = (bf16[96,384]{1,0:T(8,128)(2,1)S(1)}, bf16[96,384]{1,0:T(8,128)(2,1)S(1)}, u32[]{:S(2)}, u32[]{:S(2)}) collective-permute-start(bf16[96,384]{1,0:T(8,128)(2,1)S(1)} %get-tuple-element.44), channel_id=1, source_target_pairs={{0,8},{4,12},{8,0},{12,4},{16,24},{20,28},{24,16},{28,20},{1,9},{5... | collective-permute-start | bytes 221192 | tf_op jit(solution)/shard_map/ppermute | solution.py:487
  36.9 1.5 %collective-permute-start.16 = (bf16[96,384]{1,0:T(8,128)(2,1)S(1)}, bf16[96,384]{1,0:T(8,128)(2,1)S(1)}, u32[]{:S(2)}, u32[]{:S(2)}) collective-permute-start(bf16[96,384]{1,0:T(8,128)(2,1)S(1)} %get-tuple-element.45), channel_id=1, source_target_pairs={{0,16},{4,20},{8,24},{12,28},{16,0},{20,4},{24,8},{28,12},{1,17},{... | collective-permute-start | bytes 221192 | tf_op jit(solution)/shard_map/ppermute | solution.py:487
  38.4 0.5 %collective-permute-start.17 = (bf16[96,384]{1,0:T(8,128)(2,1)S(1)}, bf16[96,384]{1,0:T(8,128)(2,1)S(1)}, u32[]{:S(2)}, u32[]{:S(2)}) collective-permute-start(bf16[96,384]{1,0:T(8,128)(2,1)S(1)} %get-tuple-element.46), channel_id=1, source_target_pairs={{0,24},{4,28},{8,16},{12,20},{16,8},{20,12},{24,0},{28,4},{1,25},{... | collective-permute-start | bytes 221192 | tf_op jit(solution)/shard_map/ppermute | solution.py:487
  38.9 0.0 collective-permute-done.19
  38.9 1.6 %collective-permute-start.20 = (bf16[32,1024]{1,0:T(8,128)(2,1)S(1)}, bf16[32,1024]{1,0:T(8,128)(2,1)S(1)}, u32[]{:S(2)}, u32[]{:S(2)}) collective-permute-start(bf16[32,1024]{1,0:T(8,128)(2,1)S(1)} %add_convert_fusion.rest_4_), channel_id=1, source_target_pairs={{0,1},{1,0},{2,3},{3,2},{4,5},{5,4},{6,7},{7,6},{8,9},{9,8},{10,11... | collective-permute-start | bytes 196616 | tf_op jit(solution)/shard_map/ppermute | solution.py:568
  40.6 2.7 %collective-permute-done.20.rest_5_ = bf16[32,1024]{1,0:T(8,128)(2,1)S(1)} collective-permute-done((bf16[32,1024]{1,0:T(8,128)(2,1)S(1)}, bf16[32,1024]{1,0:T(8,128)(2,1)S(1)}, u32[]{:S(2)}, u32[]{:S(2)}) %collective-permute-start.20) | collective-permute-done | bytes 65568 | tf_op jit(solution)/shard_map/ppermute | solution.py:568
  43.2 0.0 collective-permute-done.15.rest_1_
  43.2 0.0 collective-permute-done.16.rest_2_
  43.2 0.4 collective-permute-done.17.rest_3_
  43.7 1.0 %unpack.1 = (bf16[1,512,512]{2,1,0:T(8,128)(2,1)}, bf16[1,512,512]{2,1,0:T(8,128)(2,1)}, bf16[1,512,512]{2,1,0:T(8,128)(2,1)}, f32[64,1024]{1,0:T(8,128)}) custom-call(bf16[2,96,128]{2,1,0:T(8,128)(2,1)S(1)} %get-tuple-element.28.sides_ref, ...), custom_call_target="tpu_custom_call", output_to_operand_aliasing={{0}: (7, {}), {1}: (8, {}), {2}: (9, {})} | custom-call | tf_op jit(solution)/shard_map/unpack/pallas_call | solution.py:590
  (3 shorter events, 0.1 us)
Async XLA Ops:
  0.6 26.3 %copy-start = (bf16[64,1024]{1,0:T(8,128)(2,1)S(1)}, bf16[64,1024]{1,0:T(8,128)(2,1)}, u32[]{:S(2)}) copy-start(bf16[64,1024]{1,0:T(8,128)(2,1)} %w_ref.3) | copy-start | bytes 393220
  2.1 19.0 %collective-permute-start.8 = (bf16[96,1024]{1,0:T(8,128)(2,1)S(1)}, bf16[96,1024]{1,0:T(8,128)(2,1)S(1)}, u32[]{:S(2)}, u32[]{:S(2)}) collective-permute-start(bf16[96,1024]{1,0:T(8,128)(2,1)S(1)} %get-tuple-element.37.rest_0_), channel_id=1, source_target_pairs={{0,8},{4,12},{8,0},{12,4},{16,24},{20,28},{24,16},{28,20},{1,9},{5... | collective-permute-start | bytes 589832 | tf_op jit(solution)/shard_map/ppermute | solution.py:487
  5.1 16.5 %collective-permute-start.10 = (bf16[96,1024]{1,0:T(8,128)(2,1)S(1)}, bf16[96,1024]{1,0:T(8,128)(2,1)S(1)}, u32[]{:S(2)}, u32[]{:S(2)}) collective-permute-start(bf16[96,1024]{1,0:T(8,128)(2,1)S(1)} %get-tuple-element.37.rest_0_), channel_id=1, source_target_pairs={{0,16},{4,20},{8,24},{12,28},{16,0},{20,4},{24,8},{28,12},{1,17},{... | collective-permute-start | bytes 589832 | tf_op jit(solution)/shard_map/ppermute | solution.py:487
  6.6 15.1 %collective-permute-start.12 = (bf16[96,1024]{1,0:T(8,128)(2,1)S(1)}, bf16[96,1024]{1,0:T(8,128)(2,1)S(1)}, u32[]{:S(2)}, u32[]{:S(2)}) collective-permute-start(bf16[96,1024]{1,0:T(8,128)(2,1)S(1)} %get-tuple-element.37.rest_0_), channel_id=1, source_target_pairs={{0,24},{4,28},{8,16},{12,20},{16,8},{20,12},{24,0},{28,4},{1,25},{... | collective-permute-start | bytes 589832 | tf_op jit(solution)/shard_map/ppermute | solution.py:487
  6.6 2.0 %collective-permute-start = (bf16[96,384]{1,0:T(8,128)(2,1)S(1)}, bf16[96,384]{1,0:T(8,128)(2,1)S(1)}, u32[]{:S(2)}, u32[]{:S(2)}) collective-permute-start(bf16[96,384]{1,0:T(8,128)(2,1)S(1)} %get-tuple-element.30.rest_0_), channel_id=1, source_target_pairs={{0,4},{4,0},{8,12},{12,8},{16,20},{20,16},{24,28},{28,24},{1,5},{5... | collective-permute-start | bytes 221192 | tf_op jit(solution)/shard_map/ppermute | solution.py:487
  6.6 9.2 %collective-permute-start.1 = (bf16[96,384]{1,0:T(8,128)(2,1)S(1)}, bf16[96,384]{1,0:T(8,128)(2,1)S(1)}, u32[]{:S(2)}, u32[]{:S(2)}) collective-permute-start(bf16[96,384]{1,0:T(8,128)(2,1)S(1)} %get-tuple-element.31), channel_id=1, source_target_pairs={{0,8},{4,12},{8,0},{12,4},{16,24},{20,28},{24,16},{28,20},{1,9},{5... | collective-permute-start | bytes 221192 | tf_op jit(solution)/shard_map/ppermute | solution.py:487
  8.6 9.9 %collective-permute-start.3 = (bf16[96,384]{1,0:T(8,128)(2,1)S(1)}, bf16[96,384]{1,0:T(8,128)(2,1)S(1)}, u32[]{:S(2)}, u32[]{:S(2)}) collective-permute-start(bf16[96,384]{1,0:T(8,128)(2,1)S(1)} %get-tuple-element.32), channel_id=1, source_target_pairs={{0,16},{4,20},{8,24},{12,28},{16,0},{20,4},{24,8},{28,12},{1,17},{... | collective-permute-start | bytes 221192 | tf_op jit(solution)/shard_map/ppermute | solution.py:487
  15.8 5.3 %collective-permute-start.5 = (bf16[96,384]{1,0:T(8,128)(2,1)S(1)}, bf16[96,384]{1,0:T(8,128)(2,1)S(1)}, u32[]{:S(2)}, u32[]{:S(2)}) collective-permute-start(bf16[96,384]{1,0:T(8,128)(2,1)S(1)} %get-tuple-element.33), channel_id=1, source_target_pairs={{0,24},{4,28},{8,16},{12,20},{16,8},{20,12},{24,0},{28,4},{1,25},{... | collective-permute-start | bytes 221192 | tf_op jit(solution)/shard_map/ppermute | solution.py:487
  18.5 3.6 %collective-permute-start.2 = (bf16[96,384]{1,0:T(8,128)(2,1)S(1)}, bf16[96,384]{1,0:T(8,128)(2,1)S(1)}, u32[]{:S(2)}, u32[]{:S(2)}) collective-permute-start(bf16[96,384]{1,0:T(8,128)(2,1)S(1)} %collective-permute-done.1.rest_2_), channel_id=1, source_target_pairs={{0,4},{4,0},{8,12},{12,8},{16,20},{20,16},{24,28},{28,24},{1,5},{5... | collective-permute-start | bytes 221192 | tf_op jit(solution)/shard_map/ppermute | solution.py:487
  21.1 5.8 %collective-permute-start.7 = (bf16[96,1024]{1,0:T(8,128)(2,1)S(1)}, bf16[96,1024]{1,0:T(8,128)(2,1)S(1)}, u32[]{:S(2)}, u32[]{:S(2)}) collective-permute-start(bf16[96,1024]{1,0:T(8,128)(2,1)S(1)} %get-tuple-element.37.rest_0_), channel_id=1, source_target_pairs={{0,4},{4,0},{8,12},{12,8},{16,20},{20,16},{24,28},{28,24},{1,5},{5... | collective-permute-start | bytes 589832 | tf_op jit(solution)/shard_map/ppermute | solution.py:487
  21.1 5.8 %collective-permute-start.9 = (bf16[96,1024]{1,0:T(8,128)(2,1)S(1)}, bf16[96,1024]{1,0:T(8,128)(2,1)S(1)}, u32[]{:S(2)}, u32[]{:S(2)}) collective-permute-start(bf16[96,1024]{1,0:T(8,128)(2,1)S(1)} %collective-permute-done.8.rest_2_), channel_id=1, source_target_pairs={{0,4},{4,0},{8,12},{12,8},{16,20},{20,16},{24,28},{28,24},{1,5},{5... | collective-permute-start | bytes 589832 | tf_op jit(solution)/shard_map/ppermute | solution.py:487
  21.6 5.3 %collective-permute-start.11 = (bf16[96,1024]{1,0:T(8,128)(2,1)S(1)}, bf16[96,1024]{1,0:T(8,128)(2,1)S(1)}, u32[]{:S(2)}, u32[]{:S(2)}) collective-permute-start(bf16[96,1024]{1,0:T(8,128)(2,1)S(1)} %collective-permute-done.10.rest_4_), channel_id=1, source_target_pairs={{0,4},{4,0},{8,12},{12,8},{16,20},{20,16},{24,28},{28,24},{1,5},{5... | collective-permute-start | bytes 589832 | tf_op jit(solution)/shard_map/ppermute | solution.py:487
  21.7 6.0 %collective-permute-start.13 = (bf16[96,1024]{1,0:T(8,128)(2,1)S(1)}, bf16[96,1024]{1,0:T(8,128)(2,1)S(1)}, u32[]{:S(2)}, u32[]{:S(2)}) collective-permute-start(bf16[96,1024]{1,0:T(8,128)(2,1)S(1)} %collective-permute-done.12.rest_0_), channel_id=1, source_target_pairs={{0,4},{4,0},{8,12},{12,8},{16,20},{20,16},{24,28},{28,24},{1,5},{5... | collective-permute-start | bytes 589832 | tf_op jit(solution)/shard_map/ppermute | solution.py:487
  22.1 1.4 %collective-permute-start.4 = (bf16[96,384]{1,0:T(8,128)(2,1)S(1)}, bf16[96,384]{1,0:T(8,128)(2,1)S(1)}, u32[]{:S(2)}, u32[]{:S(2)}) collective-permute-start(bf16[96,384]{1,0:T(8,128)(2,1)S(1)} %collective-permute-done.3.rest_4_), channel_id=1, source_target_pairs={{0,4},{4,0},{8,12},{12,8},{16,20},{20,16},{24,28},{28,24},{1,5},{5... | collective-permute-start | bytes 221192 | tf_op jit(solution)/shard_map/ppermute | solution.py:487
  23.5 1.3 %collective-permute-start.6 = (bf16[96,384]{1,0:T(8,128)(2,1)S(1)}, bf16[96,384]{1,0:T(8,128)(2,1)S(1)}, u32[]{:S(2)}, u32[]{:S(2)}) collective-permute-start(bf16[96,384]{1,0:T(8,128)(2,1)S(1)} %collective-permute-done.5.rest_6_), channel_id=1, source_target_pairs={{0,4},{4,0},{8,12},{12,8},{16,20},{20,16},{24,28},{28,24},{1,5},{5... | collective-permute-start | bytes 221192 | tf_op jit(solution)/shard_map/ppermute | solution.py:487
  28.0 4.4 %collective-permute-start.18 = (bf16[32,1024]{1,0:T(8,128)(2,1)S(1)}, bf16[32,1024]{1,0:T(8,128)(2,1)S(1)}, u32[]{:S(2)}, u32[]{:S(2)}) collective-permute-start(bf16[32,1024]{1,0:T(8,128)(2,1)S(1)} %get-tuple-element.48), channel_id=1, source_target_pairs={{0,1},{1,0},{2,3},{3,2},{4,5},{5,4},{6,7},{7,6},{8,9},{9,8},{10,11... | collective-permute-start | bytes 196616 | tf_op jit(solution)/shard_map/ppermute | solution.py:568
  31.5 3.8 %collective-permute-start.14 = (bf16[4,96,384]{2,1,0:T(8,128)(2,1)S(1)}, bf16[4,96,384]{2,1,0:T(8,128)(2,1)S(1)}, u32[]{:S(2)}, u32[]{:S(2)}) collective-permute-start(bf16[4,96,384]{2,1,0:T(8,128)(2,1)S(1)} %get-tuple-element.42), channel_id=1, source_target_pairs={{0,4},{4,0},{8,12},{12,8},{16,20},{20,16},{24,28},{28,24},{1,5},{5... | collective-permute-start | bytes 884744 | tf_op jit(solution)/shard_map/ppermute | solution.py:487
  32.5 6.4 %collective-permute-start.19 = (bf16[32,1024]{1,0:T(8,128)(2,1)S(1)}, bf16[32,1024]{1,0:T(8,128)(2,1)S(1)}, u32[]{:S(2)}, u32[]{:S(2)}) collective-permute-start(bf16[32,1024]{1,0:T(8,128)(2,1)S(1)} %add_convert_fusion.1), channel_id=1, source_target_pairs={{0,2},{1,3},{2,0},{3,1},{4,6},{5,7},{6,4},{7,5},{8,10},{9,11},{10,... | collective-permute-start | bytes 196616 | tf_op jit(solution)/shard_map/ppermute | solution.py:568
  35.3 7.9 %collective-permute-start.15 = (bf16[96,384]{1,0:T(8,128)(2,1)S(1)}, bf16[96,384]{1,0:T(8,128)(2,1)S(1)}, u32[]{:S(2)}, u32[]{:S(2)}) collective-permute-start(bf16[96,384]{1,0:T(8,128)(2,1)S(1)} %get-tuple-element.44), channel_id=1, source_target_pairs={{0,8},{4,12},{8,0},{12,4},{16,24},{20,28},{24,16},{28,20},{1,9},{5... | collective-permute-start | bytes 221192 | tf_op jit(solution)/shard_map/ppermute | solution.py:487
  36.9 6.4 %collective-permute-start.16 = (bf16[96,384]{1,0:T(8,128)(2,1)S(1)}, bf16[96,384]{1,0:T(8,128)(2,1)S(1)}, u32[]{:S(2)}, u32[]{:S(2)}) collective-permute-start(bf16[96,384]{1,0:T(8,128)(2,1)S(1)} %get-tuple-element.45), channel_id=1, source_target_pairs={{0,16},{4,20},{8,24},{12,28},{16,0},{20,4},{24,8},{28,12},{1,17},{... | collective-permute-start | bytes 221192 | tf_op jit(solution)/shard_map/ppermute | solution.py:487
  38.4 5.3 %collective-permute-start.17 = (bf16[96,384]{1,0:T(8,128)(2,1)S(1)}, bf16[96,384]{1,0:T(8,128)(2,1)S(1)}, u32[]{:S(2)}, u32[]{:S(2)}) collective-permute-start(bf16[96,384]{1,0:T(8,128)(2,1)S(1)} %get-tuple-element.46), channel_id=1, source_target_pairs={{0,24},{4,28},{8,16},{12,20},{16,8},{20,12},{24,0},{28,4},{1,25},{... | collective-permute-start | bytes 221192 | tf_op jit(solution)/shard_map/ppermute | solution.py:487
  38.9 4.3 %collective-permute-start.20 = (bf16[32,1024]{1,0:T(8,128)(2,1)S(1)}, bf16[32,1024]{1,0:T(8,128)(2,1)S(1)}, u32[]{:S(2)}, u32[]{:S(2)}) collective-permute-start(bf16[32,1024]{1,0:T(8,128)(2,1)S(1)} %add_convert_fusion.rest_4_), channel_id=1, source_target_pairs={{0,1},{1,0},{2,3},{3,2},{4,5},{5,4},{6,7},{7,6},{8,9},{9,8},{10,11... | collective-permute-start | bytes 196616 | tf_op jit(solution)/shard_map/ppermute | solution.py:568

commit v5 on v4

--- a/solution.py
+++ b/solution.py
@@ -221,7 +221,8 @@
     return (placed(returned[0]), placed(returned[1]), placed(returned[2]), weight_grad)
 
 
-ROUTES = (0, 2, 4, 6)
+ROUTES = (0, 6, 4, 2)
+EARLY = 4
 
 
 def head_lanes(core):
@@ -361,26 +362,27 @@
 
 
 def early_kernel(attended_ref, w_ref, *rest):
-    cots, dout_ref, wg_ref, cot = rest[:6], rest[6], rest[7], rest[8]
+    cots, dout_ref, wg_ref, cot = rest[:EARLY], rest[EARLY], rest[EARLY + 1], rest[EARLY + 2]
     core = lax.axis_index("seq") % 2
-    for index in range(6):
+    for index in range(EARLY):
         cot[index * MAXV : (index + 1) * MAXV, :] = cots[index][...]
     dout_ref[...] = project(cot, w_ref, core)
     wg_ref[...] = jnp.dot(
-        own_rows(attended_ref, core, slice(0, 6 * MAXV)),
+        own_rows(attended_ref, core, slice(0, EARLY * MAXV)),
         cot[...],
         preferred_element_type=jnp.float32,
     )
 
 
 def late_kernel(attended_ref, w_ref, begun_ref, *rest):
-    cots, dout_ref, kept_ref, sent_ref, cot = rest[:2], rest[2], rest[3], rest[4], rest[5]
+    cots = rest[: 8 - EARLY]
+    dout_ref, kept_ref, sent_ref, cot = rest[8 - EARLY :]
     core = lax.axis_index("seq") % 2
-    for index in range(2):
+    for index in range(8 - EARLY):
         cot[index * MAXV : (index + 1) * MAXV, :] = cots[index][...]
     dout_ref[...] = project(cot, w_ref, core)
     total = begun_ref[...] + jnp.dot(
-        own_rows(attended_ref, core, slice(6 * MAXV, 8 * MAXV)),
+        own_rows(attended_ref, core, slice(EARLY * MAXV, 8 * MAXV)),
         cot[...],
         preferred_element_type=jnp.float32,
     )
@@ -395,8 +397,8 @@
     dout, dq = rest[2:]
     core = lax.axis_index("seq") % 2
     lanes = head_lanes(core)
-    dout[: 6 * MAXV, :] = begun_ref[...]
-    dout[6 * MAXV :, :] = ended_ref[...]
+    dout[: EARLY * MAXV, :] = begun_ref[...]
+    dout[EARLY * MAXV :, :] = ended_ref[...]
     key_t = (packed[:, 128:256] * lanes).T
     value = packed[:, 256:384]
     factor = HD ** (-0.5)
@@ -550,18 +552,18 @@
     )
     begun, begun_wg = seen(
         early_kernel,
-        [pltpu.VMEM((6 * MAXV, 128), bf16), pltpu.VMEM(out_weight.shape, jnp.float32)],
-        [LOCAL] * 8,
-        (attended, out_weight, *cots[:6]),
-        [pltpu.VMEM((6 * MAXV, width), bf16)],
+        [pltpu.VMEM((EARLY * MAXV, 128), bf16), pltpu.VMEM(out_weight.shape, jnp.float32)],
+        [LOCAL] * (2 + EARLY),
+        (attended, out_weight, *cots[:EARLY]),
+        [pltpu.VMEM((EARLY * MAXV, width), bf16)],
     )
     share = jax.ShapeDtypeStruct((out_weight.shape[0] // 2, width), bf16)
     ended, mine, sent = seen(
         late_kernel,
-        [pltpu.VMEM((2 * MAXV, 128), bf16), share, share],
-        [LOCAL] * 5,
-        (attended, out_weight, begun_wg, *cots[6:]),
-        [pltpu.VMEM((2 * MAXV, width), bf16)],
+        [pltpu.VMEM(((8 - EARLY) * MAXV, 128), bf16), share, share],
+        [LOCAL] * (3 + 8 - EARLY),
+        (attended, out_weight, begun_wg, *cots[EARLY:]),
+        [pltpu.VMEM(((8 - EARLY) * MAXV, width), bf16)],
     )
 
     def across(block, step):

time: 44.8 us -> 44.5 us (level)
  starting transfers between devices: 22 us -> 20.9 us
  waiting for transfers between devices: 13.6 us -> 14.4 us
    ppermute x18, starting transfers between devices: 15.7 us -> 14.6 us  [shift(): return lax.ppermute(block, 'seq', [(i, i ^ step) for i in range(pairs)])]
    ppermute x18, waiting for transfers between devices: 10 us -> 10.8 us  [shift(): return lax.ppermute(block, 'seq', [(i, i ^ step) for i in range(pairs)])]
  transfers between devices with their start and end apart: 21 -> 21, of which waited for: 6 -> 5; matrix products, arithmetic and copies ran while one was open for 0% -> 0% of each run, Pallas kernels for 12% -> 12%
where the time goes in v5:
time: 44.5 us; the launch traced here: 44.4 us
  starting transfers between devices  20.9 us (47%)
  waiting for transfers between devices  14.4 us (32%)
  Pallas kernels  8.21 us (18%)
  between operations  0.76 us (2%)
    ppermute x18, starting transfers between devices, shift(): return lax.ppermute(block, 'seq', [(i, i ^ step) for i in range(pairs)])  14.6 us
    ppermute x18, waiting for transfers between devices, shift(): return lax.ppermute(block, 'seq', [(i, i ^ step) for i in range(pairs)])  10.8 us
    pallas_call x7, Pallas kernels, seen(): pl.pallas_call(kernel, out_shape=outs, in_specs=specs, out_specs=out_spec...  7.17 us
    ppermute x3, starting transfers between devices, across(): return lax.ppermute(block, 'clip', [(i, i ^ step) for i in range(clips)])  6.29 us
    ppermute x3, waiting for transfers between devices, across(): return lax.ppermute(block, 'clip', [(i, i ^ step) for i in range(clips)])  3.6 us
    pallas_call x1, Pallas kernels, by_heads(): pl.pallas_call(functools.partial(unpack_kernel, scale), out_shape=[full]...  1.04 us
  transfers between devices with their start and end apart: 21, of which 5 were waited for; matrix products, arithmetic and copies ran while one was open for 0% of the time, Pallas kernels for 12%

profile of v5, /device:TPU:0, one launch (start us, length us, event | category | flops | bytes accessed | tf_op | source)
XLA Modules:
  0.0 44.4 jit_solution(18400398107608725488)
XLA Ops:
  0.6 0.0 copy-start
  0.6 1.4 %shard_map.102 = (bf16[96,384]{1,0:T(8,128)(2,1)S(1)}, bf16[96,384]{1,0:T(8,128)(2,1)S(1)}, bf16[96,384]{1,0:T(8,128)(2,1)S(1)}, bf16[96,384]{1,0:T(8,128)(2,1)S...) custom-call(s32[1,8]{1,0:T(1,128)} %counts_hbm.3, s32[1,8]{1,0:T(1,128)} %offsets_hbm.3, ...), custom_call_target="tpu_custom_call" | custom-call | tf_op jit(solution)/shard_map/pallas_call | solution.py:495
  2.1 4.0 %collective-permute-start.8 = (bf16[96,1024]{1,0:T(8,128)(2,1)S(1)}, bf16[96,1024]{1,0:T(8,128)(2,1)S(1)}, u32[]{:S(2)}, u32[]{:S(2)}) collective-permute-start(bf16[96,1024]{1,0:T(8,128)(2,1)S(1)} %get-tuple-element.37.rest_0_), channel_id=1, source_target_pairs={{0,24},{4,28},{8,16},{12,20},{16,8},{20,12},{24,0},{28,4},{1,25},{... | collective-permute-start | bytes 589832 | tf_op jit(solution)/shard_map/ppermute | solution.py:489
  6.1 0.5 %collective-permute-start.10 = (bf16[96,1024]{1,0:T(8,128)(2,1)S(1)}, bf16[96,1024]{1,0:T(8,128)(2,1)S(1)}, u32[]{:S(2)}, u32[]{:S(2)}) collective-permute-start(bf16[96,1024]{1,0:T(8,128)(2,1)S(1)} %get-tuple-element.37.rest_0_), channel_id=1, source_target_pairs={{0,16},{4,20},{8,24},{12,28},{16,0},{20,4},{24,8},{28,12},{1,17},{... | collective-permute-start | bytes 589832 | tf_op jit(solution)/shard_map/ppermute | solution.py:489
  6.6 0.1 collective-permute-start.12
  6.7 0.0 collective-permute-start
  6.7 2.8 %collective-permute-start.1 = (bf16[96,384]{1,0:T(8,128)(2,1)S(1)}, bf16[96,384]{1,0:T(8,128)(2,1)S(1)}, u32[]{:S(2)}, u32[]{:S(2)}) collective-permute-start(bf16[96,384]{1,0:T(8,128)(2,1)S(1)} %get-tuple-element.31), channel_id=1, source_target_pairs={{0,24},{4,28},{8,16},{12,20},{16,8},{20,12},{24,0},{28,4},{1,25},{... | collective-permute-start | bytes 221192 | tf_op jit(solution)/shard_map/ppermute | solution.py:489
  9.6 0.0 collective-permute-done.rest_1_
  9.6 0.5 %collective-permute-start.3 = (bf16[96,384]{1,0:T(8,128)(2,1)S(1)}, bf16[96,384]{1,0:T(8,128)(2,1)S(1)}, u32[]{:S(2)}, u32[]{:S(2)}) collective-permute-start(bf16[96,384]{1,0:T(8,128)(2,1)S(1)} %get-tuple-element.32), channel_id=1, source_target_pairs={{0,16},{4,20},{8,24},{12,28},{16,0},{20,4},{24,8},{28,12},{1,17},{... | collective-permute-start | bytes 221192 | tf_op jit(solution)/shard_map/ppermute | solution.py:489
  10.1 6.8 %collective-permute-done.1.rest_2_ = bf16[96,384]{1,0:T(8,128)(2,1)S(1)} collective-permute-done((bf16[96,384]{1,0:T(8,128)(2,1)S(1)}, bf16[96,384]{1,0:T(8,128)(2,1)S(1)}, u32[]{:S(2)}, u32[]{:S(2)}) %collective-permute-start.1) | collective-permute-done | bytes 73760 | tf_op jit(solution)/shard_map/ppermute | solution.py:489
  16.9 1.7 %collective-permute-start.5 = (bf16[96,384]{1,0:T(8,128)(2,1)S(1)}, bf16[96,384]{1,0:T(8,128)(2,1)S(1)}, u32[]{:S(2)}, u32[]{:S(2)}) collective-permute-start(bf16[96,384]{1,0:T(8,128)(2,1)S(1)} %get-tuple-element.33), channel_id=1, source_target_pairs={{0,8},{4,12},{8,0},{12,4},{16,24},{20,28},{24,16},{28,20},{1,9},{5... | collective-permute-start | bytes 221192 | tf_op jit(solution)/shard_map/ppermute | solution.py:489
  18.6 0.0 collective-permute-done.3.rest_4_
  18.6 0.0 collective-permute-start.2
  18.6 2.7 %collective-permute-done.5.rest_6_ = bf16[96,384]{1,0:T(8,128)(2,1)S(1)} collective-permute-done((bf16[96,384]{1,0:T(8,128)(2,1)S(1)}, bf16[96,384]{1,0:T(8,128)(2,1)S(1)}, u32[]{:S(2)}, u32[]{:S(2)}) %collective-permute-start.5) | collective-permute-done | bytes 73760 | tf_op jit(solution)/shard_map/ppermute | solution.py:489
  21.2 0.0 collective-permute-start.7
  21.3 0.0 collective-permute-done.8.rest_2_
  21.3 0.5 %collective-permute-start.9 = (bf16[96,1024]{1,0:T(8,128)(2,1)S(1)}, bf16[96,1024]{1,0:T(8,128)(2,1)S(1)}, u32[]{:S(2)}, u32[]{:S(2)}) collective-permute-start(bf16[96,1024]{1,0:T(8,128)(2,1)S(1)} %collective-permute-done.8.rest_2_), channel_id=1, source_target_pairs={{0,4},{4,0},{8,12},{12,8},{16,20},{20,16},{24,28},{28,24},{1,5},{5... | collective-permute-start | bytes 589832 | tf_op jit(solution)/shard_map/ppermute | solution.py:489
  21.8 0.0 collective-permute-done.10.rest_0_
  21.8 0.1 collective-permute-start.11
  21.8 0.0 collective-permute-done.12.rest_2_
  21.8 0.4 collective-permute-start.13
  22.3 0.0 collective-permute-done.2.rest_3_
  22.3 0.1 collective-permute-start.4
  22.4 1.3 %collective-permute-done.4.rest_5_ = bf16[96,384]{1,0:T(8,128)(2,1)S(1)} collective-permute-done((bf16[96,384]{1,0:T(8,128)(2,1)S(1)}, bf16[96,384]{1,0:T(8,128)(2,1)S(1)}, u32[]{:S(2)}, u32[]{:S(2)}) %collective-permute-start.4) | collective-permute-done | bytes 73760 | tf_op jit(solution)/shard_map/ppermute | solution.py:489
  23.6 0.2 collective-permute-start.6
  23.9 1.0 %shard_map.103 = (f32[768,128]{1,0:T(8,128)S(1)}, bf16[1,512,512]{2,1,0:T(8,128)(2,1)}, bf16[1,512,512]{2,1,0:T(8,128)(2,1)}, bf16[1,512,512]{2,1,0:T(8,128)(2,1)}) custom-call(s32[1,8]{1,0:T(1,128)} %counts_hbm.3, s32[1,8]{1,0:T(1,128)} %offsets_hbm.3), custom_call_target="tpu_custom_call" | custom-call | tf_op jit(solution)/shard_map/pallas_call | solution.py:495
  24.9 0.0 collective-permute-done.6.rest_7_
  24.9 2.2 %shard_map.104 = (bf16[768,384]{1,0:T(8,128)(2,1)S(1)}, f32[768,768]{1,0:T(8,128)S(1)}, bf16[128,768]{1,0:T(8,128)(2,1)S(1)}) custom-call(f32[768,128]{1,0:T(8,128)S(1)} %get-tuple-element.29.bias_ref, bf16[96,384]{1,0:T(8,128)(2,1)S(1)} %get-tuple-element.30.rest_0_, bf16[96,384]{1,0:T(8,128)(2,1)S(1)} %collective-permute-done.rest_1_, ...), custom_call_target="tpu_custom_call" | custom-call | tf_op jit(solution)/shard_map/pallas_call | solution.py:495
  27.1 0.0 collective-permute-done.7.rest_1_
  27.1 0.0 collective-permute-done.9.rest_3_
  27.1 0.0 copy-done
  27.1 0.5 %shard_map.105 = (bf16[384,128]{1,0:T(8,128)(2,1)S(1)}, f32[64,1024]{1,0:T(8,128)S(1)}) custom-call(bf16[128,768]{1,0:T(8,128)(2,1)S(1)} %get-tuple-element.36.attended_ref, bf16[64,1024]{1,0:T(8,128)(2,1)S(1)} %copy-done, bf16[96,1024]{1,0:T(8,128)(2,1)S(1)} %get-tuple-element.37.rest_0_, bf16[96,1024]{1,0:T(8,128)(2,1)S(1)} %collective-permute-done.7.rest_1_, ...), custom_call_target="tpu_custom_call" | custom-call | tf_op jit(solution)/shard_map/pallas_call | solution.py:495
  27.6 0.0 collective-permute-done.11.rest_1_
  27.6 0.0 collective-permute-done.13.rest_3_
  27.6 0.5 %shard_map.106 = (bf16[384,128]{1,0:T(8,128)(2,1)S(1)}, bf16[32,1024]{1,0:T(8,128)(2,1)S(1)}, bf16[32,1024]{1,0:T(8,128)(2,1)S(1)}) custom-call(bf16[128,768]{1,0:T(8,128)(2,1)S(1)} %get-tuple-element.36.attended_ref, bf16[64,1024]{1,0:T(8,128)(2,1)S(1)} %copy-done, f32[64,1024]{1,0:T(8,128)S(1)} %get-tuple-element.39.begun_ref, ...), custom_call_target="tpu_custom_call" | custom-call | tf_op jit(solution)/shard_map/pallas_call | solution.py:495
  28.1 1.8 %collective-permute-start.18 = (bf16[32,1024]{1,0:T(8,128)(2,1)S(1)}, bf16[32,1024]{1,0:T(8,128)(2,1)S(1)}, u32[]{:S(2)}, u32[]{:S(2)}) collective-permute-start(bf16[32,1024]{1,0:T(8,128)(2,1)S(1)} %get-tuple-element.48), channel_id=1, source_target_pairs={{0,1},{1,0},{2,3},{3,2},{4,5},{5,4},{6,7},{7,6},{8,9},{9,8},{10,11... | collective-permute-start | bytes 196616 | tf_op jit(solution)/shard_map/ppermute | solution.py:570
  30.0 1.5 %shard_map.107 = (bf16[4,96,384]{2,1,0:T(8,128)(2,1)S(1)}, bf16[4,96,384]{2,1,0:T(8,128)(2,1)S(1)}) custom-call(bf16[768,384]{1,0:T(8,128)(2,1)S(1)} %get-tuple-element.34.packed, f32[768,768]{1,0:T(8,128)S(1)} %get-tuple-element.35.weights_ref, bf16[128,768]{1,0:T(8,128)(2,1)S(1)} %get-tuple-element.36.attended_ref, ...), custom_call_target="tpu_custom_call" | custom-call | tf_op jit(solution)/shard_map/pallas_call | solution.py:495
  31.5 0.1 collective-permute-start.14
  31.6 0.9 %collective-permute-done.18 = bf16[32,1024]{1,0:T(8,128)(2,1)S(1)} collective-permute-done((bf16[32,1024]{1,0:T(8,128)(2,1)S(1)}, bf16[32,1024]{1,0:T(8,128)(2,1)S(1)}, u32[]{:S(2)}, u32[]{:S(2)}) %collective-permute-start.18) | collective-permute-done | bytes 65568 | tf_op jit(solution)/shard_map/ppermute | solution.py:570
  32.5 2.8 %collective-permute-start.19 = (bf16[32,1024]{1,0:T(8,128)(2,1)S(1)}, bf16[32,1024]{1,0:T(8,128)(2,1)S(1)}, u32[]{:S(2)}, u32[]{:S(2)}) collective-permute-start(bf16[32,1024]{1,0:T(8,128)(2,1)S(1)} %add_convert_fusion.1), channel_id=1, source_target_pairs={{0,2},{1,3},{2,0},{3,1},{4,6},{5,7},{6,4},{7,5},{8,10},{9,11},{10,... | collective-permute-start | bytes 196616 | tf_op jit(solution)/shard_map/ppermute | solution.py:570
  35.3 0.0 collective-permute-done.14.crossed
  35.4 2.5 %collective-permute-start.15 = (bf16[96,384]{1,0:T(8,128)(2,1)S(1)}, bf16[96,384]{1,0:T(8,128)(2,1)S(1)}, u32[]{:S(2)}, u32[]{:S(2)}) collective-permute-start(bf16[96,384]{1,0:T(8,128)(2,1)S(1)} %get-tuple-element.44), channel_id=1, source_target_pairs={{0,24},{4,28},{8,16},{12,20},{16,8},{20,12},{24,0},{28,4},{1,25},{... | collective-permute-start | bytes 221192 | tf_op jit(solution)/shard_map/ppermute | solution.py:489
  37.9 0.5 %collective-permute-start.16 = (bf16[96,384]{1,0:T(8,128)(2,1)S(1)}, bf16[96,384]{1,0:T(8,128)(2,1)S(1)}, u32[]{:S(2)}, u32[]{:S(2)}) collective-permute-start(bf16[96,384]{1,0:T(8,128)(2,1)S(1)} %get-tuple-element.45), channel_id=1, source_target_pairs={{0,16},{4,20},{8,24},{12,28},{16,0},{20,4},{24,8},{28,12},{1,17},{... | collective-permute-start | bytes 221192 | tf_op jit(solution)/shard_map/ppermute | solution.py:489
  38.4 0.5 %collective-permute-start.17 = (bf16[96,384]{1,0:T(8,128)(2,1)S(1)}, bf16[96,384]{1,0:T(8,128)(2,1)S(1)}, u32[]{:S(2)}, u32[]{:S(2)}) collective-permute-start(bf16[96,384]{1,0:T(8,128)(2,1)S(1)} %get-tuple-element.46), channel_id=1, source_target_pairs={{0,8},{4,12},{8,0},{12,4},{16,24},{20,28},{24,16},{28,20},{1,9},{5... | collective-permute-start | bytes 221192 | tf_op jit(solution)/shard_map/ppermute | solution.py:489
  39.0 0.0 collective-permute-done.19
  39.0 1.6 %collective-permute-start.20 = (bf16[32,1024]{1,0:T(8,128)(2,1)S(1)}, bf16[32,1024]{1,0:T(8,128)(2,1)S(1)}, u32[]{:S(2)}, u32[]{:S(2)}) collective-permute-start(bf16[32,1024]{1,0:T(8,128)(2,1)S(1)} %add_convert_fusion.rest_4_), channel_id=1, source_target_pairs={{0,1},{1,0},{2,3},{3,2},{4,5},{5,4},{6,7},{7,6},{8,9},{9,8},{10,11... | collective-permute-start | bytes 196616 | tf_op jit(solution)/shard_map/ppermute | solution.py:570
  40.6 2.7 %collective-permute-done.20.rest_5_ = bf16[32,1024]{1,0:T(8,128)(2,1)S(1)} collective-permute-done((bf16[32,1024]{1,0:T(8,128)(2,1)S(1)}, bf16[32,1024]{1,0:T(8,128)(2,1)S(1)}, u32[]{:S(2)}, u32[]{:S(2)}) %collective-permute-start.20) | collective-permute-done | bytes 65568 | tf_op jit(solution)/shard_map/ppermute | solution.py:570
  43.3 0.0 collective-permute-done.15.rest_1_
  43.3 0.0 collective-permute-done.16.rest_2_
  43.3 0.0 collective-permute-done.17.rest_3_
  43.3 1.0 %unpack.1 = (bf16[1,512,512]{2,1,0:T(8,128)(2,1)}, bf16[1,512,512]{2,1,0:T(8,128)(2,1)}, bf16[1,512,512]{2,1,0:T(8,128)(2,1)}, f32[64,1024]{1,0:T(8,128)}) custom-call(bf16[2,96,128]{2,1,0:T(8,128)(2,1)S(1)} %get-tuple-element.28.sides_ref, ...), custom_call_target="tpu_custom_call", output_to_operand_aliasing={{0}: (7, {}), {1}: (8, {}), {2}: (9, {})} | custom-call | tf_op jit(solution)/shard_map/unpack/pallas_call | solution.py:592
  (3 shorter events, 0.1 us)
Async XLA Ops:
  0.6 26.5 %copy-start = (bf16[64,1024]{1,0:T(8,128)(2,1)S(1)}, bf16[64,1024]{1,0:T(8,128)(2,1)}, u32[]{:S(2)}) copy-start(bf16[64,1024]{1,0:T(8,128)(2,1)} %w_ref.3) | copy-start | bytes 393220
  2.1 19.2 %collective-permute-start.8 = (bf16[96,1024]{1,0:T(8,128)(2,1)S(1)}, bf16[96,1024]{1,0:T(8,128)(2,1)S(1)}, u32[]{:S(2)}, u32[]{:S(2)}) collective-permute-start(bf16[96,1024]{1,0:T(8,128)(2,1)S(1)} %get-tuple-element.37.rest_0_), channel_id=1, source_target_pairs={{0,24},{4,28},{8,16},{12,20},{16,8},{20,12},{24,0},{28,4},{1,25},{... | collective-permute-start | bytes 589832 | tf_op jit(solution)/shard_map/ppermute | solution.py:489
  6.1 15.7 %collective-permute-start.10 = (bf16[96,1024]{1,0:T(8,128)(2,1)S(1)}, bf16[96,1024]{1,0:T(8,128)(2,1)S(1)}, u32[]{:S(2)}, u32[]{:S(2)}) collective-permute-start(bf16[96,1024]{1,0:T(8,128)(2,1)S(1)} %get-tuple-element.37.rest_0_), channel_id=1, source_target_pairs={{0,16},{4,20},{8,24},{12,28},{16,0},{20,4},{24,8},{28,12},{1,17},{... | collective-permute-start | bytes 589832 | tf_op jit(solution)/shard_map/ppermute | solution.py:489
  6.6 15.3 %collective-permute-start.12 = (bf16[96,1024]{1,0:T(8,128)(2,1)S(1)}, bf16[96,1024]{1,0:T(8,128)(2,1)S(1)}, u32[]{:S(2)}, u32[]{:S(2)}) collective-permute-start(bf16[96,1024]{1,0:T(8,128)(2,1)S(1)} %get-tuple-element.37.rest_0_), channel_id=1, source_target_pairs={{0,8},{4,12},{8,0},{12,4},{16,24},{20,28},{24,16},{28,20},{1,9},{5... | collective-permute-start | bytes 589832 | tf_op jit(solution)/shard_map/ppermute | solution.py:489
  6.7 2.9 %collective-permute-start = (bf16[96,384]{1,0:T(8,128)(2,1)S(1)}, bf16[96,384]{1,0:T(8,128)(2,1)S(1)}, u32[]{:S(2)}, u32[]{:S(2)}) collective-permute-start(bf16[96,384]{1,0:T(8,128)(2,1)S(1)} %get-tuple-element.30.rest_0_), channel_id=1, source_target_pairs={{0,4},{4,0},{8,12},{12,8},{16,20},{20,16},{24,28},{28,24},{1,5},{5... | collective-permute-start | bytes 221192 | tf_op jit(solution)/shard_map/ppermute | solution.py:489
  6.7 10.2 %collective-permute-start.1 = (bf16[96,384]{1,0:T(8,128)(2,1)S(1)}, bf16[96,384]{1,0:T(8,128)(2,1)S(1)}, u32[]{:S(2)}, u32[]{:S(2)}) collective-permute-start(bf16[96,384]{1,0:T(8,128)(2,1)S(1)} %get-tuple-element.31), channel_id=1, source_target_pairs={{0,24},{4,28},{8,16},{12,20},{16,8},{20,12},{24,0},{28,4},{1,25},{... | collective-permute-start | bytes 221192 | tf_op jit(solution)/shard_map/ppermute | solution.py:489
  9.6 9.0 %collective-permute-start.3 = (bf16[96,384]{1,0:T(8,128)(2,1)S(1)}, bf16[96,384]{1,0:T(8,128)(2,1)S(1)}, u32[]{:S(2)}, u32[]{:S(2)}) collective-permute-start(bf16[96,384]{1,0:T(8,128)(2,1)S(1)} %get-tuple-element.32), channel_id=1, source_target_pairs={{0,16},{4,20},{8,24},{12,28},{16,0},{20,4},{24,8},{28,12},{1,17},{... | collective-permute-start | bytes 221192 | tf_op jit(solution)/shard_map/ppermute | solution.py:489
  16.9 4.4 %collective-permute-start.5 = (bf16[96,384]{1,0:T(8,128)(2,1)S(1)}, bf16[96,384]{1,0:T(8,128)(2,1)S(1)}, u32[]{:S(2)}, u32[]{:S(2)}) collective-permute-start(bf16[96,384]{1,0:T(8,128)(2,1)S(1)} %get-tuple-element.33), channel_id=1, source_target_pairs={{0,8},{4,12},{8,0},{12,4},{16,24},{20,28},{24,16},{28,20},{1,9},{5... | collective-permute-start | bytes 221192 | tf_op jit(solution)/shard_map/ppermute | solution.py:489
  18.6 3.7 %collective-permute-start.2 = (bf16[96,384]{1,0:T(8,128)(2,1)S(1)}, bf16[96,384]{1,0:T(8,128)(2,1)S(1)}, u32[]{:S(2)}, u32[]{:S(2)}) collective-permute-start(bf16[96,384]{1,0:T(8,128)(2,1)S(1)} %collective-permute-done.1.rest_2_), channel_id=1, source_target_pairs={{0,4},{4,0},{8,12},{12,8},{16,20},{20,16},{24,28},{28,24},{1,5},{5... | collective-permute-start | bytes 221192 | tf_op jit(solution)/shard_map/ppermute | solution.py:489
  21.2 5.8 %collective-permute-start.7 = (bf16[96,1024]{1,0:T(8,128)(2,1)S(1)}, bf16[96,1024]{1,0:T(8,128)(2,1)S(1)}, u32[]{:S(2)}, u32[]{:S(2)}) collective-permute-start(bf16[96,1024]{1,0:T(8,128)(2,1)S(1)} %get-tuple-element.37.rest_0_), channel_id=1, source_target_pairs={{0,4},{4,0},{8,12},{12,8},{16,20},{20,16},{24,28},{28,24},{1,5},{5... | collective-permute-start | bytes 589832 | tf_op jit(solution)/shard_map/ppermute | solution.py:489
  21.3 5.8 %collective-permute-start.9 = (bf16[96,1024]{1,0:T(8,128)(2,1)S(1)}, bf16[96,1024]{1,0:T(8,128)(2,1)S(1)}, u32[]{:S(2)}, u32[]{:S(2)}) collective-permute-start(bf16[96,1024]{1,0:T(8,128)(2,1)S(1)} %collective-permute-done.8.rest_2_), channel_id=1, source_target_pairs={{0,4},{4,0},{8,12},{12,8},{16,20},{20,16},{24,28},{28,24},{1,5},{5... | collective-permute-start | bytes 589832 | tf_op jit(solution)/shard_map/ppermute | solution.py:489
  21.8 5.9 %collective-permute-start.11 = (bf16[96,1024]{1,0:T(8,128)(2,1)S(1)}, bf16[96,1024]{1,0:T(8,128)(2,1)S(1)}, u32[]{:S(2)}, u32[]{:S(2)}) collective-permute-start(bf16[96,1024]{1,0:T(8,128)(2,1)S(1)} %collective-permute-done.10.rest_0_), channel_id=1, source_target_pairs={{0,4},{4,0},{8,12},{12,8},{16,20},{20,16},{24,28},{28,24},{1,5},{5... | collective-permute-start | bytes 589832 | tf_op jit(solution)/shard_map/ppermute | solution.py:489
  21.8 5.8 %collective-permute-start.13 = (bf16[96,1024]{1,0:T(8,128)(2,1)S(1)}, bf16[96,1024]{1,0:T(8,128)(2,1)S(1)}, u32[]{:S(2)}, u32[]{:S(2)}) collective-permute-start(bf16[96,1024]{1,0:T(8,128)(2,1)S(1)} %collective-permute-done.12.rest_2_), channel_id=1, source_target_pairs={{0,4},{4,0},{8,12},{12,8},{16,20},{20,16},{24,28},{28,24},{1,5},{5... | collective-permute-start | bytes 589832 | tf_op jit(solution)/shard_map/ppermute | solution.py:489
  22.3 1.4 %collective-permute-start.4 = (bf16[96,384]{1,0:T(8,128)(2,1)S(1)}, bf16[96,384]{1,0:T(8,128)(2,1)S(1)}, u32[]{:S(2)}, u32[]{:S(2)}) collective-permute-start(bf16[96,384]{1,0:T(8,128)(2,1)S(1)} %collective-permute-done.3.rest_4_), channel_id=1, source_target_pairs={{0,4},{4,0},{8,12},{12,8},{16,20},{20,16},{24,28},{28,24},{1,5},{5... | collective-permute-start | bytes 221192 | tf_op jit(solution)/shard_map/ppermute | solution.py:489
  23.6 1.3 %collective-permute-start.6 = (bf16[96,384]{1,0:T(8,128)(2,1)S(1)}, bf16[96,384]{1,0:T(8,128)(2,1)S(1)}, u32[]{:S(2)}, u32[]{:S(2)}) collective-permute-start(bf16[96,384]{1,0:T(8,128)(2,1)S(1)} %collective-permute-done.5.rest_6_), channel_id=1, source_target_pairs={{0,4},{4,0},{8,12},{12,8},{16,20},{20,16},{24,28},{28,24},{1,5},{5... | collective-permute-start | bytes 221192 | tf_op jit(solution)/shard_map/ppermute | solution.py:489
  28.1 4.4 %collective-permute-start.18 = (bf16[32,1024]{1,0:T(8,128)(2,1)S(1)}, bf16[32,1024]{1,0:T(8,128)(2,1)S(1)}, u32[]{:S(2)}, u32[]{:S(2)}) collective-permute-start(bf16[32,1024]{1,0:T(8,128)(2,1)S(1)} %get-tuple-element.48), channel_id=1, source_target_pairs={{0,1},{1,0},{2,3},{3,2},{4,5},{5,4},{6,7},{7,6},{8,9},{9,8},{10,11... | collective-permute-start | bytes 196616 | tf_op jit(solution)/shard_map/ppermute | solution.py:570
  31.5 3.8 %collective-permute-start.14 = (bf16[4,96,384]{2,1,0:T(8,128)(2,1)S(1)}, bf16[4,96,384]{2,1,0:T(8,128)(2,1)S(1)}, u32[]{:S(2)}, u32[]{:S(2)}) collective-permute-start(bf16[4,96,384]{2,1,0:T(8,128)(2,1)S(1)} %get-tuple-element.42), channel_id=1, source_target_pairs={{0,4},{4,0},{8,12},{12,8},{16,20},{20,16},{24,28},{28,24},{1,5},{5... | collective-permute-start | bytes 884744 | tf_op jit(solution)/shard_map/ppermute | solution.py:489
  32.5 6.4 %collective-permute-start.19 = (bf16[32,1024]{1,0:T(8,128)(2,1)S(1)}, bf16[32,1024]{1,0:T(8,128)(2,1)S(1)}, u32[]{:S(2)}, u32[]{:S(2)}) collective-permute-start(bf16[32,1024]{1,0:T(8,128)(2,1)S(1)} %add_convert_fusion.1), channel_id=1, source_target_pairs={{0,2},{1,3},{2,0},{3,1},{4,6},{5,7},{6,4},{7,5},{8,10},{9,11},{10,... | collective-permute-start | bytes 196616 | tf_op jit(solution)/shard_map/ppermute | solution.py:570
  35.4 7.9 %collective-permute-start.15 = (bf16[96,384]{1,0:T(8,128)(2,1)S(1)}, bf16[96,384]{1,0:T(8,128)(2,1)S(1)}, u32[]{:S(2)}, u32[]{:S(2)}) collective-permute-start(bf16[96,384]{1,0:T(8,128)(2,1)S(1)} %get-tuple-element.44), channel_id=1, source_target_pairs={{0,24},{4,28},{8,16},{12,20},{16,8},{20,12},{24,0},{28,4},{1,25},{... | collective-permute-start | bytes 221192 | tf_op jit(solution)/shard_map/ppermute | solution.py:489
  37.9 5.4 %collective-permute-start.16 = (bf16[96,384]{1,0:T(8,128)(2,1)S(1)}, bf16[96,384]{1,0:T(8,128)(2,1)S(1)}, u32[]{:S(2)}, u32[]{:S(2)}) collective-permute-start(bf16[96,384]{1,0:T(8,128)(2,1)S(1)} %get-tuple-element.45), channel_id=1, source_target_pairs={{0,16},{4,20},{8,24},{12,28},{16,0},{20,4},{24,8},{28,12},{1,17},{... | collective-permute-start | bytes 221192 | tf_op jit(solution)/shard_map/ppermute | solution.py:489
  38.4 4.9 %collective-permute-start.17 = (bf16[96,384]{1,0:T(8,128)(2,1)S(1)}, bf16[96,384]{1,0:T(8,128)(2,1)S(1)}, u32[]{:S(2)}, u32[]{:S(2)}) collective-permute-start(bf16[96,384]{1,0:T(8,128)(2,1)S(1)} %get-tuple-element.46), channel_id=1, source_target_pairs={{0,8},{4,12},{8,0},{12,4},{16,24},{20,28},{24,16},{28,20},{1,9},{5... | collective-permute-start | bytes 221192 | tf_op jit(solution)/shard_map/ppermute | solution.py:489
  39.0 4.3 %collective-permute-start.20 = (bf16[32,1024]{1,0:T(8,128)(2,1)S(1)}, bf16[32,1024]{1,0:T(8,128)(2,1)S(1)}, u32[]{:S(2)}, u32[]{:S(2)}) collective-permute-start(bf16[32,1024]{1,0:T(8,128)(2,1)S(1)} %add_convert_fusion.rest_4_), channel_id=1, source_target_pairs={{0,1},{1,0},{2,3},{3,2},{4,5},{5,4},{6,7},{7,6},{8,9},{9,8},{10,11... | collective-permute-start | bytes 196616 | tf_op jit(solution)/shard_map/ppermute | solution.py:570

commit v6 on v5

--- a/solution.py
+++ b/solution.py
@@ -222,7 +222,6 @@
 
 
 ROUTES = (0, 6, 4, 2)
-EARLY = 4
 
 
 def head_lanes(core):
@@ -321,98 +320,88 @@
 
 def forward_kernel(bias_ref, *rest):
     blocks = rest[:8]
-    packed, weights_ref, attended_ref = rest[8:]
-    lanes = head_lanes(lax.axis_index("seq") % 2)
+    shared, query, weights_ref, attended_ref = rest[8:]
     for index in range(8):
-        packed[index * MAXV : (index + 1) * MAXV, :] = blocks[index][...]
+        shared[index * MAXV : (index + 1) * MAXV, :] = blocks[index][:, 128:384]
+    for index in range(4):
+        query[index * MAXV : (index + 1) * MAXV, :] = blocks[2 * index][:, 0:128]
     bias = bias_ref[...]
-    bias = jnp.concatenate([bias, bias], axis=1)
+    bias = jnp.concatenate([bias, bias, bias], axis=1)
     factor = HD ** (-0.5)
-    key = packed[:, 128:256] * lanes
-    value_t = packed[:, 256:384].T
-    for step in range(3):
-        rows = slice(step * 256, (step + 1) * 256)
+    value_t = shared[:, 128:256].T
+    for head in range(2):
+        key = shared[:, 0:128] * head_lanes(head)
         scores = (
             lax.dot_general(
-                key, packed[rows, 0:128], (((1,), (1,)), ((), ())), preferred_element_type=jnp.float32
+                key, query[...], (((1,), (1,)), ((), ())), preferred_element_type=jnp.float32
             )
             * factor
         )
         scores = scores + bias
         scores = jnp.exp(scores - jnp.max(scores, axis=0, keepdims=True))
         weights = scores * (1.0 / jnp.sum(scores, axis=0, keepdims=True))
-        weights_ref[:, rows] = weights
-        attended_ref[:, rows] = jnp.dot(
+        weights_ref[head] = weights
+        own = slice(head * HD, (head + 1) * HD)
+        attended_ref[own, :] = jnp.dot(
             value_t, weights.astype(jnp.bfloat16), preferred_element_type=jnp.float32
-        ).astype(jnp.bfloat16)
-
-
-def own_rows(ref, core, columns):
-    both = ref[:, columns].astype(jnp.float32)
-    return jnp.where(core == 0, both[:HD], both[HD:]).astype(jnp.bfloat16)
-
-
-def project(cot, w_ref, core):
-    top = (core == 0).astype(jnp.float32).astype(jnp.bfloat16)
-    bottom = (core == 1).astype(jnp.float32).astype(jnp.bfloat16)
-    w_both = jnp.concatenate([w_ref[...] * top, w_ref[...] * bottom], axis=0)
+        )[own].astype(jnp.bfloat16)
+
+
+def gather_cots(cots, cot):
+    for index, block in enumerate(cots):
+        cot[index * MAXV : (index + 1) * MAXV, :] = block[...]
+
+
+def project(cot, w_ref, w_other_ref, core):
+    first = (core == 0).astype(jnp.float32).astype(jnp.bfloat16)
+    second = (core == 1).astype(jnp.float32).astype(jnp.bfloat16)
+    top = w_ref[...] * first + w_other_ref[...] * second
+    bottom = w_ref[...] * second + w_other_ref[...] * first
     return lax.dot_general(
-        cot[...], w_both, (((1,), (1,)), ((), ())), preferred_element_type=jnp.float32
+        cot[...],
+        jnp.concatenate([top, bottom], axis=0),
+        (((1,), (1,)), ((), ())),
+        preferred_element_type=jnp.float32,
     ).astype(jnp.bfloat16)
 
 
-def early_kernel(attended_ref, w_ref, *rest):
-    cots, dout_ref, wg_ref, cot = rest[:EARLY], rest[EARLY], rest[EARLY + 1], rest[EARLY + 2]
+def early_kernel(attended_ref, w_ref, w_other_ref, *rest):
+    cots, dout_ref, wg_ref, cot = rest[:2], rest[2], rest[3], rest[4]
+    gather_cots(cots, cot)
+    dout_ref[...] = project(cot, w_ref, w_other_ref, lax.axis_index("seq") % 2)
+    wg_ref[...] = jnp.dot(
+        attended_ref[:, : 2 * MAXV], cot[...], preferred_element_type=jnp.float32
+    )
+
+
+def late_kernel(attended_ref, w_ref, w_other_ref, begun_ref, *rest):
+    cots, dout_ref, own_ref, other_ref, cot = rest[:2], rest[2], rest[3], rest[4], rest[5]
     core = lax.axis_index("seq") % 2
-    for index in range(EARLY):
-        cot[index * MAXV : (index + 1) * MAXV, :] = cots[index][...]
-    dout_ref[...] = project(cot, w_ref, core)
-    wg_ref[...] = jnp.dot(
-        own_rows(attended_ref, core, slice(0, EARLY * MAXV)),
-        cot[...],
-        preferred_element_type=jnp.float32,
-    )
-
-
-def late_kernel(attended_ref, w_ref, begun_ref, *rest):
-    cots = rest[: 8 - EARLY]
-    dout_ref, kept_ref, sent_ref, cot = rest[8 - EARLY :]
-    core = lax.axis_index("seq") % 2
-    for index in range(8 - EARLY):
-        cot[index * MAXV : (index + 1) * MAXV, :] = cots[index][...]
-    dout_ref[...] = project(cot, w_ref, core)
+    gather_cots(cots, cot)
     total = begun_ref[...] + jnp.dot(
-        own_rows(attended_ref, core, slice(EARLY * MAXV, 8 * MAXV)),
-        cot[...],
-        preferred_element_type=jnp.float32,
-    )
-    half = total.shape[0] // 2
-    lower = lax.axis_index("clip") % 2 == 0
-    kept_ref[...] = jnp.where(lower, total[:half], total[half:]).astype(jnp.bfloat16)
-    sent_ref[...] = jnp.where(lower, total[half:], total[:half]).astype(jnp.bfloat16)
-
-
-def backward_kernel(packed, weights_ref, attended_ref, begun_ref, ended_ref, *rest):
-    outs = rest[:2]
-    dout, dq = rest[2:]
-    core = lax.axis_index("seq") % 2
-    lanes = head_lanes(core)
-    dout[: EARLY * MAXV, :] = begun_ref[...]
-    dout[EARLY * MAXV :, :] = ended_ref[...]
-    key_t = (packed[:, 128:256] * lanes).T
-    value = packed[:, 256:384]
+        attended_ref[:, 2 * MAXV :], cot[...], preferred_element_type=jnp.float32
+    )
+    own_ref[...] = jnp.where(core == 0, total[:HD], total[HD:])
+    other_ref[...] = jnp.where(core == 0, total[HD:], total[:HD]).astype(jnp.bfloat16)
+    dout_ref[...] = project(cot, w_ref, w_other_ref, core)
+
+
+def backward_kernel(shared, query, weights_ref, attended_ref, begun_ref, ended_ref, *rest):
+    kept_query, kept_shared, leaving, dout = rest
+    dout[: 2 * MAXV, :] = begun_ref[...]
+    dout[2 * MAXV :, :] = ended_ref[...]
     factor = HD ** (-0.5)
-    dout_t = dout[...].astype(jnp.float32).T
+    products = dout[...].astype(jnp.float32).T * attended_ref[...].astype(jnp.float32)
+    value = shared[:, 128:256]
     key_grad = jnp.zeros((8 * MAXV, 128), jnp.float32)
     value_grad = jnp.zeros((8 * MAXV, 128), jnp.float32)
-    for step in range(3):
-        rows = slice(step * 256, (step + 1) * 256)
-        query_own = packed[rows, 0:128] * lanes
-        dout_own = dout[rows, :]
-        weights = weights_ref[:, rows]
-        inner = jnp.sum(
-            dout_t[:, rows] * attended_ref[:, rows].astype(jnp.float32), axis=0, keepdims=True
-        )
+    query_grad = jnp.zeros((128, 4 * MAXV), jnp.float32)
+    for head in range(2):
+        lanes = head_lanes(head)
+        dout_own = dout[...] * lanes
+        key_t = (shared[:, 0:128] * lanes).T
+        inner = jnp.sum(products[head * HD : (head + 1) * HD], axis=0, keepdims=True)
+        weights = weights_ref[head]
         dweights = lax.dot_general(
             value, dout_own, (((1,), (1,)), ((), ())), preferred_element_type=jnp.float32
         )
@@ -420,21 +409,26 @@
         value_grad += jnp.dot(
             weights.astype(jnp.bfloat16), dout_own, preferred_element_type=jnp.float32
         )
-        key_grad += jnp.dot(dscores, query_own, preferred_element_type=jnp.float32)
-        dq_t = jnp.dot(key_t, dscores, preferred_element_type=jnp.float32) * factor
-        dq[rows, :] = dq_t.T.astype(jnp.bfloat16)
-    key_grad = (key_grad * factor).astype(jnp.bfloat16)
-    value_grad = value_grad.astype(jnp.bfloat16)
-    for index in range(8):
-        rows = slice(index * MAXV, (index + 1) * MAXV)
-        outs[index % 2][index // 2, :, 0:128] = dq[rows, :]
-        outs[index % 2][index // 2, :, 128:256] = key_grad[rows]
-        outs[index % 2][index // 2, :, 256:384] = value_grad[rows]
-
-
-def combine_kernel(kept, crossed, *outs):
+        key_grad += jnp.dot(dscores, query[...] * lanes, preferred_element_type=jnp.float32)
+        query_grad += jnp.dot(key_t, dscores, preferred_element_type=jnp.float32)
+    query_grad = (query_grad * factor).T.astype(jnp.bfloat16)
+    key_grad = key_grad * factor
     for index in range(4):
-        outs[index][...] = kept[index] + crossed[index]
+        kept_query[index] = query_grad[index * MAXV : (index + 1) * MAXV]
+        rows = slice(2 * index * MAXV, (2 * index + 1) * MAXV)
+        kept_shared[index, :, 0:128] = key_grad[rows]
+        kept_shared[index, :, 128:256] = value_grad[rows]
+        rows = slice((2 * index + 1) * MAXV, (2 * index + 2) * MAXV)
+        leaving[index, :, 0:128] = key_grad[rows].astype(jnp.bfloat16)
+        leaving[index, :, 128:256] = value_grad[rows].astype(jnp.bfloat16)
+
+
+def combine_kernel(kept_query, kept_shared, crossed, *outs):
+    for index in range(4):
+        outs[index][:, 0:128] = kept_query[index]
+        outs[index][:, 128:384] = (
+            kept_shared[index] + crossed[index].astype(jnp.float32)
+        ).astype(jnp.bfloat16)
 
 
 def unpack_kernel(scale, sides_ref, *rest):
@@ -459,11 +453,7 @@
                 )
             )
             copies[-1].start()
-    lower = lax.axis_index("clip") % 2 == 0
-    mine, other = [share[...].astype(jnp.float32) * scale for share in shares]
-    half = mine.shape[0]
-    wg_ref[:half, :] = jnp.where(lower, mine, other)
-    wg_ref[half:, :] = jnp.where(lower, other, mine)
+    wg_ref[...] = (shares[0][...].astype(jnp.float32) + shares[1][...].astype(jnp.float32)) * scale
     copies.append(pltpu.make_async_copy(wg_ref, wg_hbm, sems.at[len(copies)]))
     copies[-1].start()
     for copy in copies:
@@ -523,9 +513,8 @@
     even = [sends[0]] + [shift(sends[i], ROUTES[i]) for i in (1, 2, 3)]
     even_cot = [cot] + [shift(cot, ROUTES[i]) for i in (1, 2, 3)]
     odd = [shift(block, 1) for block in even]
-    odd_cot = [shift(block, 1) for block in even_cot]
+    w_other = shift(out_weight, 1)
     blocks = [block for pair in zip(even, odd) for block in pair]
-    cots = [block for pair in zip(even_cot, odd_cot) for block in pair]
     full = jax.ShapeDtypeStruct(queries.shape, bf16)
     bias, *blanks = seen(
         tables_kernel,
@@ -540,52 +529,64 @@
         ],
         [LOCAL] + [ANYWHERE] * 3,
     )
-    packed, weights, attended = seen(
+    own_rows = 4 * MAXV
+    shared, query, weights, attended = seen(
         forward_kernel,
         [
-            pltpu.VMEM((rows, 384), bf16),
-            pltpu.VMEM((rows, rows), jnp.float32),
-            pltpu.VMEM((128, rows), bf16),
+            pltpu.VMEM((rows, 256), bf16),
+            pltpu.VMEM((own_rows, 128), bf16),
+            pltpu.VMEM((2, rows, own_rows), jnp.float32),
+            pltpu.VMEM((128, own_rows), bf16),
         ],
         [LOCAL] * 9,
         (bias, *blocks),
     )
+    projected = pltpu.VMEM((2 * MAXV, 128), bf16)
+    gathered = [pltpu.VMEM((2 * MAXV, width), bf16)]
     begun, begun_wg = seen(
         early_kernel,
-        [pltpu.VMEM((EARLY * MAXV, 128), bf16), pltpu.VMEM(out_weight.shape, jnp.float32)],
-        [LOCAL] * (2 + EARLY),
-        (attended, out_weight, *cots[:EARLY]),
-        [pltpu.VMEM((EARLY * MAXV, width), bf16)],
-    )
-    share = jax.ShapeDtypeStruct((out_weight.shape[0] // 2, width), bf16)
-    ended, mine, sent = seen(
+        [projected, pltpu.VMEM((128, width), jnp.float32)],
+        [LOCAL] * 5,
+        (attended, out_weight, w_other, *even_cot[:2]),
+        gathered,
+    )
+    ended, wg_own, wg_other = seen(
         late_kernel,
-        [pltpu.VMEM(((8 - EARLY) * MAXV, 128), bf16), share, share],
-        [LOCAL] * (3 + 8 - EARLY),
-        (attended, out_weight, begun_wg, *cots[EARLY:]),
-        [pltpu.VMEM(((8 - EARLY) * MAXV, width), bf16)],
-    )
+        [
+            projected,
+            pltpu.VMEM(out_weight.shape, jnp.float32),
+            jax.ShapeDtypeStruct(out_weight.shape, bf16),
+        ],
+        [LOCAL] * 6,
+        (attended, out_weight, w_other, begun_wg, *even_cot[2:]),
+        gathered,
+    )
+    wg_crossed = shift(wg_other, 1)
+    mine = (wg_own + wg_crossed.astype(jnp.float32)).astype(bf16)
 
     def across(block, step):
         return lax.ppermute(block, "clip", [(i, i ^ step) for i in range(clips)])
 
-    other = across(sent, 1)
-    step = 1
+    other = across(mine, 1)
+    step = 3
     while step < clips:
         mine = (mine.astype(jnp.float32) + other.astype(jnp.float32)).astype(bf16)
-        step *= 2
-        if step < clips:
-            other = across(mine, step)
-    shares = [mine, across(mine, 1)]
-    kept, leaving = seen(
+        other = across(mine, step)
+        step = 2 * step + 1
+    shares = [mine, other]
+    kept_query, kept_shared, leaving = seen(
         backward_kernel,
-        [jax.ShapeDtypeStruct((4, MAXV, 384), bf16)] * 2,
-        [LOCAL] * 5,
-        (packed, weights, attended, begun, ended),
-        [pltpu.VMEM((rows, 128), bf16)] * 2,
+        [
+            jax.ShapeDtypeStruct((4, MAXV, 128), bf16),
+            jax.ShapeDtypeStruct((4, MAXV, 256), jnp.float32),
+            jax.ShapeDtypeStruct((4, MAXV, 256), bf16),
+        ],
+        [LOCAL] * 6,
+        (shared, query, weights, attended, begun, ended),
+        [pltpu.VMEM((own_rows, 128), bf16)],
     )
     crossed = shift(leaving, 1)
-    joined = seen(combine_kernel, [narrow] * 4, [LOCAL] * 2, (kept, crossed))
+    joined = seen(combine_kernel, [narrow] * 4, [LOCAL] * 3, (kept_query, kept_shared, crossed))
     home = [joined[0]] + [shift(joined[i], ROUTES[i]) for i in (1, 2, 3)]
     scale = (clips * VIS_DEV * pairs) ** (-0.5)
     return tuple(

time: 44.5 us -> 41.7 us (0.937)
  starting transfers between devices: 20.9 us -> 18 us
  waiting for transfers between devices: 14.4 us -> 15.5 us
  Pallas kernels: 8.21 us -> 7.25 us
    ppermute x18 -> x16, waiting for transfers between devices: 10.8 us -> 12.7 us  [shift(): return lax.ppermute(block, 'seq', [(i, i ^ step) for i in range(pairs)])]
    ppermute x18 -> x16, starting transfers between devices: 14.6 us -> 13.1 us  [shift(): return lax.ppermute(block, 'seq', [(i, i ^ step) for i in range(pairs)])]
    ppermute x3 -> x2, starting transfers between devices: 6.29 us -> 4.86 us  [across(): return lax.ppermute(block, 'clip', [(i, i ^ step) for i in range(clips)])]
    pallas_call x7, Pallas kernels: 7.17 us -> 6.22 us  [seen(): pl.pallas_call(kernel, out_shape=outs, in_specs=specs, out_specs=out_spec...]
    ppermute x3 -> x2, waiting for transfers between devices: 3.6 us -> 2.75 us  [across(): return lax.ppermute(block, 'clip', [(i, i ^ step) for i in range(clips)])]
  transfers between devices with their start and end apart: 21 -> 18, of which waited for: 5 -> 10; matrix products, arithmetic and copies ran while one was open for 0% -> 0% of each run, Pallas kernels for 12% -> 11%
where the time goes in v6:
time: 41.7 us; the launch traced here: 41.5 us
  starting transfers between devices  18 us (43%)
  waiting for transfers between devices  15.5 us (37%)
  Pallas kernels  7.25 us (17%)
  between operations  0.74 us (2%)
    ppermute x16, starting transfers between devices, shift(): return lax.ppermute(block, 'seq', [(i, i ^ step) for i in range(pairs)])  13.1 us
    ppermute x16, waiting for transfers between devices, shift(): return lax.ppermute(block, 'seq', [(i, i ^ step) for i in range(pairs)])  12.7 us
    pallas_call x7, Pallas kernels, seen(): pl.pallas_call(kernel, out_shape=outs, in_specs=specs, out_specs=out_spec...  6.22 us
    ppermute x2, starting transfers between devices, across(): return lax.ppermute(block, 'clip', [(i, i ^ step) for i in range(clips)])  4.86 us
    ppermute x2, waiting for transfers between devices, across(): return lax.ppermute(block, 'clip', [(i, i ^ step) for i in range(clips)])  2.75 us
    pallas_call x1, Pallas kernels, by_heads(): pl.pallas_call(functools.partial(unpack_kernel, scale), out_shape=[full]...  1.03 us
  transfers between devices with their start and end apart: 18, of which 10 were waited for; matrix products, arithmetic and copies ran while one was open for 0% of the time, Pallas kernels for 11%

profile of v6, /device:TPU:0, one launch (start us, length us, event | category | flops | bytes accessed | tf_op | source)
XLA Modules:
  0.0 41.5 jit_solution(10401871706926381263)
XLA Ops:
  0.6 0.0 copy-start
  0.6 1.4 %shard_map.102 = (bf16[96,384]{1,0:T(8,128)(2,1)S(1)}, bf16[96,384]{1,0:T(8,128)(2,1)S(1)}, bf16[96,384]{1,0:T(8,128)(2,1)S(1)}, bf16[96,384]{1,0:T(8,128)(2,1)S...) custom-call(s32[1,8]{1,0:T(1,128)} %counts_hbm.3, s32[1,8]{1,0:T(1,128)} %offsets_hbm.3, ...), custom_call_target="tpu_custom_call" | custom-call | tf_op jit(solution)/shard_map/pallas_call | solution.py:485
  2.1 4.0 %collective-permute-start.1 = (bf16[96,384]{1,0:T(8,128)(2,1)S(1)}, bf16[96,384]{1,0:T(8,128)(2,1)S(1)}, u32[]{:S(2)}, u32[]{:S(2)}) collective-permute-start(bf16[96,384]{1,0:T(8,128)(2,1)S(1)} %get-tuple-element.33), channel_id=1, source_target_pairs={{0,24},{4,28},{8,16},{12,20},{16,8},{20,12},{24,0},{28,4},{1,25},{... | collective-permute-start | bytes 221192 | tf_op jit(solution)/shard_map/ppermute | solution.py:479
  6.1 0.0 collective-permute-start
  6.1 0.5 %collective-permute-start.3 = (bf16[96,384]{1,0:T(8,128)(2,1)S(1)}, bf16[96,384]{1,0:T(8,128)(2,1)S(1)}, u32[]{:S(2)}, u32[]{:S(2)}) collective-permute-start(bf16[96,384]{1,0:T(8,128)(2,1)S(1)} %get-tuple-element.34), channel_id=1, source_target_pairs={{0,16},{4,20},{8,24},{12,28},{16,0},{20,4},{24,8},{28,12},{1,17},{... | collective-permute-start | bytes 221192 | tf_op jit(solution)/shard_map/ppermute | solution.py:479
  6.6 0.2 collective-permute-start.5
  6.8 1.9 %collective-permute-done.1.rest_2_ = bf16[96,384]{1,0:T(8,128)(2,1)S(1)} collective-permute-done((bf16[96,384]{1,0:T(8,128)(2,1)S(1)}, bf16[96,384]{1,0:T(8,128)(2,1)S(1)}, u32[]{:S(2)}, u32[]{:S(2)}) %collective-permute-start.1) | collective-permute-done | bytes 73760 | tf_op jit(solution)/shard_map/ppermute | solution.py:479
  8.6 0.0 collective-permute-start.2
  8.6 3.4 %collective-permute-start.8 = (bf16[96,1024]{1,0:T(8,128)(2,1)S(1)}, bf16[96,1024]{1,0:T(8,128)(2,1)S(1)}, u32[]{:S(2)}, u32[]{:S(2)}) collective-permute-start(bf16[96,1024]{1,0:T(8,128)(2,1)S(1)} %get-tuple-element.40.rest_0_), channel_id=1, source_target_pairs={{0,24},{4,28},{8,16},{12,20},{16,8},{20,12},{24,0},{28,4},{1,25},{... | collective-permute-start | bytes 589832 | tf_op jit(solution)/shard_map/ppermute | solution.py:479
  12.0 0.0 collective-permute-done.rest_1_
  12.0 0.0 collective-permute-start.9
  12.0 0.0 collective-permute-done.3.rest_4_
  12.0 0.6 %collective-permute-start.10 = (bf16[96,1024]{1,0:T(8,128)(2,1)S(1)}, bf16[96,1024]{1,0:T(8,128)(2,1)S(1)}, u32[]{:S(2)}, u32[]{:S(2)}) collective-permute-start(bf16[96,1024]{1,0:T(8,128)(2,1)S(1)} %get-tuple-element.40.rest_0_), channel_id=1, source_target_pairs={{0,8},{4,12},{8,0},{12,4},{16,24},{20,28},{24,16},{28,20},{1,9},{5... | collective-permute-start | bytes 589832 | tf_op jit(solution)/shard_map/ppermute | solution.py:479
  12.7 0.0 collective-permute-done.5.rest_6_
  12.7 0.0 collective-permute-start.4
  12.7 0.0 collective-permute-done.2.rest_3_
  12.7 0.0 copy-done
  12.7 0.5 %collective-permute-start.7 = (bf16[64,1024]{1,0:T(8,128)(2,1)S(1)}, bf16[64,1024]{1,0:T(8,128)(2,1)S(1)}, u32[]{:S(2)}, u32[]{:S(2)}) collective-permute-start(bf16[64,1024]{1,0:T(8,128)(2,1)S(1)} %copy-done), channel_id=1, source_target_pairs={{0,4},{4,0},{8,12},{12,8},{16,20},{20,16},{24,28},{28,24},{1,5},{5... | collective-permute-start | bytes 393224 | tf_op jit(solution)/shard_map/ppermute | solution.py:479
  13.2 0.7 %collective-permute-done.4.rest_5_ = bf16[96,384]{1,0:T(8,128)(2,1)S(1)} collective-permute-done((bf16[96,384]{1,0:T(8,128)(2,1)S(1)}, bf16[96,384]{1,0:T(8,128)(2,1)S(1)}, u32[]{:S(2)}, u32[]{:S(2)}) %collective-permute-start.4) | collective-permute-done | bytes 73760 | tf_op jit(solution)/shard_map/ppermute | solution.py:479
  13.9 0.2 collective-permute-start.6
  14.1 1.0 %shard_map.103 = (f32[768,128]{1,0:T(8,128)S(1)}, bf16[1,512,512]{2,1,0:T(8,128)(2,1)}, bf16[1,512,512]{2,1,0:T(8,128)(2,1)}, bf16[1,512,512]{2,1,0:T(8,128)(2,1)}) custom-call(s32[1,8]{1,0:T(1,128)} %counts_hbm.3, s32[1,8]{1,0:T(1,128)} %offsets_hbm.3), custom_call_target="tpu_custom_call" | custom-call | tf_op jit(solution)/shard_map/pallas_call | solution.py:485
  15.1 0.1 collective-permute-done.6.rest_7_
  15.2 1.6 %shard_map.104 = (bf16[768,256]{1,0:T(8,128)(2,1)S(1)}, bf16[384,128]{1,0:T(8,128)(2,1)S(1)}, f32[2,768,384]{2,1,0:T(8,128)S(1)}, bf16[128,384]{1,0:T(8,128)(2,1)S(1)}) custom-call(f32[768,128]{1,0:T(8,128)S(1)} %get-tuple-element.31.bias_ref, bf16[96,384]{1,0:T(8,128)(2,1)S(1)} %get-tuple-element.32.rest_0_, ...), custom_call_target="tpu_custom_call" | custom-call | tf_op jit(solution)/shard_map/pallas_call | solution.py:485
  16.8 0.0 collective-permute-done.7.w_other_ref
  16.9 1.0 %collective-permute-done.8.rest_1_ = bf16[96,1024]{1,0:T(8,128)(2,1)S(1)} collective-permute-done((bf16[96,1024]{1,0:T(8,128)(2,1)S(1)}, bf16[96,1024]{1,0:T(8,128)(2,1)S(1)}, u32[]{:S(2)}, u32[]{:S(2)}) %collective-permute-start.8) | collective-permute-done | bytes 196640 | tf_op jit(solution)/shard_map/ppermute | solution.py:479
  17.8 0.4 shard_map.105
  18.2 3.6 %collective-permute-done.9.rest_0_ = bf16[96,1024]{1,0:T(8,128)(2,1)S(1)} collective-permute-done((bf16[96,1024]{1,0:T(8,128)(2,1)S(1)}, bf16[96,1024]{1,0:T(8,128)(2,1)S(1)}, u32[]{:S(2)}, u32[]{:S(2)}) %collective-permute-start.9) | collective-permute-done | bytes 196640 | tf_op jit(solution)/shard_map/ppermute | solution.py:479
  21.8 0.0 collective-permute-done.10.rest_1_
  21.8 0.4 shard_map.106
  22.2 0.1 collective-permute-start.15
  22.3 1.3 %collective-permute-done.15 = bf16[64,1024]{1,0:T(8,128)(2,1)S(1)} collective-permute-done((bf16[64,1024]{1,0:T(8,128)(2,1)S(1)}, bf16[64,1024]{1,0:T(8,128)(2,1)S(1)}, u32[]{:S(2)}, u32[]{:S(2)}) %collective-permute-start.15) | collective-permute-done | bytes 131104 | tf_op jit(solution)/shard_map/ppermute | solution.py:479
  23.6 1.4 %collective-permute-start.16 = (bf16[64,1024]{1,0:T(8,128)(2,1)S(1)}, bf16[64,1024]{1,0:T(8,128)(2,1)S(1)}, u32[]{:S(2)}, u32[]{:S(2)}) collective-permute-start(bf16[64,1024]{1,0:T(8,128)(2,1)S(1)} %add_convert_fusion.1), channel_id=1, source_target_pairs={{0,1},{1,0},{2,3},{3,2},{4,5},{5,4},{6,7},{7,6},{8,9},{9,8},{10,11... | collective-permute-start | bytes 393224 | tf_op jit(solution)/shard_map/ppermute | solution.py:568
  25.1 1.4 %shard_map.107 = (bf16[4,96,128]{2,1,0:T(8,128)(2,1)S(1)}, f32[4,96,256]{2,1,0:T(8,128)S(1)}, bf16[4,96,256]{2,1,0:T(8,128)(2,1)S(1)}) custom-call(bf16[768,256]{1,0:T(8,128)(2,1)S(1)} %get-tuple-element.36.shared, bf16[384,128]{1,0:T(8,128)(2,1)S(1)} %get-tuple-element.37.query, f32[2,768,384]{2,1,0:T(8,128)S(1)} %get-tuple-element.38.weights_ref, ...), custom_call_target="tpu_custom_call" | custom-call | tf_op jit(solution)/shard_map/pallas_call | solution.py:485
  26.4 0.1 collective-permute-start.11
  26.5 2.7 %collective-permute-done.16 = bf16[64,1024]{1,0:T(8,128)(2,1)S(1)} collective-permute-done((bf16[64,1024]{1,0:T(8,128)(2,1)S(1)}, bf16[64,1024]{1,0:T(8,128)(2,1)S(1)}, u32[]{:S(2)}, u32[]{:S(2)}) %collective-permute-start.16) | collective-permute-done | bytes 131104 | tf_op jit(solution)/shard_map/ppermute | solution.py:568
  29.3 3.4 %collective-permute-start.17 = (bf16[64,1024]{1,0:T(8,128)(2,1)S(1)}, bf16[64,1024]{1,0:T(8,128)(2,1)S(1)}, u32[]{:S(2)}, u32[]{:S(2)}) collective-permute-start(bf16[64,1024]{1,0:T(8,128)(2,1)S(1)} %add_convert_fusion.rest_4_), channel_id=1, source_target_pairs={{0,3},{1,2},{2,1},{3,0},{4,7},{5,6},{6,5},{7,4},{8,11},{9,10},{10,... | collective-permute-start | bytes 393224 | tf_op jit(solution)/shard_map/ppermute | solution.py:568
  32.7 0.0 collective-permute-done.11.crossed
  32.8 1.8 %collective-permute-start.12 = (bf16[96,384]{1,0:T(8,128)(2,1)S(1)}, bf16[96,384]{1,0:T(8,128)(2,1)S(1)}, u32[]{:S(2)}, u32[]{:S(2)}) collective-permute-start(bf16[96,384]{1,0:T(8,128)(2,1)S(1)} %get-tuple-element.48), channel_id=1, source_target_pairs={{0,24},{4,28},{8,16},{12,20},{16,8},{20,12},{24,0},{28,4},{1,25},{... | collective-permute-start | bytes 221192 | tf_op jit(solution)/shard_map/ppermute | solution.py:479
  34.6 1.5 %collective-permute-start.13 = (bf16[96,384]{1,0:T(8,128)(2,1)S(1)}, bf16[96,384]{1,0:T(8,128)(2,1)S(1)}, u32[]{:S(2)}, u32[]{:S(2)}) collective-permute-start(bf16[96,384]{1,0:T(8,128)(2,1)S(1)} %get-tuple-element.49), channel_id=1, source_target_pairs={{0,16},{4,20},{8,24},{12,28},{16,0},{20,4},{24,8},{28,12},{1,17},{... | collective-permute-start | bytes 221192 | tf_op jit(solution)/shard_map/ppermute | solution.py:479
  36.1 0.2 collective-permute-start.14
  36.3 2.4 %collective-permute-done.12.rest_1_ = bf16[96,384]{1,0:T(8,128)(2,1)S(1)} collective-permute-done((bf16[96,384]{1,0:T(8,128)(2,1)S(1)}, bf16[96,384]{1,0:T(8,128)(2,1)S(1)}, u32[]{:S(2)}, u32[]{:S(2)}) %collective-permute-start.12) | collective-permute-done | bytes 73760 | tf_op jit(solution)/shard_map/ppermute | solution.py:479
  38.8 0.5 %collective-permute-done.13.rest_2_ = bf16[96,384]{1,0:T(8,128)(2,1)S(1)} collective-permute-done((bf16[96,384]{1,0:T(8,128)(2,1)S(1)}, bf16[96,384]{1,0:T(8,128)(2,1)S(1)}, u32[]{:S(2)}, u32[]{:S(2)}) %collective-permute-start.13) | collective-permute-done | bytes 73760 | tf_op jit(solution)/shard_map/ppermute | solution.py:479
  39.3 1.1 %collective-permute-done.14.rest_3_ = bf16[96,384]{1,0:T(8,128)(2,1)S(1)} collective-permute-done((bf16[96,384]{1,0:T(8,128)(2,1)S(1)}, bf16[96,384]{1,0:T(8,128)(2,1)S(1)}, u32[]{:S(2)}, u32[]{:S(2)}) %collective-permute-start.14) | collective-permute-done | bytes 73760 | tf_op jit(solution)/shard_map/ppermute | solution.py:479
  40.5 0.0 collective-permute-done.17.rest_5_
  40.5 1.0 %unpack.1 = (bf16[1,512,512]{2,1,0:T(8,128)(2,1)}, bf16[1,512,512]{2,1,0:T(8,128)(2,1)}, bf16[1,512,512]{2,1,0:T(8,128)(2,1)}, f32[64,1024]{1,0:T(8,128)}) custom-call(bf16[2,96,128]{2,1,0:T(8,128)(2,1)S(1)} %get-tuple-element.30.sides_ref, ...), custom_call_target="tpu_custom_call", output_to_operand_aliasing={{0}: (7, {}), {1}: (8, {}), {2}: (9, {})} | custom-call | tf_op jit(solution)/shard_map/unpack/pallas_call | solution.py:593
  (3 shorter events, 0.1 us)
Async XLA Ops:
  0.6 12.0 %copy-start = (bf16[64,1024]{1,0:T(8,128)(2,1)S(1)}, bf16[64,1024]{1,0:T(8,128)(2,1)}, u32[]{:S(2)}) copy-start(bf16[64,1024]{1,0:T(8,128)(2,1)} %w_ref.3) | copy-start | bytes 393220
  2.1 6.6 %collective-permute-start.1 = (bf16[96,384]{1,0:T(8,128)(2,1)S(1)}, bf16[96,384]{1,0:T(8,128)(2,1)S(1)}, u32[]{:S(2)}, u32[]{:S(2)}) collective-permute-start(bf16[96,384]{1,0:T(8,128)(2,1)S(1)} %get-tuple-element.33), channel_id=1, source_target_pairs={{0,24},{4,28},{8,16},{12,20},{16,8},{20,12},{24,0},{28,4},{1,25},{... | collective-permute-start | bytes 221192 | tf_op jit(solution)/shard_map/ppermute | solution.py:479
  6.1 6.0 %collective-permute-start = (bf16[96,384]{1,0:T(8,128)(2,1)S(1)}, bf16[96,384]{1,0:T(8,128)(2,1)S(1)}, u32[]{:S(2)}, u32[]{:S(2)}) collective-permute-start(bf16[96,384]{1,0:T(8,128)(2,1)S(1)} %get-tuple-element.32.rest_0_), channel_id=1, source_target_pairs={{0,4},{4,0},{8,12},{12,8},{16,20},{20,16},{24,28},{28,24},{1,5},{5... | collective-permute-start | bytes 221192 | tf_op jit(solution)/shard_map/ppermute | solution.py:479
  6.1 6.0 %collective-permute-start.3 = (bf16[96,384]{1,0:T(8,128)(2,1)S(1)}, bf16[96,384]{1,0:T(8,128)(2,1)S(1)}, u32[]{:S(2)}, u32[]{:S(2)}) collective-permute-start(bf16[96,384]{1,0:T(8,128)(2,1)S(1)} %get-tuple-element.34), channel_id=1, source_target_pairs={{0,16},{4,20},{8,24},{12,28},{16,0},{20,4},{24,8},{28,12},{1,17},{... | collective-permute-start | bytes 221192 | tf_op jit(solution)/shard_map/ppermute | solution.py:479
  6.6 6.1 %collective-permute-start.5 = (bf16[96,384]{1,0:T(8,128)(2,1)S(1)}, bf16[96,384]{1,0:T(8,128)(2,1)S(1)}, u32[]{:S(2)}, u32[]{:S(2)}) collective-permute-start(bf16[96,384]{1,0:T(8,128)(2,1)S(1)} %get-tuple-element.35), channel_id=1, source_target_pairs={{0,8},{4,12},{8,0},{12,4},{16,24},{20,28},{24,16},{28,20},{1,9},{5... | collective-permute-start | bytes 221192 | tf_op jit(solution)/shard_map/ppermute | solution.py:479
  8.6 4.0 %collective-permute-start.2 = (bf16[96,384]{1,0:T(8,128)(2,1)S(1)}, bf16[96,384]{1,0:T(8,128)(2,1)S(1)}, u32[]{:S(2)}, u32[]{:S(2)}) collective-permute-start(bf16[96,384]{1,0:T(8,128)(2,1)S(1)} %collective-permute-done.1.rest_2_), channel_id=1, source_target_pairs={{0,4},{4,0},{8,12},{12,8},{16,20},{20,16},{24,28},{28,24},{1,5},{5... | collective-permute-start | bytes 221192 | tf_op jit(solution)/shard_map/ppermute | solution.py:479
  8.6 9.2 %collective-permute-start.8 = (bf16[96,1024]{1,0:T(8,128)(2,1)S(1)}, bf16[96,1024]{1,0:T(8,128)(2,1)S(1)}, u32[]{:S(2)}, u32[]{:S(2)}) collective-permute-start(bf16[96,1024]{1,0:T(8,128)(2,1)S(1)} %get-tuple-element.40.rest_0_), channel_id=1, source_target_pairs={{0,24},{4,28},{8,16},{12,20},{16,8},{20,12},{24,0},{28,4},{1,25},{... | collective-permute-start | bytes 589832 | tf_op jit(solution)/shard_map/ppermute | solution.py:479
  12.0 9.8 %collective-permute-start.9 = (bf16[96,1024]{1,0:T(8,128)(2,1)S(1)}, bf16[96,1024]{1,0:T(8,128)(2,1)S(1)}, u32[]{:S(2)}, u32[]{:S(2)}) collective-permute-start(bf16[96,1024]{1,0:T(8,128)(2,1)S(1)} %get-tuple-element.40.rest_0_), channel_id=1, source_target_pairs={{0,16},{4,20},{8,24},{12,28},{16,0},{20,4},{24,8},{28,12},{1,17},{... | collective-permute-start | bytes 589832 | tf_op jit(solution)/shard_map/ppermute | solution.py:479
  12.0 9.8 %collective-permute-start.10 = (bf16[96,1024]{1,0:T(8,128)(2,1)S(1)}, bf16[96,1024]{1,0:T(8,128)(2,1)S(1)}, u32[]{:S(2)}, u32[]{:S(2)}) collective-permute-start(bf16[96,1024]{1,0:T(8,128)(2,1)S(1)} %get-tuple-element.40.rest_0_), channel_id=1, source_target_pairs={{0,8},{4,12},{8,0},{12,4},{16,24},{20,28},{24,16},{28,20},{1,9},{5... | collective-permute-start | bytes 589832 | tf_op jit(solution)/shard_map/ppermute | solution.py:479
  12.7 1.3 %collective-permute-start.4 = (bf16[96,384]{1,0:T(8,128)(2,1)S(1)}, bf16[96,384]{1,0:T(8,128)(2,1)S(1)}, u32[]{:S(2)}, u32[]{:S(2)}) collective-permute-start(bf16[96,384]{1,0:T(8,128)(2,1)S(1)} %collective-permute-done.3.rest_4_), channel_id=1, source_target_pairs={{0,4},{4,0},{8,12},{12,8},{16,20},{20,16},{24,28},{28,24},{1,5},{5... | collective-permute-start | bytes 221192 | tf_op jit(solution)/shard_map/ppermute | solution.py:479
  12.7 4.2 %collective-permute-start.7 = (bf16[64,1024]{1,0:T(8,128)(2,1)S(1)}, bf16[64,1024]{1,0:T(8,128)(2,1)S(1)}, u32[]{:S(2)}, u32[]{:S(2)}) collective-permute-start(bf16[64,1024]{1,0:T(8,128)(2,1)S(1)} %copy-done), channel_id=1, source_target_pairs={{0,4},{4,0},{8,12},{12,8},{16,20},{20,16},{24,28},{28,24},{1,5},{5... | collective-permute-start | bytes 393224 | tf_op jit(solution)/shard_map/ppermute | solution.py:479
  13.9 1.3 %collective-permute-start.6 = (bf16[96,384]{1,0:T(8,128)(2,1)S(1)}, bf16[96,384]{1,0:T(8,128)(2,1)S(1)}, u32[]{:S(2)}, u32[]{:S(2)}) collective-permute-start(bf16[96,384]{1,0:T(8,128)(2,1)S(1)} %collective-permute-done.5.rest_6_), channel_id=1, source_target_pairs={{0,4},{4,0},{8,12},{12,8},{16,20},{20,16},{24,28},{28,24},{1,5},{5... | collective-permute-start | bytes 221192 | tf_op jit(solution)/shard_map/ppermute | solution.py:479
  22.2 1.4 %collective-permute-start.15 = (bf16[64,1024]{1,0:T(8,128)(2,1)S(1)}, bf16[64,1024]{1,0:T(8,128)(2,1)S(1)}, u32[]{:S(2)}, u32[]{:S(2)}) collective-permute-start(bf16[64,1024]{1,0:T(8,128)(2,1)S(1)} %get-tuple-element.52), channel_id=1, source_target_pairs={{0,4},{4,0},{8,12},{12,8},{16,20},{20,16},{24,28},{28,24},{1,5},{5... | collective-permute-start | bytes 393224 | tf_op jit(solution)/shard_map/ppermute | solution.py:479
  23.6 5.6 %collective-permute-start.16 = (bf16[64,1024]{1,0:T(8,128)(2,1)S(1)}, bf16[64,1024]{1,0:T(8,128)(2,1)S(1)}, u32[]{:S(2)}, u32[]{:S(2)}) collective-permute-start(bf16[64,1024]{1,0:T(8,128)(2,1)S(1)} %add_convert_fusion.1), channel_id=1, source_target_pairs={{0,1},{1,0},{2,3},{3,2},{4,5},{5,4},{6,7},{7,6},{8,9},{9,8},{10,11... | collective-permute-start | bytes 393224 | tf_op jit(solution)/shard_map/ppermute | solution.py:568
  26.4 6.3 %collective-permute-start.11 = (bf16[4,96,256]{2,1,0:T(8,128)(2,1)S(1)}, bf16[4,96,256]{2,1,0:T(8,128)(2,1)S(1)}, u32[]{:S(2)}, u32[]{:S(2)}) collective-permute-start(bf16[4,96,256]{2,1,0:T(8,128)(2,1)S(1)} %get-tuple-element.46), channel_id=1, source_target_pairs={{0,4},{4,0},{8,12},{12,8},{16,20},{20,16},{24,28},{28,24},{1,5},{5... | collective-permute-start | bytes 589832 | tf_op jit(solution)/shard_map/ppermute | solution.py:479
  29.3 11.2 %collective-permute-start.17 = (bf16[64,1024]{1,0:T(8,128)(2,1)S(1)}, bf16[64,1024]{1,0:T(8,128)(2,1)S(1)}, u32[]{:S(2)}, u32[]{:S(2)}) collective-permute-start(bf16[64,1024]{1,0:T(8,128)(2,1)S(1)} %add_convert_fusion.rest_4_), channel_id=1, source_target_pairs={{0,3},{1,2},{2,1},{3,0},{4,7},{5,6},{6,5},{7,4},{8,11},{9,10},{10,... | collective-permute-start | bytes 393224 | tf_op jit(solution)/shard_map/ppermute | solution.py:568
  32.8 6.0 %collective-permute-start.12 = (bf16[96,384]{1,0:T(8,128)(2,1)S(1)}, bf16[96,384]{1,0:T(8,128)(2,1)S(1)}, u32[]{:S(2)}, u32[]{:S(2)}) collective-permute-start(bf16[96,384]{1,0:T(8,128)(2,1)S(1)} %get-tuple-element.48), channel_id=1, source_target_pairs={{0,24},{4,28},{8,16},{12,20},{16,8},{20,12},{24,0},{28,4},{1,25},{... | collective-permute-start | bytes 221192 | tf_op jit(solution)/shard_map/ppermute | solution.py:479
  34.6 4.7 %collective-permute-start.13 = (bf16[96,384]{1,0:T(8,128)(2,1)S(1)}, bf16[96,384]{1,0:T(8,128)(2,1)S(1)}, u32[]{:S(2)}, u32[]{:S(2)}) collective-permute-start(bf16[96,384]{1,0:T(8,128)(2,1)S(1)} %get-tuple-element.49), channel_id=1, source_target_pairs={{0,16},{4,20},{8,24},{12,28},{16,0},{20,4},{24,8},{28,12},{1,17},{... | collective-permute-start | bytes 221192 | tf_op jit(solution)/shard_map/ppermute | solution.py:479
  36.1 4.4 %collective-permute-start.14 = (bf16[96,384]{1,0:T(8,128)(2,1)S(1)}, bf16[96,384]{1,0:T(8,128)(2,1)S(1)}, u32[]{:S(2)}, u32[]{:S(2)}) collective-permute-start(bf16[96,384]{1,0:T(8,128)(2,1)S(1)} %get-tuple-element.50), channel_id=1, source_target_pairs={{0,8},{4,12},{8,0},{12,4},{16,24},{20,28},{24,16},{28,20},{1,9},{5... | collective-permute-start | bytes 221192 | tf_op jit(solution)/shard_map/ppermute | solution.py:479

commit v7 on v6

--- a/solution.py
+++ b/solution.py
@@ -222,6 +222,7 @@
 
 
 ROUTES = (0, 6, 4, 2)
+FIRST = 128
 
 
 def head_lanes(core):
@@ -320,7 +321,7 @@
 
 def forward_kernel(bias_ref, *rest):
     blocks = rest[:8]
-    shared, query, weights_ref, attended_ref = rest[8:]
+    shared, query, first_ref, second_ref, attended_ref = rest[8:]
     for index in range(8):
         shared[index * MAXV : (index + 1) * MAXV, :] = blocks[index][:, 128:384]
     for index in range(4):
@@ -340,7 +341,8 @@
         scores = scores + bias
         scores = jnp.exp(scores - jnp.max(scores, axis=0, keepdims=True))
         weights = scores * (1.0 / jnp.sum(scores, axis=0, keepdims=True))
-        weights_ref[head] = weights
+        first_ref[head] = weights[:, :FIRST]
+        second_ref[head] = weights[:, FIRST:]
         own = slice(head * HD, (head + 1) * HD)
         attended_ref[own, :] = jnp.dot(
             value_t, weights.astype(jnp.bfloat16), preferred_element_type=jnp.float32
@@ -386,19 +388,14 @@
     dout_ref[...] = project(cot, w_ref, w_other_ref, core)
 
 
-def backward_kernel(shared, query, weights_ref, attended_ref, begun_ref, ended_ref, *rest):
-    kept_query, kept_shared, leaving, dout = rest
-    dout[: 2 * MAXV, :] = begun_ref[...]
-    dout[2 * MAXV :, :] = ended_ref[...]
-    factor = HD ** (-0.5)
-    products = dout[...].astype(jnp.float32).T * attended_ref[...].astype(jnp.float32)
+def pass_over(queries, shared, query, weights_ref, attended_ref, dout):
+    products = dout.astype(jnp.float32).T * attended_ref[:, queries].astype(jnp.float32)
+    own_query = query[queries, :]
     value = shared[:, 128:256]
-    key_grad = jnp.zeros((8 * MAXV, 128), jnp.float32)
-    value_grad = jnp.zeros((8 * MAXV, 128), jnp.float32)
-    query_grad = jnp.zeros((128, 4 * MAXV), jnp.float32)
+    key_grad, value_grad, query_grad = [], [], []
     for head in range(2):
         lanes = head_lanes(head)
-        dout_own = dout[...] * lanes
+        dout_own = dout * lanes
         key_t = (shared[:, 0:128] * lanes).T
         inner = jnp.sum(products[head * HD : (head + 1) * HD], axis=0, keepdims=True)
         weights = weights_ref[head]
@@ -406,15 +403,39 @@
             value, dout_own, (((1,), (1,)), ((), ())), preferred_element_type=jnp.float32
         )
         dscores = (weights * (dweights - inner)).astype(jnp.bfloat16)
-        value_grad += jnp.dot(
-            weights.astype(jnp.bfloat16), dout_own, preferred_element_type=jnp.float32
-        )
-        key_grad += jnp.dot(dscores, query[...] * lanes, preferred_element_type=jnp.float32)
-        query_grad += jnp.dot(key_t, dscores, preferred_element_type=jnp.float32)
-    query_grad = (query_grad * factor).T.astype(jnp.bfloat16)
-    key_grad = key_grad * factor
+        value_grad.append(
+            jnp.dot(weights.astype(jnp.bfloat16), dout_own, preferred_element_type=jnp.float32)
+        )
+        key_grad.append(
+            jnp.dot(dscores, own_query * lanes, preferred_element_type=jnp.float32)
+        )
+        query_grad.append(jnp.dot(key_t, dscores, preferred_element_type=jnp.float32))
+    query_grad = (sum(query_grad) * HD ** (-0.5)).T.astype(jnp.bfloat16)
+    return query_grad, sum(key_grad), sum(value_grad)
+
+
+def backward_first_kernel(shared, query, weights_ref, attended_ref, dout_ref, *outs):
+    results = pass_over(
+        slice(0, FIRST), shared, query, weights_ref, attended_ref, dout_ref[:FIRST, :]
+    )
+    for out, result in zip(outs, results):
+        out[...] = result
+
+
+def backward_kernel(shared, query, weights_ref, attended_ref, begun_ref, ended_ref, *rest):
+    begun_query, begun_key, begun_value, kept_query, kept_shared, leaving, dout, dq = rest
+    split = 2 * MAXV - FIRST
+    dout[:split, :] = begun_ref[FIRST:, :]
+    dout[split:, :] = ended_ref[...]
+    query_grad, key_grad, value_grad = pass_over(
+        slice(FIRST, 4 * MAXV), shared, query, weights_ref, attended_ref, dout[...]
+    )
+    dq[:FIRST, :] = begun_query[...]
+    dq[FIRST:, :] = query_grad
+    key_grad = (begun_key[...] + key_grad) * HD ** (-0.5)
+    value_grad = begun_value[...] + value_grad
     for index in range(4):
-        kept_query[index] = query_grad[index * MAXV : (index + 1) * MAXV]
+        kept_query[index] = dq[index * MAXV : (index + 1) * MAXV, :]
         rows = slice(2 * index * MAXV, (2 * index + 1) * MAXV)
         kept_shared[index, :, 0:128] = key_grad[rows]
         kept_shared[index, :, 128:256] = value_grad[rows]
@@ -530,12 +551,13 @@
         [LOCAL] + [ANYWHERE] * 3,
     )
     own_rows = 4 * MAXV
-    shared, query, weights, attended = seen(
+    shared, query, first, second, attended = seen(
         forward_kernel,
         [
             pltpu.VMEM((rows, 256), bf16),
             pltpu.VMEM((own_rows, 128), bf16),
-            pltpu.VMEM((2, rows, own_rows), jnp.float32),
+            pltpu.VMEM((2, rows, FIRST), jnp.float32),
+            pltpu.VMEM((2, rows, own_rows - FIRST), jnp.float32),
             pltpu.VMEM((128, own_rows), bf16),
         ],
         [LOCAL] * 9,
@@ -549,6 +571,16 @@
         [LOCAL] * 5,
         (attended, out_weight, w_other, *even_cot[:2]),
         gathered,
+    )
+    partial = seen(
+        backward_first_kernel,
+        [
+            pltpu.VMEM((FIRST, 128), bf16),
+            pltpu.VMEM((rows, 128), jnp.float32),
+            pltpu.VMEM((rows, 128), jnp.float32),
+        ],
+        [LOCAL] * 5,
+        (shared, query, first, attended, begun),
     )
     ended, wg_own, wg_other = seen(
         late_kernel,
@@ -581,9 +613,9 @@
             jax.ShapeDtypeStruct((4, MAXV, 256), jnp.float32),
             jax.ShapeDtypeStruct((4, MAXV, 256), bf16),
         ],
-        [LOCAL] * 6,
-        (shared, query, weights, attended, begun, ended),
-        [pltpu.VMEM((own_rows, 128), bf16)],
+        [LOCAL] * 9,
+        (shared, query, second, attended, begun, ended, *partial),
+        [pltpu.VMEM((own_rows - FIRST, 128), bf16), pltpu.VMEM((own_rows, 128), bf16)],
     )
     crossed = shift(leaving, 1)
     joined = seen(combine_kernel, [narrow] * 4, [LOCAL] * 3, (kept_query, kept_shared, crossed))

time: 41.7 us -> 41.7 us (level)
    pallas_call x7 -> x8, Pallas kernels: 6.22 us -> 6.43 us  [seen(): pl.pallas_call(kernel, out_shape=outs, in_specs=specs, out_specs=out_spec...]
where the time goes in v7:
time: 41.7 us; the launch traced here: 41.5 us
  starting transfers between devices  18 us (43%)
  waiting for transfers between devices  15.2 us (36%)
  Pallas kernels  7.47 us (18%)
  between operations  0.74 us (2%)
    ppermute x16, starting transfers between devices, shift(): return lax.ppermute(block, 'seq', [(i, i ^ step) for i in range(pairs)])  13.1 us
    ppermute x16, waiting for transfers between devices, shift(): return lax.ppermute(block, 'seq', [(i, i ^ step) for i in range(pairs)])  12.7 us
    pallas_call x8, Pallas kernels, seen(): pl.pallas_call(kernel, out_shape=outs, in_specs=specs, out_specs=out_spec...  6.43 us
    ppermute x2, starting transfers between devices, across(): return lax.ppermute(block, 'clip', [(i, i ^ step) for i in range(clips)])  4.86 us
    ppermute x2, waiting for transfers between devices, across(): return lax.ppermute(block, 'clip', [(i, i ^ step) for i in range(clips)])  2.54 us
    pallas_call x1, Pallas kernels, by_heads(): pl.pallas_call(functools.partial(unpack_kernel, scale), out_shape=[full]...  1.03 us
  transfers between devices with their start and end apart: 18, of which 10 were waited for; matrix products, arithmetic and copies ran while one was open for 0% of the time, Pallas kernels for 11%

profile of v7, /device:TPU:0, one launch (start us, length us, event | category | flops | bytes accessed | tf_op | source)
XLA Modules:
  0.0 41.5 jit_solution(7827664771449247463)
XLA Ops:
  0.6 0.0 copy-start
  0.6 1.4 %shard_map.102 = (bf16[96,384]{1,0:T(8,128)(2,1)S(1)}, bf16[96,384]{1,0:T(8,128)(2,1)S(1)}, bf16[96,384]{1,0:T(8,128)(2,1)S(1)}, bf16[96,384]{1,0:T(8,128)(2,1)S...) custom-call(s32[1,8]{1,0:T(1,128)} %counts_hbm.3, s32[1,8]{1,0:T(1,128)} %offsets_hbm.3, ...), custom_call_target="tpu_custom_call" | custom-call | tf_op jit(solution)/shard_map/pallas_call | solution.py:506
  2.1 4.0 %collective-permute-start.1 = (bf16[96,384]{1,0:T(8,128)(2,1)S(1)}, bf16[96,384]{1,0:T(8,128)(2,1)S(1)}, u32[]{:S(2)}, u32[]{:S(2)}) collective-permute-start(bf16[96,384]{1,0:T(8,128)(2,1)S(1)} %get-tuple-element.37), channel_id=1, source_target_pairs={{0,24},{4,28},{8,16},{12,20},{16,8},{20,12},{24,0},{28,4},{1,25},{... | collective-permute-start | bytes 221192 | tf_op jit(solution)/shard_map/ppermute | solution.py:500
  6.1 0.0 collective-permute-start
  6.1 0.5 %collective-permute-start.3 = (bf16[96,384]{1,0:T(8,128)(2,1)S(1)}, bf16[96,384]{1,0:T(8,128)(2,1)S(1)}, u32[]{:S(2)}, u32[]{:S(2)}) collective-permute-start(bf16[96,384]{1,0:T(8,128)(2,1)S(1)} %get-tuple-element.38), channel_id=1, source_target_pairs={{0,16},{4,20},{8,24},{12,28},{16,0},{20,4},{24,8},{28,12},{1,17},{... | collective-permute-start | bytes 221192 | tf_op jit(solution)/shard_map/ppermute | solution.py:500
  6.6 0.2 collective-permute-start.5
  6.8 1.9 %collective-permute-done.1.rest_2_ = bf16[96,384]{1,0:T(8,128)(2,1)S(1)} collective-permute-done((bf16[96,384]{1,0:T(8,128)(2,1)S(1)}, bf16[96,384]{1,0:T(8,128)(2,1)S(1)}, u32[]{:S(2)}, u32[]{:S(2)}) %collective-permute-start.1) | collective-permute-done | bytes 73760 | tf_op jit(solution)/shard_map/ppermute | solution.py:500
  8.6 0.0 collective-permute-start.2
  8.6 3.4 %collective-permute-start.8 = (bf16[96,1024]{1,0:T(8,128)(2,1)S(1)}, bf16[96,1024]{1,0:T(8,128)(2,1)S(1)}, u32[]{:S(2)}, u32[]{:S(2)}) collective-permute-start(bf16[96,1024]{1,0:T(8,128)(2,1)S(1)} %get-tuple-element.44.rest_0_), channel_id=1, source_target_pairs={{0,24},{4,28},{8,16},{12,20},{16,8},{20,12},{24,0},{28,4},{1,25},{... | collective-permute-start | bytes 589832 | tf_op jit(solution)/shard_map/ppermute | solution.py:500
  12.0 0.0 collective-permute-done.rest_1_
  12.0 0.0 collective-permute-start.9
  12.0 0.0 collective-permute-done.3.rest_4_
  12.0 0.6 %collective-permute-start.10 = (bf16[96,1024]{1,0:T(8,128)(2,1)S(1)}, bf16[96,1024]{1,0:T(8,128)(2,1)S(1)}, u32[]{:S(2)}, u32[]{:S(2)}) collective-permute-start(bf16[96,1024]{1,0:T(8,128)(2,1)S(1)} %get-tuple-element.44.rest_0_), channel_id=1, source_target_pairs={{0,8},{4,12},{8,0},{12,4},{16,24},{20,28},{24,16},{28,20},{1,9},{5... | collective-permute-start | bytes 589832 | tf_op jit(solution)/shard_map/ppermute | solution.py:500
  12.7 0.0 collective-permute-done.5.rest_6_
  12.7 0.0 collective-permute-start.4
  12.7 0.0 collective-permute-done.2.rest_3_
  12.7 0.0 copy-done
  12.7 0.5 %collective-permute-start.7 = (bf16[64,1024]{1,0:T(8,128)(2,1)S(1)}, bf16[64,1024]{1,0:T(8,128)(2,1)S(1)}, u32[]{:S(2)}, u32[]{:S(2)}) collective-permute-start(bf16[64,1024]{1,0:T(8,128)(2,1)S(1)} %copy-done), channel_id=1, source_target_pairs={{0,4},{4,0},{8,12},{12,8},{16,20},{20,16},{24,28},{28,24},{1,5},{5... | collective-permute-start | bytes 393224 | tf_op jit(solution)/shard_map/ppermute | solution.py:500
  13.2 0.7 %collective-permute-done.4.rest_5_ = bf16[96,384]{1,0:T(8,128)(2,1)S(1)} collective-permute-done((bf16[96,384]{1,0:T(8,128)(2,1)S(1)}, bf16[96,384]{1,0:T(8,128)(2,1)S(1)}, u32[]{:S(2)}, u32[]{:S(2)}) %collective-permute-start.4) | collective-permute-done | bytes 73760 | tf_op jit(solution)/shard_map/ppermute | solution.py:500
  13.9 0.2 collective-permute-start.6
  14.1 1.0 %shard_map.103 = (f32[768,128]{1,0:T(8,128)S(1)}, bf16[1,512,512]{2,1,0:T(8,128)(2,1)}, bf16[1,512,512]{2,1,0:T(8,128)(2,1)}, bf16[1,512,512]{2,1,0:T(8,128)(2,1)}) custom-call(s32[1,8]{1,0:T(1,128)} %counts_hbm.3, s32[1,8]{1,0:T(1,128)} %offsets_hbm.3), custom_call_target="tpu_custom_call" | custom-call | tf_op jit(solution)/shard_map/pallas_call | solution.py:506
  15.1 0.1 collective-permute-done.6.rest_7_
  15.2 1.6 %shard_map.104 = (bf16[768,256]{1,0:T(8,128)(2,1)S(1)}, bf16[384,128]{1,0:T(8,128)(2,1)S(1)}, f32[2,768,128]{2,1,0:T(8,128)S(1)}, f32[2,768,256]{2,1,0:T(8,128)S(1)}, bf16[128,384]{1,0:T(8,128)(2,1)S(1)}) custom-call(f32[768,128]{1,0:T(8,128)S(1)} %get-tuple-element.35.bias_ref, bf16[96,384]{1,0:T(8,128)(2,1)S(1)} %get-tuple-element.36.rest_0_, ...), custom_call_target="tpu_custom_call" | custom-call | tf_op jit(solution)/shard_map/pallas_call | solution.py:506
  16.9 0.0 collective-permute-done.7.w_other_ref
  16.9 1.0 %collective-permute-done.8.rest_1_ = bf16[96,1024]{1,0:T(8,128)(2,1)S(1)} collective-permute-done((bf16[96,1024]{1,0:T(8,128)(2,1)S(1)}, bf16[96,1024]{1,0:T(8,128)(2,1)S(1)}, u32[]{:S(2)}, u32[]{:S(2)}) %collective-permute-start.8) | collective-permute-done | bytes 196640 | tf_op jit(solution)/shard_map/ppermute | solution.py:500
  17.8 0.4 shard_map.105
  18.2 3.6 %collective-permute-done.9.rest_0_ = bf16[96,1024]{1,0:T(8,128)(2,1)S(1)} collective-permute-done((bf16[96,1024]{1,0:T(8,128)(2,1)S(1)}, bf16[96,1024]{1,0:T(8,128)(2,1)S(1)}, u32[]{:S(2)}, u32[]{:S(2)}) %collective-permute-start.9) | collective-permute-done | bytes 196640 | tf_op jit(solution)/shard_map/ppermute | solution.py:500
  21.8 0.0 collective-permute-done.10.rest_1_
  21.8 0.4 shard_map.106
  22.2 0.1 collective-permute-start.15
  22.3 1.3 %collective-permute-done.15 = bf16[64,1024]{1,0:T(8,128)(2,1)S(1)} collective-permute-done((bf16[64,1024]{1,0:T(8,128)(2,1)S(1)}, bf16[64,1024]{1,0:T(8,128)(2,1)S(1)}, u32[]{:S(2)}, u32[]{:S(2)}) %collective-permute-start.15) | collective-permute-done | bytes 131104 | tf_op jit(solution)/shard_map/ppermute | solution.py:500
  23.6 1.4 %collective-permute-start.16 = (bf16[64,1024]{1,0:T(8,128)(2,1)S(1)}, bf16[64,1024]{1,0:T(8,128)(2,1)S(1)}, u32[]{:S(2)}, u32[]{:S(2)}) collective-permute-start(bf16[64,1024]{1,0:T(8,128)(2,1)S(1)} %add_convert_fusion.1), channel_id=1, source_target_pairs={{0,1},{1,0},{2,3},{3,2},{4,5},{5,4},{6,7},{7,6},{8,9},{9,8},{10,11... | collective-permute-start | bytes 393224 | tf_op jit(solution)/shard_map/ppermute | solution.py:600
  25.1 0.6 %shard_map.107 = (bf16[128,128]{1,0:T(8,128)(2,1)S(1)}, f32[768,128]{1,0:T(8,128)S(1)}, f32[768,128]{1,0:T(8,128)S(1)}) custom-call(bf16[768,256]{1,0:T(8,128)(2,1)S(1)} %get-tuple-element.40.shared, bf16[384,128]{1,0:T(8,128)(2,1)S(1)} %get-tuple-element.41.query, f32[2,768,128]{2,1,0:T(8,128)S(1)} %get-tuple-element.48.weights_ref, ...), custom_call_target="tpu_custom_call" | custom-call | tf_op jit(solution)/shard_map/pallas_call | solution.py:506
  25.7 1.0 %shard_map.108 = (bf16[4,96,128]{2,1,0:T(8,128)(2,1)S(1)}, f32[4,96,256]{2,1,0:T(8,128)S(1)}, bf16[4,96,256]{2,1,0:T(8,128)(2,1)S(1)}) custom-call(bf16[768,256]{1,0:T(8,128)(2,1)S(1)} %get-tuple-element.40.shared, bf16[384,128]{1,0:T(8,128)(2,1)S(1)} %get-tuple-element.41.query, f32[2,768,256]{2,1,0:T(8,128)S(1)} %get-tuple-element.42.weights_ref, ...), custom_call_target="tpu_custom_call" | custom-call | tf_op jit(solution)/shard_map/pallas_call | solution.py:506
  26.6 0.1 collective-permute-start.11
  26.7 2.5 %collective-permute-done.16 = bf16[64,1024]{1,0:T(8,128)(2,1)S(1)} collective-permute-done((bf16[64,1024]{1,0:T(8,128)(2,1)S(1)}, bf16[64,1024]{1,0:T(8,128)(2,1)S(1)}, u32[]{:S(2)}, u32[]{:S(2)}) %collective-permute-start.16) | collective-permute-done | bytes 131104 | tf_op jit(solution)/shard_map/ppermute | solution.py:600
  29.3 3.4 %collective-permute-start.17 = (bf16[64,1024]{1,0:T(8,128)(2,1)S(1)}, bf16[64,1024]{1,0:T(8,128)(2,1)S(1)}, u32[]{:S(2)}, u32[]{:S(2)}) collective-permute-start(bf16[64,1024]{1,0:T(8,128)(2,1)S(1)} %add_convert_fusion.rest_4_), channel_id=1, source_target_pairs={{0,3},{1,2},{2,1},{3,0},{4,7},{5,6},{6,5},{7,4},{8,11},{9,10},{10,... | collective-permute-start | bytes 393224 | tf_op jit(solution)/shard_map/ppermute | solution.py:600
  32.7 0.0 collective-permute-done.11.crossed
  32.8 1.8 %collective-permute-start.12 = (bf16[96,384]{1,0:T(8,128)(2,1)S(1)}, bf16[96,384]{1,0:T(8,128)(2,1)S(1)}, u32[]{:S(2)}, u32[]{:S(2)}) collective-permute-start(bf16[96,384]{1,0:T(8,128)(2,1)S(1)} %get-tuple-element.56), channel_id=1, source_target_pairs={{0,24},{4,28},{8,16},{12,20},{16,8},{20,12},{24,0},{28,4},{1,25},{... | collective-permute-start | bytes 221192 | tf_op jit(solution)/shard_map/ppermute | solution.py:500
  34.6 1.5 %collective-permute-start.13 = (bf16[96,384]{1,0:T(8,128)(2,1)S(1)}, bf16[96,384]{1,0:T(8,128)(2,1)S(1)}, u32[]{:S(2)}, u32[]{:S(2)}) collective-permute-start(bf16[96,384]{1,0:T(8,128)(2,1)S(1)} %get-tuple-element.57), channel_id=1, source_target_pairs={{0,16},{4,20},{8,24},{12,28},{16,0},{20,4},{24,8},{28,12},{1,17},{... | collective-permute-start | bytes 221192 | tf_op jit(solution)/shard_map/ppermute | solution.py:500
  36.1 0.2 collective-permute-start.14
  36.3 2.4 %collective-permute-done.12.rest_1_ = bf16[96,384]{1,0:T(8,128)(2,1)S(1)} collective-permute-done((bf16[96,384]{1,0:T(8,128)(2,1)S(1)}, bf16[96,384]{1,0:T(8,128)(2,1)S(1)}, u32[]{:S(2)}, u32[]{:S(2)}) %collective-permute-start.12) | collective-permute-done | bytes 73760 | tf_op jit(solution)/shard_map/ppermute | solution.py:500
  38.8 0.5 %collective-permute-done.13.rest_2_ = bf16[96,384]{1,0:T(8,128)(2,1)S(1)} collective-permute-done((bf16[96,384]{1,0:T(8,128)(2,1)S(1)}, bf16[96,384]{1,0:T(8,128)(2,1)S(1)}, u32[]{:S(2)}, u32[]{:S(2)}) %collective-permute-start.13) | collective-permute-done | bytes 73760 | tf_op jit(solution)/shard_map/ppermute | solution.py:500
  39.3 1.1 %collective-permute-done.14.rest_3_ = bf16[96,384]{1,0:T(8,128)(2,1)S(1)} collective-permute-done((bf16[96,384]{1,0:T(8,128)(2,1)S(1)}, bf16[96,384]{1,0:T(8,128)(2,1)S(1)}, u32[]{:S(2)}, u32[]{:S(2)}) %collective-permute-start.14) | collective-permute-done | bytes 73760 | tf_op jit(solution)/shard_map/ppermute | solution.py:500
  40.5 0.0 collective-permute-done.17.rest_5_
  40.5 1.0 %unpack.1 = (bf16[1,512,512]{2,1,0:T(8,128)(2,1)}, bf16[1,512,512]{2,1,0:T(8,128)(2,1)}, bf16[1,512,512]{2,1,0:T(8,128)(2,1)}, f32[64,1024]{1,0:T(8,128)}) custom-call(bf16[2,96,128]{2,1,0:T(8,128)(2,1)S(1)} %get-tuple-element.34.sides_ref, ...), custom_call_target="tpu_custom_call", output_to_operand_aliasing={{0}: (7, {}), {1}: (8, {}), {2}: (9, {})} | custom-call | tf_op jit(solution)/shard_map/unpack/pallas_call | solution.py:625
  (3 shorter events, 0.1 us)
Async XLA Ops:
  0.6 12.0 %copy-start = (bf16[64,1024]{1,0:T(8,128)(2,1)S(1)}, bf16[64,1024]{1,0:T(8,128)(2,1)}, u32[]{:S(2)}) copy-start(bf16[64,1024]{1,0:T(8,128)(2,1)} %w_ref.3) | copy-start | bytes 393220
  2.1 6.6 %collective-permute-start.1 = (bf16[96,384]{1,0:T(8,128)(2,1)S(1)}, bf16[96,384]{1,0:T(8,128)(2,1)S(1)}, u32[]{:S(2)}, u32[]{:S(2)}) collective-permute-start(bf16[96,384]{1,0:T(8,128)(2,1)S(1)} %get-tuple-element.37), channel_id=1, source_target_pairs={{0,24},{4,28},{8,16},{12,20},{16,8},{20,12},{24,0},{28,4},{1,25},{... | collective-permute-start | bytes 221192 | tf_op jit(solution)/shard_map/ppermute | solution.py:500
  6.1 6.0 %collective-permute-start = (bf16[96,384]{1,0:T(8,128)(2,1)S(1)}, bf16[96,384]{1,0:T(8,128)(2,1)S(1)}, u32[]{:S(2)}, u32[]{:S(2)}) collective-permute-start(bf16[96,384]{1,0:T(8,128)(2,1)S(1)} %get-tuple-element.36.rest_0_), channel_id=1, source_target_pairs={{0,4},{4,0},{8,12},{12,8},{16,20},{20,16},{24,28},{28,24},{1,5},{5... | collective-permute-start | bytes 221192 | tf_op jit(solution)/shard_map/ppermute | solution.py:500
  6.1 6.0 %collective-permute-start.3 = (bf16[96,384]{1,0:T(8,128)(2,1)S(1)}, bf16[96,384]{1,0:T(8,128)(2,1)S(1)}, u32[]{:S(2)}, u32[]{:S(2)}) collective-permute-start(bf16[96,384]{1,0:T(8,128)(2,1)S(1)} %get-tuple-element.38), channel_id=1, source_target_pairs={{0,16},{4,20},{8,24},{12,28},{16,0},{20,4},{24,8},{28,12},{1,17},{... | collective-permute-start | bytes 221192 | tf_op jit(solution)/shard_map/ppermute | solution.py:500
  6.6 6.1 %collective-permute-start.5 = (bf16[96,384]{1,0:T(8,128)(2,1)S(1)}, bf16[96,384]{1,0:T(8,128)(2,1)S(1)}, u32[]{:S(2)}, u32[]{:S(2)}) collective-permute-start(bf16[96,384]{1,0:T(8,128)(2,1)S(1)} %get-tuple-element.39), channel_id=1, source_target_pairs={{0,8},{4,12},{8,0},{12,4},{16,24},{20,28},{24,16},{28,20},{1,9},{5... | collective-permute-start | bytes 221192 | tf_op jit(solution)/shard_map/ppermute | solution.py:500
  8.6 4.0 %collective-permute-start.2 = (bf16[96,384]{1,0:T(8,128)(2,1)S(1)}, bf16[96,384]{1,0:T(8,128)(2,1)S(1)}, u32[]{:S(2)}, u32[]{:S(2)}) collective-permute-start(bf16[96,384]{1,0:T(8,128)(2,1)S(1)} %collective-permute-done.1.rest_2_), channel_id=1, source_target_pairs={{0,4},{4,0},{8,12},{12,8},{16,20},{20,16},{24,28},{28,24},{1,5},{5... | collective-permute-start | bytes 221192 | tf_op jit(solution)/shard_map/ppermute | solution.py:500
  8.6 9.2 %collective-permute-start.8 = (bf16[96,1024]{1,0:T(8,128)(2,1)S(1)}, bf16[96,1024]{1,0:T(8,128)(2,1)S(1)}, u32[]{:S(2)}, u32[]{:S(2)}) collective-permute-start(bf16[96,1024]{1,0:T(8,128)(2,1)S(1)} %get-tuple-element.44.rest_0_), channel_id=1, source_target_pairs={{0,24},{4,28},{8,16},{12,20},{16,8},{20,12},{24,0},{28,4},{1,25},{... | collective-permute-start | bytes 589832 | tf_op jit(solution)/shard_map/ppermute | solution.py:500
  12.0 9.8 %collective-permute-start.9 = (bf16[96,1024]{1,0:T(8,128)(2,1)S(1)}, bf16[96,1024]{1,0:T(8,128)(2,1)S(1)}, u32[]{:S(2)}, u32[]{:S(2)}) collective-permute-start(bf16[96,1024]{1,0:T(8,128)(2,1)S(1)} %get-tuple-element.44.rest_0_), channel_id=1, source_target_pairs={{0,16},{4,20},{8,24},{12,28},{16,0},{20,4},{24,8},{28,12},{1,17},{... | collective-permute-start | bytes 589832 | tf_op jit(solution)/shard_map/ppermute | solution.py:500
  12.0 9.8 %collective-permute-start.10 = (bf16[96,1024]{1,0:T(8,128)(2,1)S(1)}, bf16[96,1024]{1,0:T(8,128)(2,1)S(1)}, u32[]{:S(2)}, u32[]{:S(2)}) collective-permute-start(bf16[96,1024]{1,0:T(8,128)(2,1)S(1)} %get-tuple-element.44.rest_0_), channel_id=1, source_target_pairs={{0,8},{4,12},{8,0},{12,4},{16,24},{20,28},{24,16},{28,20},{1,9},{5... | collective-permute-start | bytes 589832 | tf_op jit(solution)/shard_map/ppermute | solution.py:500
  12.7 1.3 %collective-permute-start.4 = (bf16[96,384]{1,0:T(8,128)(2,1)S(1)}, bf16[96,384]{1,0:T(8,128)(2,1)S(1)}, u32[]{:S(2)}, u32[]{:S(2)}) collective-permute-start(bf16[96,384]{1,0:T(8,128)(2,1)S(1)} %collective-permute-done.3.rest_4_), channel_id=1, source_target_pairs={{0,4},{4,0},{8,12},{12,8},{16,20},{20,16},{24,28},{28,24},{1,5},{5... | collective-permute-start | bytes 221192 | tf_op jit(solution)/shard_map/ppermute | solution.py:500
  12.7 4.2 %collective-permute-start.7 = (bf16[64,1024]{1,0:T(8,128)(2,1)S(1)}, bf16[64,1024]{1,0:T(8,128)(2,1)S(1)}, u32[]{:S(2)}, u32[]{:S(2)}) collective-permute-start(bf16[64,1024]{1,0:T(8,128)(2,1)S(1)} %copy-done), channel_id=1, source_target_pairs={{0,4},{4,0},{8,12},{12,8},{16,20},{20,16},{24,28},{28,24},{1,5},{5... | collective-permute-start | bytes 393224 | tf_op jit(solution)/shard_map/ppermute | solution.py:500
  13.9 1.3 %collective-permute-start.6 = (bf16[96,384]{1,0:T(8,128)(2,1)S(1)}, bf16[96,384]{1,0:T(8,128)(2,1)S(1)}, u32[]{:S(2)}, u32[]{:S(2)}) collective-permute-start(bf16[96,384]{1,0:T(8,128)(2,1)S(1)} %collective-permute-done.5.rest_6_), channel_id=1, source_target_pairs={{0,4},{4,0},{8,12},{12,8},{16,20},{20,16},{24,28},{28,24},{1,5},{5... | collective-permute-start | bytes 221192 | tf_op jit(solution)/shard_map/ppermute | solution.py:500
  22.2 1.4 %collective-permute-start.15 = (bf16[64,1024]{1,0:T(8,128)(2,1)S(1)}, bf16[64,1024]{1,0:T(8,128)(2,1)S(1)}, u32[]{:S(2)}, u32[]{:S(2)}) collective-permute-start(bf16[64,1024]{1,0:T(8,128)(2,1)S(1)} %get-tuple-element.60), channel_id=1, source_target_pairs={{0,4},{4,0},{8,12},{12,8},{16,20},{20,16},{24,28},{28,24},{1,5},{5... | collective-permute-start | bytes 393224 | tf_op jit(solution)/shard_map/ppermute | solution.py:500
  23.6 5.6 %collective-permute-start.16 = (bf16[64,1024]{1,0:T(8,128)(2,1)S(1)}, bf16[64,1024]{1,0:T(8,128)(2,1)S(1)}, u32[]{:S(2)}, u32[]{:S(2)}) collective-permute-start(bf16[64,1024]{1,0:T(8,128)(2,1)S(1)} %add_convert_fusion.1), channel_id=1, source_target_pairs={{0,1},{1,0},{2,3},{3,2},{4,5},{5,4},{6,7},{7,6},{8,9},{9,8},{10,11... | collective-permute-start | bytes 393224 | tf_op jit(solution)/shard_map/ppermute | solution.py:600
  26.6 6.1 %collective-permute-start.11 = (bf16[4,96,256]{2,1,0:T(8,128)(2,1)S(1)}, bf16[4,96,256]{2,1,0:T(8,128)(2,1)S(1)}, u32[]{:S(2)}, u32[]{:S(2)}) collective-permute-start(bf16[4,96,256]{2,1,0:T(8,128)(2,1)S(1)} %get-tuple-element.54), channel_id=1, source_target_pairs={{0,4},{4,0},{8,12},{12,8},{16,20},{20,16},{24,28},{28,24},{1,5},{5... | collective-permute-start | bytes 589832 | tf_op jit(solution)/shard_map/ppermute | solution.py:500
  29.3 11.2 %collective-permute-start.17 = (bf16[64,1024]{1,0:T(8,128)(2,1)S(1)}, bf16[64,1024]{1,0:T(8,128)(2,1)S(1)}, u32[]{:S(2)}, u32[]{:S(2)}) collective-permute-start(bf16[64,1024]{1,0:T(8,128)(2,1)S(1)} %add_convert_fusion.rest_4_), channel_id=1, source_target_pairs={{0,3},{1,2},{2,1},{3,0},{4,7},{5,6},{6,5},{7,4},{8,11},{9,10},{10,... | collective-permute-start | bytes 393224 | tf_op jit(solution)/shard_map/ppermute | solution.py:600
  32.8 6.0 %collective-permute-start.12 = (bf16[96,384]{1,0:T(8,128)(2,1)S(1)}, bf16[96,384]{1,0:T(8,128)(2,1)S(1)}, u32[]{:S(2)}, u32[]{:S(2)}) collective-permute-start(bf16[96,384]{1,0:T(8,128)(2,1)S(1)} %get-tuple-element.56), channel_id=1, source_target_pairs={{0,24},{4,28},{8,16},{12,20},{16,8},{20,12},{24,0},{28,4},{1,25},{... | collective-permute-start | bytes 221192 | tf_op jit(solution)/shard_map/ppermute | solution.py:500
  34.6 4.7 %collective-permute-start.13 = (bf16[96,384]{1,0:T(8,128)(2,1)S(1)}, bf16[96,384]{1,0:T(8,128)(2,1)S(1)}, u32[]{:S(2)}, u32[]{:S(2)}) collective-permute-start(bf16[96,384]{1,0:T(8,128)(2,1)S(1)} %get-tuple-element.57), channel_id=1, source_target_pairs={{0,16},{4,20},{8,24},{12,28},{16,0},{20,4},{24,8},{28,12},{1,17},{... | collective-permute-start | bytes 221192 | tf_op jit(solution)/shard_map/ppermute | solution.py:500
  36.1 4.4 %collective-permute-start.14 = (bf16[96,384]{1,0:T(8,128)(2,1)S(1)}, bf16[96,384]{1,0:T(8,128)(2,1)S(1)}, u32[]{:S(2)}, u32[]{:S(2)}) collective-permute-start(bf16[96,384]{1,0:T(8,128)(2,1)S(1)} %get-tuple-element.58), channel_id=1, source_target_pairs={{0,8},{4,12},{8,0},{12,4},{16,24},{20,28},{24,16},{28,20},{1,9},{5... | collective-permute-start | bytes 221192 | tf_op jit(solution)/shard_map/ppermute | solution.py:500

commit v8 on v7

--- a/solution.py
+++ b/solution.py
@@ -452,9 +452,9 @@
         ).astype(jnp.bfloat16)
 
 
-def unpack_kernel(scale, sides_ref, *rest):
-    blocks, shares, outs, wg_hbm = rest[:4], rest[4:6], rest[9:12], rest[12]
-    edges, wg_ref, sems = rest[13:]
+def unpack_kernel(sides_ref, *rest):
+    blocks, outs = rest[:4], rest[7:10]
+    edges, sems = rest[10:]
     device = lax.axis_index("seq")
     last = outs[0].shape[1] - MAXV
     copies = []
@@ -474,9 +474,26 @@
                 )
             )
             copies[-1].start()
-    wg_ref[...] = (shares[0][...].astype(jnp.float32) + shares[1][...].astype(jnp.float32)) * scale
-    copies.append(pltpu.make_async_copy(wg_ref, wg_hbm, sems.at[len(copies)]))
-    copies[-1].start()
+    for copy in copies:
+        copy.wait()
+
+
+def finish_kernel(scale, mine_ref, other_ref, wg_hbm, wg_ref, sems):
+    half = wg_ref.shape[0] // 2
+    copies = []
+    for part in range(2):
+        rows = slice(part * half, (part + 1) * half)
+        wg_ref[rows, :] = (
+            mine_ref[rows, :].astype(jnp.float32) + other_ref[rows, :].astype(jnp.float32)
+        ) * scale
+        copies.append(
+            pltpu.make_async_copy(
+                wg_ref.at[pl.ds(part * half, half)],
+                wg_hbm.at[pl.ds(part * half, half)],
+                sems.at[part],
+            )
+        )
+        copies[-1].start()
     for copy in copies:
         copy.wait()
 
@@ -621,22 +638,28 @@
     joined = seen(combine_kernel, [narrow] * 4, [LOCAL] * 3, (kept_query, kept_shared, crossed))
     home = [joined[0]] + [shift(joined[i], ROUTES[i]) for i in (1, 2, 3)]
     scale = (clips * VIS_DEV * pairs) ** (-0.5)
-    return tuple(
-        pl.pallas_call(
-            functools.partial(unpack_kernel, scale),
-            out_shape=[full] * 3 + [jax.ShapeDtypeStruct(out_weight.shape, jnp.float32)],
-            in_specs=[LOCAL] * 7 + [ANYWHERE] * 3,
-            out_specs=[ANYWHERE] * 4,
-            scratch_shapes=[
-                pltpu.VMEM((3, 2, MAXV, queries.shape[2]), bf16),
-                pltpu.VMEM(out_weight.shape, jnp.float32),
-                pltpu.SemaphoreType.DMA((7,)),
-            ],
-            input_output_aliases={7: 0, 8: 1, 9: 2},
-            compiler_params=PARAMS,
-            name="unpack",
-        )(sides, *home, *shares, *blanks)
-    )
+    outs = pl.pallas_call(
+        unpack_kernel,
+        out_shape=[full] * 3,
+        in_specs=[LOCAL] * 5 + [ANYWHERE] * 3,
+        out_specs=[ANYWHERE] * 3,
+        scratch_shapes=[
+            pltpu.VMEM((3, 2, MAXV, queries.shape[2]), bf16),
+            pltpu.SemaphoreType.DMA((6,)),
+        ],
+        input_output_aliases={5: 0, 6: 1, 7: 2},
+        compiler_params=PARAMS,
+        name="unpack",
+    )(sides, *home, *blanks)
+    weight_grad = seen(
+        functools.partial(finish_kernel, scale),
+        [jax.ShapeDtypeStruct(out_weight.shape, jnp.float32)],
+        [LOCAL] * 2,
+        shares,
+        [pltpu.VMEM(out_weight.shape, jnp.float32), pltpu.SemaphoreType.DMA((2,))],
+        [ANYWHERE],
+    )[0]
+    return (*outs, weight_grad)
 
 
 def local(*arrays):

time: 41.7 us -> 42.3 us (1.014)
  Pallas kernels: 7.47 us -> 8.09 us
    pallas_call x8 -> x9, Pallas kernels: 6.43 us -> 7.16 us  [seen(): pl.pallas_call(kernel, out_shape=outs, in_specs=specs, out_specs=out_spec...]
  transfers between devices with their start and end apart: 18 -> 18, of which waited for: 10 -> 10; matrix products, arithmetic and copies ran while one was open for 0% -> 0% of each run, Pallas kernels for 11% -> 13%
where the time goes in v8:
time: 42.3 us; the launch traced here: 42.1 us
  starting transfers between devices  18 us (43%)
  waiting for transfers between devices  15.2 us (36%)
  Pallas kernels  8.09 us (19%)
  between operations  0.76 us (2%)
    ppermute x16, starting transfers between devices, shift(): return lax.ppermute(block, 'seq', [(i, i ^ step) for i in range(pairs)])  13.1 us
    ppermute x16, waiting for transfers between devices, shift(): return lax.ppermute(block, 'seq', [(i, i ^ step) for i in range(pairs)])  12.7 us
    pallas_call x9, Pallas kernels, seen(): pl.pallas_call(kernel, out_shape=outs, in_specs=specs, out_specs=out_spec...  7.16 us
    ppermute x2, starting transfers between devices, across(): return lax.ppermute(block, 'clip', [(i, i ^ step) for i in range(clips)])  4.86 us
    ppermute x2, waiting for transfers between devices, across(): return lax.ppermute(block, 'clip', [(i, i ^ step) for i in range(clips)])  2.54 us
    pallas_call x1, Pallas kernels, by_heads(): pl.pallas_call(unpack_kernel, out_shape=[full] * 3, in_specs=[LOCAL] * 5...  0.93 us
  transfers between devices with their start and end apart: 18, of which 10 were waited for; matrix products, arithmetic and copies ran while one was open for 0% of the time, Pallas kernels for 13%

profile of v8, /device:TPU:0, one launch (start us, length us, event | category | flops | bytes accessed | tf_op | source)
XLA Modules:
  0.0 42.1 jit_solution(13528453031487946169)
XLA Ops:
  0.6 0.0 copy-start
  0.6 1.4 %shard_map.102 = (bf16[96,384]{1,0:T(8,128)(2,1)S(1)}, bf16[96,384]{1,0:T(8,128)(2,1)S(1)}, bf16[96,384]{1,0:T(8,128)(2,1)S(1)}, bf16[96,384]{1,0:T(8,128)(2,1)S...) custom-call(s32[1,8]{1,0:T(1,128)} %counts_hbm.3, s32[1,8]{1,0:T(1,128)} %offsets_hbm.3, ...), custom_call_target="tpu_custom_call" | custom-call | tf_op jit(solution)/shard_map/pallas_call | solution.py:523
  2.1 4.0 %collective-permute-start.1 = (bf16[96,384]{1,0:T(8,128)(2,1)S(1)}, bf16[96,384]{1,0:T(8,128)(2,1)S(1)}, u32[]{:S(2)}, u32[]{:S(2)}) collective-permute-start(bf16[96,384]{1,0:T(8,128)(2,1)S(1)} %get-tuple-element.40), channel_id=1, source_target_pairs={{0,24},{4,28},{8,16},{12,20},{16,8},{20,12},{24,0},{28,4},{1,25},{... | collective-permute-start | bytes 221192 | tf_op jit(solution)/shard_map/ppermute | solution.py:517
  6.1 0.0 collective-permute-start
  6.1 0.5 %collective-permute-start.3 = (bf16[96,384]{1,0:T(8,128)(2,1)S(1)}, bf16[96,384]{1,0:T(8,128)(2,1)S(1)}, u32[]{:S(2)}, u32[]{:S(2)}) collective-permute-start(bf16[96,384]{1,0:T(8,128)(2,1)S(1)} %get-tuple-element.41), channel_id=1, source_target_pairs={{0,16},{4,20},{8,24},{12,28},{16,0},{20,4},{24,8},{28,12},{1,17},{... | collective-permute-start | bytes 221192 | tf_op jit(solution)/shard_map/ppermute | solution.py:517
  6.6 0.2 collective-permute-start.5
  6.8 1.9 %collective-permute-done.1.rest_2_ = bf16[96,384]{1,0:T(8,128)(2,1)S(1)} collective-permute-done((bf16[96,384]{1,0:T(8,128)(2,1)S(1)}, bf16[96,384]{1,0:T(8,128)(2,1)S(1)}, u32[]{:S(2)}, u32[]{:S(2)}) %collective-permute-start.1) | collective-permute-done | bytes 73760 | tf_op jit(solution)/shard_map/ppermute | solution.py:517
  8.6 0.0 collective-permute-start.2
  8.6 3.4 %collective-permute-start.8 = (bf16[96,1024]{1,0:T(8,128)(2,1)S(1)}, bf16[96,1024]{1,0:T(8,128)(2,1)S(1)}, u32[]{:S(2)}, u32[]{:S(2)}) collective-permute-start(bf16[96,1024]{1,0:T(8,128)(2,1)S(1)} %get-tuple-element.47.rest_0_), channel_id=1, source_target_pairs={{0,24},{4,28},{8,16},{12,20},{16,8},{20,12},{24,0},{28,4},{1,25},{... | collective-permute-start | bytes 589832 | tf_op jit(solution)/shard_map/ppermute | solution.py:517
  12.0 0.0 collective-permute-done.rest_1_
  12.0 0.0 collective-permute-start.9
  12.0 0.0 collective-permute-done.3.rest_4_
  12.0 0.6 %collective-permute-start.10 = (bf16[96,1024]{1,0:T(8,128)(2,1)S(1)}, bf16[96,1024]{1,0:T(8,128)(2,1)S(1)}, u32[]{:S(2)}, u32[]{:S(2)}) collective-permute-start(bf16[96,1024]{1,0:T(8,128)(2,1)S(1)} %get-tuple-element.47.rest_0_), channel_id=1, source_target_pairs={{0,8},{4,12},{8,0},{12,4},{16,24},{20,28},{24,16},{28,20},{1,9},{5... | collective-permute-start | bytes 589832 | tf_op jit(solution)/shard_map/ppermute | solution.py:517
  12.7 0.0 collective-permute-done.5.rest_6_
  12.7 0.0 collective-permute-start.4
  12.7 0.0 collective-permute-done.2.rest_3_
  12.7 0.0 copy-done
  12.7 0.5 %collective-permute-start.7 = (bf16[64,1024]{1,0:T(8,128)(2,1)S(1)}, bf16[64,1024]{1,0:T(8,128)(2,1)S(1)}, u32[]{:S(2)}, u32[]{:S(2)}) collective-permute-start(bf16[64,1024]{1,0:T(8,128)(2,1)S(1)} %copy-done), channel_id=1, source_target_pairs={{0,4},{4,0},{8,12},{12,8},{16,20},{20,16},{24,28},{28,24},{1,5},{5... | collective-permute-start | bytes 393224 | tf_op jit(solution)/shard_map/ppermute | solution.py:517
  13.2 0.7 %collective-permute-done.4.rest_5_ = bf16[96,384]{1,0:T(8,128)(2,1)S(1)} collective-permute-done((bf16[96,384]{1,0:T(8,128)(2,1)S(1)}, bf16[96,384]{1,0:T(8,128)(2,1)S(1)}, u32[]{:S(2)}, u32[]{:S(2)}) %collective-permute-start.4) | collective-permute-done | bytes 73760 | tf_op jit(solution)/shard_map/ppermute | solution.py:517
  13.9 0.2 collective-permute-start.6
  14.1 1.0 %shard_map.103 = (f32[768,128]{1,0:T(8,128)S(1)}, bf16[1,512,512]{2,1,0:T(8,128)(2,1)}, bf16[1,512,512]{2,1,0:T(8,128)(2,1)}, bf16[1,512,512]{2,1,0:T(8,128)(2,1)}) custom-call(s32[1,8]{1,0:T(1,128)} %counts_hbm.3, s32[1,8]{1,0:T(1,128)} %offsets_hbm.3), custom_call_target="tpu_custom_call" | custom-call | tf_op jit(solution)/shard_map/pallas_call | solution.py:523
  15.1 0.1 collective-permute-done.6.rest_7_
  15.2 1.6 %shard_map.104 = (bf16[768,256]{1,0:T(8,128)(2,1)S(1)}, bf16[384,128]{1,0:T(8,128)(2,1)S(1)}, f32[2,768,128]{2,1,0:T(8,128)S(1)}, f32[2,768,256]{2,1,0:T(8,128)S(1)}, bf16[128,384]{1,0:T(8,128)(2,1)S(1)}) custom-call(f32[768,128]{1,0:T(8,128)S(1)} %get-tuple-element.38.bias_ref, bf16[96,384]{1,0:T(8,128)(2,1)S(1)} %get-tuple-element.39.rest_0_, ...), custom_call_target="tpu_custom_call" | custom-call | tf_op jit(solution)/shard_map/pallas_call | solution.py:523
  16.9 0.0 collective-permute-done.7.w_other_ref
  16.9 0.9 %collective-permute-done.8.rest_1_ = bf16[96,1024]{1,0:T(8,128)(2,1)S(1)} collective-permute-done((bf16[96,1024]{1,0:T(8,128)(2,1)S(1)}, bf16[96,1024]{1,0:T(8,128)(2,1)S(1)}, u32[]{:S(2)}, u32[]{:S(2)}) %collective-permute-start.8) | collective-permute-done | bytes 196640 | tf_op jit(solution)/shard_map/ppermute | solution.py:517
  17.8 0.4 shard_map.105
  18.2 3.6 %collective-permute-done.9.rest_0_ = bf16[96,1024]{1,0:T(8,128)(2,1)S(1)} collective-permute-done((bf16[96,1024]{1,0:T(8,128)(2,1)S(1)}, bf16[96,1024]{1,0:T(8,128)(2,1)S(1)}, u32[]{:S(2)}, u32[]{:S(2)}) %collective-permute-start.9) | collective-permute-done | bytes 196640 | tf_op jit(solution)/shard_map/ppermute | solution.py:517
  21.8 0.0 collective-permute-done.10.rest_1_
  21.8 0.4 shard_map.106
  22.2 0.1 collective-permute-start.15
  22.3 1.3 %collective-permute-done.15 = bf16[64,1024]{1,0:T(8,128)(2,1)S(1)} collective-permute-done((bf16[64,1024]{1,0:T(8,128)(2,1)S(1)}, bf16[64,1024]{1,0:T(8,128)(2,1)S(1)}, u32[]{:S(2)}, u32[]{:S(2)}) %collective-permute-start.15) | collective-permute-done | bytes 131104 | tf_op jit(solution)/shard_map/ppermute | solution.py:517
  23.6 1.4 %collective-permute-start.16 = (bf16[64,1024]{1,0:T(8,128)(2,1)S(1)}, bf16[64,1024]{1,0:T(8,128)(2,1)S(1)}, u32[]{:S(2)}, u32[]{:S(2)}) collective-permute-start(bf16[64,1024]{1,0:T(8,128)(2,1)S(1)} %add_convert_fusion.1), channel_id=1, source_target_pairs={{0,1},{1,0},{2,3},{3,2},{4,5},{5,4},{6,7},{7,6},{8,9},{9,8},{10,11... | collective-permute-start | bytes 393224 | tf_op jit(solution)/shard_map/ppermute | solution.py:617
  25.1 0.6 %shard_map.107 = (bf16[128,128]{1,0:T(8,128)(2,1)S(1)}, f32[768,128]{1,0:T(8,128)S(1)}, f32[768,128]{1,0:T(8,128)S(1)}) custom-call(bf16[768,256]{1,0:T(8,128)(2,1)S(1)} %get-tuple-element.43.shared, bf16[384,128]{1,0:T(8,128)(2,1)S(1)} %get-tuple-element.44.query, f32[2,768,128]{2,1,0:T(8,128)S(1)} %get-tuple-element.51.weights_ref, ...), custom_call_target="tpu_custom_call" | custom-call | tf_op jit(solution)/shard_map/pallas_call | solution.py:523
  25.7 1.0 %shard_map.108 = (bf16[4,96,128]{2,1,0:T(8,128)(2,1)S(1)}, f32[4,96,256]{2,1,0:T(8,128)S(1)}, bf16[4,96,256]{2,1,0:T(8,128)(2,1)S(1)}) custom-call(bf16[768,256]{1,0:T(8,128)(2,1)S(1)} %get-tuple-element.43.shared, bf16[384,128]{1,0:T(8,128)(2,1)S(1)} %get-tuple-element.44.query, f32[2,768,256]{2,1,0:T(8,128)S(1)} %get-tuple-element.45.weights_ref, ...), custom_call_target="tpu_custom_call" | custom-call | tf_op jit(solution)/shard_map/pallas_call | solution.py:523
  26.6 0.1 collective-permute-start.11
  26.7 2.5 %collective-permute-done.16 = bf16[64,1024]{1,0:T(8,128)(2,1)S(1)} collective-permute-done((bf16[64,1024]{1,0:T(8,128)(2,1)S(1)}, bf16[64,1024]{1,0:T(8,128)(2,1)S(1)}, u32[]{:S(2)}, u32[]{:S(2)}) %collective-permute-start.16) | collective-permute-done | bytes 131104 | tf_op jit(solution)/shard_map/ppermute | solution.py:617
  29.3 3.4 %collective-permute-start.17 = (bf16[64,1024]{1,0:T(8,128)(2,1)S(1)}, bf16[64,1024]{1,0:T(8,128)(2,1)S(1)}, u32[]{:S(2)}, u32[]{:S(2)}) collective-permute-start(bf16[64,1024]{1,0:T(8,128)(2,1)S(1)} %add_convert_fusion.mine_ref), channel_id=1, source_target_pairs={{0,3},{1,2},{2,1},{3,0},{4,7},{5,6},{6,5},{7,4},{8,11},{9,10},{10,... | collective-permute-start | bytes 393224 | tf_op jit(solution)/shard_map/ppermute | solution.py:617
  32.7 0.0 collective-permute-done.11.crossed
  32.8 1.8 %collective-permute-start.12 = (bf16[96,384]{1,0:T(8,128)(2,1)S(1)}, bf16[96,384]{1,0:T(8,128)(2,1)S(1)}, u32[]{:S(2)}, u32[]{:S(2)}) collective-permute-start(bf16[96,384]{1,0:T(8,128)(2,1)S(1)} %get-tuple-element.59), channel_id=1, source_target_pairs={{0,24},{4,28},{8,16},{12,20},{16,8},{20,12},{24,0},{28,4},{1,25},{... | collective-permute-start | bytes 221192 | tf_op jit(solution)/shard_map/ppermute | solution.py:517
  34.6 1.5 %collective-permute-start.13 = (bf16[96,384]{1,0:T(8,128)(2,1)S(1)}, bf16[96,384]{1,0:T(8,128)(2,1)S(1)}, u32[]{:S(2)}, u32[]{:S(2)}) collective-permute-start(bf16[96,384]{1,0:T(8,128)(2,1)S(1)} %get-tuple-element.60), channel_id=1, source_target_pairs={{0,16},{4,20},{8,24},{12,28},{16,0},{20,4},{24,8},{28,12},{1,17},{... | collective-permute-start | bytes 221192 | tf_op jit(solution)/shard_map/ppermute | solution.py:517
  36.1 0.2 collective-permute-start.14
  36.3 2.4 %collective-permute-done.12.rest_1_ = bf16[96,384]{1,0:T(8,128)(2,1)S(1)} collective-permute-done((bf16[96,384]{1,0:T(8,128)(2,1)S(1)}, bf16[96,384]{1,0:T(8,128)(2,1)S(1)}, u32[]{:S(2)}, u32[]{:S(2)}) %collective-permute-start.12) | collective-permute-done | bytes 73760 | tf_op jit(solution)/shard_map/ppermute | solution.py:517
  38.8 0.5 %collective-permute-done.13.rest_2_ = bf16[96,384]{1,0:T(8,128)(2,1)S(1)} collective-permute-done((bf16[96,384]{1,0:T(8,128)(2,1)S(1)}, bf16[96,384]{1,0:T(8,128)(2,1)S(1)}, u32[]{:S(2)}, u32[]{:S(2)}) %collective-permute-start.13) | collective-permute-done | bytes 73760 | tf_op jit(solution)/shard_map/ppermute | solution.py:517
  39.3 1.1 %collective-permute-done.14.rest_3_ = bf16[96,384]{1,0:T(8,128)(2,1)S(1)} collective-permute-done((bf16[96,384]{1,0:T(8,128)(2,1)S(1)}, bf16[96,384]{1,0:T(8,128)(2,1)S(1)}, u32[]{:S(2)}, u32[]{:S(2)}) %collective-permute-start.14) | collective-permute-done | bytes 73760 | tf_op jit(solution)/shard_map/ppermute | solution.py:517
  40.5 0.9 %unpack.1 = (bf16[1,512,512]{2,1,0:T(8,128)(2,1)}, bf16[1,512,512]{2,1,0:T(8,128)(2,1)}, bf16[1,512,512]{2,1,0:T(8,128)(2,1)}) custom-call(bf16[2,96,128]{2,1,0:T(8,128)(2,1)S(1)} %get-tuple-element.37.sides_ref, bf16[96,384]{1,0:T(8,128)(2,1)S(1)} %get-tuple-element.58.rest_0_, ...), custom_call_target="tpu_custom_call", output_to_operand_aliasing={{0}: (5, {}), {1}: (6, {}), {2}: (7, {})} | custom-call | tf_op jit(solution)/shard_map/unpack/pallas_call | solution.py:641
  41.4 0.0 collective-permute-done.17.other_ref
  41.4 0.7 %shard_map.110 = f32[64,1024]{1,0:T(8,128)} custom-call(bf16[64,1024]{1,0:T(8,128)(2,1)S(1)} %add_convert_fusion.mine_ref, bf16[64,1024]{1,0:T(8,128)(2,1)S(1)} %collective-permute-done.17.other_ref), custom_call_target="tpu_custom_call" | custom-call | tf_op jit(solution)/shard_map/pallas_call | solution.py:523
  (3 shorter events, 0.1 us)
Async XLA Ops:
  0.6 12.0 %copy-start = (bf16[64,1024]{1,0:T(8,128)(2,1)S(1)}, bf16[64,1024]{1,0:T(8,128)(2,1)}, u32[]{:S(2)}) copy-start(bf16[64,1024]{1,0:T(8,128)(2,1)} %w_ref.3) | copy-start | bytes 393220
  2.1 6.6 %collective-permute-start.1 = (bf16[96,384]{1,0:T(8,128)(2,1)S(1)}, bf16[96,384]{1,0:T(8,128)(2,1)S(1)}, u32[]{:S(2)}, u32[]{:S(2)}) collective-permute-start(bf16[96,384]{1,0:T(8,128)(2,1)S(1)} %get-tuple-element.40), channel_id=1, source_target_pairs={{0,24},{4,28},{8,16},{12,20},{16,8},{20,12},{24,0},{28,4},{1,25},{... | collective-permute-start | bytes 221192 | tf_op jit(solution)/shard_map/ppermute | solution.py:517
  6.1 6.0 %collective-permute-start = (bf16[96,384]{1,0:T(8,128)(2,1)S(1)}, bf16[96,384]{1,0:T(8,128)(2,1)S(1)}, u32[]{:S(2)}, u32[]{:S(2)}) collective-permute-start(bf16[96,384]{1,0:T(8,128)(2,1)S(1)} %get-tuple-element.39.rest_0_), channel_id=1, source_target_pairs={{0,4},{4,0},{8,12},{12,8},{16,20},{20,16},{24,28},{28,24},{1,5},{5... | collective-permute-start | bytes 221192 | tf_op jit(solution)/shard_map/ppermute | solution.py:517
  6.1 6.0 %collective-permute-start.3 = (bf16[96,384]{1,0:T(8,128)(2,1)S(1)}, bf16[96,384]{1,0:T(8,128)(2,1)S(1)}, u32[]{:S(2)}, u32[]{:S(2)}) collective-permute-start(bf16[96,384]{1,0:T(8,128)(2,1)S(1)} %get-tuple-element.41), channel_id=1, source_target_pairs={{0,16},{4,20},{8,24},{12,28},{16,0},{20,4},{24,8},{28,12},{1,17},{... | collective-permute-start | bytes 221192 | tf_op jit(solution)/shard_map/ppermute | solution.py:517
  6.6 6.1 %collective-permute-start.5 = (bf16[96,384]{1,0:T(8,128)(2,1)S(1)}, bf16[96,384]{1,0:T(8,128)(2,1)S(1)}, u32[]{:S(2)}, u32[]{:S(2)}) collective-permute-start(bf16[96,384]{1,0:T(8,128)(2,1)S(1)} %get-tuple-element.42), channel_id=1, source_target_pairs={{0,8},{4,12},{8,0},{12,4},{16,24},{20,28},{24,16},{28,20},{1,9},{5... | collective-permute-start | bytes 221192 | tf_op jit(solution)/shard_map/ppermute | solution.py:517
  8.6 4.0 %collective-permute-start.2 = (bf16[96,384]{1,0:T(8,128)(2,1)S(1)}, bf16[96,384]{1,0:T(8,128)(2,1)S(1)}, u32[]{:S(2)}, u32[]{:S(2)}) collective-permute-start(bf16[96,384]{1,0:T(8,128)(2,1)S(1)} %collective-permute-done.1.rest_2_), channel_id=1, source_target_pairs={{0,4},{4,0},{8,12},{12,8},{16,20},{20,16},{24,28},{28,24},{1,5},{5... | collective-permute-start | bytes 221192 | tf_op jit(solution)/shard_map/ppermute | solution.py:517
  8.6 9.2 %collective-permute-start.8 = (bf16[96,1024]{1,0:T(8,128)(2,1)S(1)}, bf16[96,1024]{1,0:T(8,128)(2,1)S(1)}, u32[]{:S(2)}, u32[]{:S(2)}) collective-permute-start(bf16[96,1024]{1,0:T(8,128)(2,1)S(1)} %get-tuple-element.47.rest_0_), channel_id=1, source_target_pairs={{0,24},{4,28},{8,16},{12,20},{16,8},{20,12},{24,0},{28,4},{1,25},{... | collective-permute-start | bytes 589832 | tf_op jit(solution)/shard_map/ppermute | solution.py:517
  12.0 9.8 %collective-permute-start.9 = (bf16[96,1024]{1,0:T(8,128)(2,1)S(1)}, bf16[96,1024]{1,0:T(8,128)(2,1)S(1)}, u32[]{:S(2)}, u32[]{:S(2)}) collective-permute-start(bf16[96,1024]{1,0:T(8,128)(2,1)S(1)} %get-tuple-element.47.rest_0_), channel_id=1, source_target_pairs={{0,16},{4,20},{8,24},{12,28},{16,0},{20,4},{24,8},{28,12},{1,17},{... | collective-permute-start | bytes 589832 | tf_op jit(solution)/shard_map/ppermute | solution.py:517
  12.0 9.8 %collective-permute-start.10 = (bf16[96,1024]{1,0:T(8,128)(2,1)S(1)}, bf16[96,1024]{1,0:T(8,128)(2,1)S(1)}, u32[]{:S(2)}, u32[]{:S(2)}) collective-permute-start(bf16[96,1024]{1,0:T(8,128)(2,1)S(1)} %get-tuple-element.47.rest_0_), channel_id=1, source_target_pairs={{0,8},{4,12},{8,0},{12,4},{16,24},{20,28},{24,16},{28,20},{1,9},{5... | collective-permute-start | bytes 589832 | tf_op jit(solution)/shard_map/ppermute | solution.py:517
  12.7 1.3 %collective-permute-start.4 = (bf16[96,384]{1,0:T(8,128)(2,1)S(1)}, bf16[96,384]{1,0:T(8,128)(2,1)S(1)}, u32[]{:S(2)}, u32[]{:S(2)}) collective-permute-start(bf16[96,384]{1,0:T(8,128)(2,1)S(1)} %collective-permute-done.3.rest_4_), channel_id=1, source_target_pairs={{0,4},{4,0},{8,12},{12,8},{16,20},{20,16},{24,28},{28,24},{1,5},{5... | collective-permute-start | bytes 221192 | tf_op jit(solution)/shard_map/ppermute | solution.py:517
  12.7 4.2 %collective-permute-start.7 = (bf16[64,1024]{1,0:T(8,128)(2,1)S(1)}, bf16[64,1024]{1,0:T(8,128)(2,1)S(1)}, u32[]{:S(2)}, u32[]{:S(2)}) collective-permute-start(bf16[64,1024]{1,0:T(8,128)(2,1)S(1)} %copy-done), channel_id=1, source_target_pairs={{0,4},{4,0},{8,12},{12,8},{16,20},{20,16},{24,28},{28,24},{1,5},{5... | collective-permute-start | bytes 393224 | tf_op jit(solution)/shard_map/ppermute | solution.py:517
  13.9 1.3 %collective-permute-start.6 = (bf16[96,384]{1,0:T(8,128)(2,1)S(1)}, bf16[96,384]{1,0:T(8,128)(2,1)S(1)}, u32[]{:S(2)}, u32[]{:S(2)}) collective-permute-start(bf16[96,384]{1,0:T(8,128)(2,1)S(1)} %collective-permute-done.5.rest_6_), channel_id=1, source_target_pairs={{0,4},{4,0},{8,12},{12,8},{16,20},{20,16},{24,28},{28,24},{1,5},{5... | collective-permute-start | bytes 221192 | tf_op jit(solution)/shard_map/ppermute | solution.py:517
  22.2 1.4 %collective-permute-start.15 = (bf16[64,1024]{1,0:T(8,128)(2,1)S(1)}, bf16[64,1024]{1,0:T(8,128)(2,1)S(1)}, u32[]{:S(2)}, u32[]{:S(2)}) collective-permute-start(bf16[64,1024]{1,0:T(8,128)(2,1)S(1)} %get-tuple-element.69), channel_id=1, source_target_pairs={{0,4},{4,0},{8,12},{12,8},{16,20},{20,16},{24,28},{28,24},{1,5},{5... | collective-permute-start | bytes 393224 | tf_op jit(solution)/shard_map/ppermute | solution.py:517
  23.6 5.6 %collective-permute-start.16 = (bf16[64,1024]{1,0:T(8,128)(2,1)S(1)}, bf16[64,1024]{1,0:T(8,128)(2,1)S(1)}, u32[]{:S(2)}, u32[]{:S(2)}) collective-permute-start(bf16[64,1024]{1,0:T(8,128)(2,1)S(1)} %add_convert_fusion.1), channel_id=1, source_target_pairs={{0,1},{1,0},{2,3},{3,2},{4,5},{5,4},{6,7},{7,6},{8,9},{9,8},{10,11... | collective-permute-start | bytes 393224 | tf_op jit(solution)/shard_map/ppermute | solution.py:617
  26.6 6.1 %collective-permute-start.11 = (bf16[4,96,256]{2,1,0:T(8,128)(2,1)S(1)}, bf16[4,96,256]{2,1,0:T(8,128)(2,1)S(1)}, u32[]{:S(2)}, u32[]{:S(2)}) collective-permute-start(bf16[4,96,256]{2,1,0:T(8,128)(2,1)S(1)} %get-tuple-element.57), channel_id=1, source_target_pairs={{0,4},{4,0},{8,12},{12,8},{16,20},{20,16},{24,28},{28,24},{1,5},{5... | collective-permute-start | bytes 589832 | tf_op jit(solution)/shard_map/ppermute | solution.py:517
  29.3 12.1 %collective-permute-start.17 = (bf16[64,1024]{1,0:T(8,128)(2,1)S(1)}, bf16[64,1024]{1,0:T(8,128)(2,1)S(1)}, u32[]{:S(2)}, u32[]{:S(2)}) collective-permute-start(bf16[64,1024]{1,0:T(8,128)(2,1)S(1)} %add_convert_fusion.mine_ref), channel_id=1, source_target_pairs={{0,3},{1,2},{2,1},{3,0},{4,7},{5,6},{6,5},{7,4},{8,11},{9,10},{10,... | collective-permute-start | bytes 393224 | tf_op jit(solution)/shard_map/ppermute | solution.py:617
  32.8 6.0 %collective-permute-start.12 = (bf16[96,384]{1,0:T(8,128)(2,1)S(1)}, bf16[96,384]{1,0:T(8,128)(2,1)S(1)}, u32[]{:S(2)}, u32[]{:S(2)}) collective-permute-start(bf16[96,384]{1,0:T(8,128)(2,1)S(1)} %get-tuple-element.59), channel_id=1, source_target_pairs={{0,24},{4,28},{8,16},{12,20},{16,8},{20,12},{24,0},{28,4},{1,25},{... | collective-permute-start | bytes 221192 | tf_op jit(solution)/shard_map/ppermute | solution.py:517
  34.6 4.7 %collective-permute-start.13 = (bf16[96,384]{1,0:T(8,128)(2,1)S(1)}, bf16[96,384]{1,0:T(8,128)(2,1)S(1)}, u32[]{:S(2)}, u32[]{:S(2)}) collective-permute-start(bf16[96,384]{1,0:T(8,128)(2,1)S(1)} %get-tuple-element.60), channel_id=1, source_target_pairs={{0,16},{4,20},{8,24},{12,28},{16,0},{20,4},{24,8},{28,12},{1,17},{... | collective-permute-start | bytes 221192 | tf_op jit(solution)/shard_map/ppermute | solution.py:517
  36.1 4.4 %collective-permute-start.14 = (bf16[96,384]{1,0:T(8,128)(2,1)S(1)}, bf16[96,384]{1,0:T(8,128)(2,1)S(1)}, u32[]{:S(2)}, u32[]{:S(2)}) collective-permute-start(bf16[96,384]{1,0:T(8,128)(2,1)S(1)} %get-tuple-element.61), channel_id=1, source_target_pairs={{0,8},{4,12},{8,0},{12,4},{16,24},{20,28},{24,16},{28,20},{1,9},{5... | collective-permute-start | bytes 221192 | tf_op jit(solution)/shard_map/ppermute | solution.py:517
